TPU v7x, 32 devices: a whole 2x2x4 slice. The times are simulated.
32 devices in a mesh: rep: 8 (over y, x, core), shard: 4 (over z).
Axes of the slice: x: 2, y: 2, z: 4, core: 2. Of those that a mesh axis runs over, the one named last changes fastest.
Arguments:
- hidden_in: bfloat16 [2, 8192, 2048], P(None, ('rep', 'shard')), may hold values from -6 to 6
- prefix: int32 [2, 8], P(None, 'rep'), may hold values from 102 to 512
- ln1_gain: bfloat16 [2048], P('shard'), may hold values from 0.5 to 1.5
- ln1_bias: bfloat16 [2048], P('shard'), may hold values from -3 to 3
- qkv_weight: bfloat16 [2048, 6144], P('shard'), may hold values from -0.125 to 0.125
- q_bias: bfloat16 [2048], P('shard'), may hold values from -3 to 3
- v_bias: bfloat16 [2048], P('shard'), may hold values from -3 to 3
- out_weight: bfloat16 [2048, 2048], P('shard'), may hold values from -1.5 to 1.5
- out_bias: bfloat16 [2048], P('shard'), may hold values from -3 to 3
- ln2_gain: bfloat16 [2048], P('shard'), may hold values from 0.5 to 1.5
- ln2_bias: bfloat16 [2048], P('shard'), may hold values from -3 to 3
- fc1_weight: bfloat16 [2048, 8192], P('shard'), may hold values from -0.125 to 0.125
- fc1_bias: bfloat16 [8192], P('shard'), may hold values from -3 to 3
- fc2_weight: bfloat16 [8192, 2048], P('shard'), may hold values from -0.09375 to 0.09375
- fc2_bias: bfloat16 [2048], P('shard'), may hold values from -3 to 3
- grad_out: bfloat16 [2, 8192, 2048], P(None, ('rep', 'shard')), may hold values from -6 to 6
Outputs:
- result: bfloat16 [2, 8192, 2048], P(None, ('rep', 'shard'))
- grad_in: bfloat16 [2, 8192, 2048], P(None, ('rep', 'shard'))
- ln1_gain_grad: float32 [2048], P('shard')
- ln1_bias_grad: float32 [2048], P('shard')
- qkv_weight_grad: float32 [2048, 6144], P('shard')
- q_bias_grad: float32 [2048], P('shard')
- v_bias_grad: float32 [2048], P('shard')
- out_weight_grad: float32 [2048, 2048], P('shard')
- out_bias_grad: float32 [2048], P('shard')
- ln2_gain_grad: float32 [2048], P('shard')
- ln2_bias_grad: float32 [2048], P('shard')
- fc1_weight_grad: float32 [2048, 8192], P('shard')
- fc1_bias_grad: float32 [8192], P('shard')
- fc2_weight_grad: float32 [8192, 2048], P('shard')
- fc2_bias_grad: float32 [2048], P('shard')
Inputs may be any that keep to these rules, and one draw needn't show every extreme that they name: One prefix length for each sequence.
All inputs are finite; a program needn't handle non-finite values.
Results may differ from a plain program's by a relative error of at most 0.019.
Values may be sent and summed in bfloat16 or wider, within the bound.
No kernel may reach another device: no remote copies, remote signals or barrier semaphores. Data moves between devices by JAX's collectives and lax.ppermute only.
A program may use at most 576 MiB of HBM per device.

v0:
```python
import math

import jax
import jax.numpy as jnp
from jax import lax
from jax.sharding import PartitionSpec as P

HEADS = 16
HEAD_DIM = 128


EPSILON = 1e-05
MASKED = -1e30


def normalize(values, gain_vec, shift_vec):
    centred = values - jnp.mean(values, axis=-1, keepdims=True)
    spread = jnp.mean(centred * centred, axis=-1, keepdims=True)
    return centred * lax.rsqrt(spread + EPSILON) * gain_vec + shift_vec


def gelu_exact(values):
    return jax.nn.gelu(values, approximate=False)


def cross_rows(left_side, right_side):
    return lax.dot_general(
        left_side, right_side, (((0,), (0,)), ((), ())), preferred_element_type=jnp.float32
    )


def times_rows(left_side, right_side):
    return lax.dot_general(
        left_side, right_side, (((1,), (1,)), ((), ())), preferred_element_type=jnp.float32
    )


def local(
    hidden_in,
    prefix,
    ln1_gain,
    ln1_bias,
    qkv_weight,
    q_bias,
    v_bias,
    out_weight,
    out_bias,
    ln2_gain,
    ln2_bias,
    fc1_weight,
    fc1_bias,
    fc2_weight,
    fc2_bias,
    grad_out,
):
    micro_count, tok_rows, model_width = hidden_in.shape
    all_rows = micro_count * tok_rows
    head_count = HEADS
    head_size = HEAD_DIM
    score_scale = 1.0 / math.sqrt(head_size)
    gathered = (
        lax.all_gather(qkv_weight, "shard", axis=0, tiled=True),
        lax.all_gather(out_weight, "shard", axis=0, tiled=True),
        lax.all_gather(ln1_gain, "shard", axis=0, tiled=True),
        lax.all_gather(ln1_bias, "shard", axis=0, tiled=True),
        lax.all_gather(q_bias, "shard", axis=0, tiled=True),
        lax.all_gather(v_bias, "shard", axis=0, tiled=True),
        lax.all_gather(out_bias, "shard", axis=0, tiled=True),
        lax.all_gather(ln2_gain, "shard", axis=0, tiled=True),
        lax.all_gather(ln2_bias, "shard", axis=0, tiled=True),
        lax.all_gather(fc1_bias, "shard", axis=0, tiled=True),
        lax.all_gather(fc2_bias, "shard", axis=0, tiled=True),
    )
    qkv_full = gathered[0]
    out_full = gathered[1]
    (
        gain_one,
        shift_one,
        bias_query,
        bias_value,
        bias_out,
        gain_two,
        shift_two,
        bias_up,
        bias_down,
    ) = [member.astype(jnp.float32) for member in gathered[2:]]
    inputs_f = hidden_in.reshape(all_rows, model_width).astype(jnp.float32)
    normed_one = normalize(inputs_f, gain_one, shift_one).astype(jnp.bfloat16)
    projected = jnp.dot(normed_one, qkv_full, preferred_element_type=jnp.float32)
    projected = projected + jnp.concatenate([bias_query, jnp.zeros_like(bias_query), bias_value])
    queries = projected[:, :model_width].astype(jnp.bfloat16)
    keys_mine = (
        projected[:, model_width : 2 * model_width]
        .astype(jnp.bfloat16)
        .reshape(micro_count, tok_rows, model_width)
    )
    values_mine = (
        projected[:, 2 * model_width :]
        .astype(jnp.bfloat16)
        .reshape(micro_count, tok_rows, model_width)
    )
    keys_all, values_all = (
        lax.all_gather(keys_mine, "shard", axis=1, tiled=True),
        lax.all_gather(values_mine, "shard", axis=1, tiled=True),
    )
    seq_len = keys_all.shape[1]
    first_row = lax.axis_index("shard") * tok_rows
    query_pos = first_row + lax.broadcasted_iota(jnp.int32, (tok_rows, seq_len), 0)
    key_pos = lax.broadcasted_iota(jnp.int32, (tok_rows, seq_len), 1)
    visible = (key_pos <= query_pos)[None] | (key_pos[None] < prefix[:, :, None])
    visible = visible[:, None]
    query_four = queries.reshape(micro_count, tok_rows, head_count, head_size)
    keys_four = keys_all.reshape(micro_count, seq_len, head_count, head_size)
    values_four = values_all.reshape(micro_count, seq_len, head_count, head_size)

    def masked_scores():
        raw_scores = (
            jnp.einsum("bqhd,bkhd->bhqk", query_four, keys_four, preferred_element_type=jnp.float32)
            * score_scale
        )
        return jnp.where(visible, raw_scores, MASKED)

    scores = masked_scores()
    row_max = jnp.max(scores, axis=-1, keepdims=True)
    exp_terms = jnp.exp(scores - row_max)
    row_total = jnp.sum(exp_terms, axis=-1, keepdims=True)
    log_total = row_max + jnp.log(row_total)
    soft_low = (exp_terms / row_total).astype(jnp.bfloat16)
    context = jnp.einsum(
        "bhqk,bkhd->bqhd", soft_low, values_four, preferred_element_type=jnp.float32
    )
    context_low = context.reshape(all_rows, model_width).astype(jnp.bfloat16)
    middle = inputs_f + (
        jnp.dot(context_low, out_full, preferred_element_type=jnp.float32) + bias_out
    )
    normed_two = normalize(middle, gain_two, shift_two).astype(jnp.bfloat16)
    columns = normed_two
    pre_act = (
        jnp.dot(
            columns,
            lax.all_gather(fc1_weight, "shard", axis=0, tiled=True),
            preferred_element_type=jnp.float32,
        )
        + bias_up
    )
    activated = gelu_exact(pre_act).astype(jnp.bfloat16)
    columns = activated
    branch_out = (
        jnp.dot(
            columns,
            lax.all_gather(fc2_weight, "shard", axis=0, tiled=True),
            preferred_element_type=jnp.float32,
        )
        + bias_down
    )
    result = (middle + branch_out).astype(jnp.bfloat16).reshape(micro_count, tok_rows, model_width)
    grad_low = grad_out.reshape(all_rows, model_width)
    grad_rows = grad_low.astype(jnp.float32)
    down_bias_grad = jnp.sum(grad_rows, axis=0)
    d_activated = times_rows(grad_low, lax.all_gather(fc2_weight, "shard", axis=0, tiled=True))
    d_pre = jax.vjp(gelu_exact, pre_act)[1](d_activated)[0].astype(jnp.bfloat16)
    up_bias_grad = jnp.sum(d_pre, axis=0, dtype=jnp.float32)
    d_normed_two = times_rows(d_pre, lax.all_gather(fc1_weight, "shard", axis=0, tiled=True))
    back_two = jax.vjp(normalize, middle, gain_two, shift_two)[1]
    d_middle, gain_two_grad, shift_two_grad = back_two(d_normed_two)
    d_middle = d_middle + grad_rows
    d_attn = d_middle.astype(jnp.bfloat16)
    out_bias_grad = jnp.sum(d_attn, axis=0, dtype=jnp.float32)
    d_context = (
        times_rows(d_attn, out_full)
        .astype(jnp.bfloat16)
        .reshape(micro_count, tok_rows, head_count, head_size)
    )
    soft_full = jnp.exp(masked_scores() - log_total)
    soft_again = soft_full.astype(jnp.bfloat16)
    d_values = jnp.einsum(
        "bhqk,bqhd->bkhd", soft_again, d_context, preferred_element_type=jnp.float32
    )
    d_soft = jnp.einsum(
        "bqhd,bkhd->bhqk", d_context, values_four, preferred_element_type=jnp.float32
    )
    d_scores = (
        soft_full * (d_soft - jnp.sum(soft_full * d_soft, axis=-1, keepdims=True)) * score_scale
    ).astype(jnp.bfloat16)
    d_queries = jnp.einsum(
        "bhqk,bkhd->bqhd", d_scores, keys_four, preferred_element_type=jnp.float32
    )
    d_keys = jnp.einsum("bhqk,bqhd->bkhd", d_scores, query_four, preferred_element_type=jnp.float32)
    keys_grad, values_grad = (
        lax.psum_scatter(
            d_keys.reshape(micro_count, seq_len, model_width).astype(jnp.bfloat16),
            "shard",
            scatter_dimension=1,
            tiled=True,
        ).astype(jnp.float32),
        lax.psum_scatter(
            d_values.reshape(micro_count, seq_len, model_width).astype(jnp.bfloat16),
            "shard",
            scatter_dimension=1,
            tiled=True,
        ).astype(jnp.float32),
    )
    d_projected = jnp.concatenate(
        [
            d_queries.reshape(all_rows, model_width).astype(jnp.bfloat16),
            keys_grad.reshape(all_rows, model_width).astype(jnp.bfloat16),
            values_grad.reshape(all_rows, model_width).astype(jnp.bfloat16),
        ],
        axis=1,
    )
    query_bias_grad = jnp.sum(d_projected[:, :model_width], axis=0, dtype=jnp.float32)
    value_bias_grad = jnp.sum(d_projected[:, 2 * model_width :], axis=0, dtype=jnp.float32)
    d_normed_one = times_rows(d_projected, qkv_full)
    back_one = jax.vjp(normalize, inputs_f, gain_one, shift_one)[1]
    d_inputs, gain_one_grad, shift_one_grad = back_one(d_normed_one)
    grad_in = (d_middle + d_inputs).astype(jnp.bfloat16).reshape(micro_count, tok_rows, model_width)
    down_weight_grad = lax.psum_scatter(
        cross_rows(activated, grad_low).astype(jnp.bfloat16),
        "shard",
        scatter_dimension=0,
        tiled=True,
    )
    up_weight_grad = lax.psum_scatter(
        cross_rows(normed_two, d_pre).astype(jnp.bfloat16), "shard", scatter_dimension=0, tiled=True
    )
    qkv_term = cross_rows(normed_one, d_projected)
    out_term = cross_rows(context_low, d_attn)
    front_grad = lax.psum_scatter(
        jnp.concatenate([qkv_term, out_term], axis=1).astype(jnp.bfloat16),
        "shard",
        scatter_dimension=0,
        tiled=True,
    )
    vectors = (
        lax.psum_scatter(
            gain_one_grad.astype(jnp.bfloat16), "shard", scatter_dimension=0, tiled=True
        ).astype(jnp.float32),
        lax.psum_scatter(
            shift_one_grad.astype(jnp.bfloat16), "shard", scatter_dimension=0, tiled=True
        ).astype(jnp.float32),
        lax.psum_scatter(
            query_bias_grad.astype(jnp.bfloat16), "shard", scatter_dimension=0, tiled=True
        ).astype(jnp.float32),
        lax.psum_scatter(
            value_bias_grad.astype(jnp.bfloat16), "shard", scatter_dimension=0, tiled=True
        ).astype(jnp.float32),
        lax.psum_scatter(
            out_bias_grad.astype(jnp.bfloat16), "shard", scatter_dimension=0, tiled=True
        ).astype(jnp.float32),
        lax.psum_scatter(
            gain_two_grad.astype(jnp.bfloat16), "shard", scatter_dimension=0, tiled=True
        ).astype(jnp.float32),
        lax.psum_scatter(
            shift_two_grad.astype(jnp.bfloat16), "shard", scatter_dimension=0, tiled=True
        ).astype(jnp.float32),
        lax.psum_scatter(
            up_bias_grad.astype(jnp.bfloat16), "shard", scatter_dimension=0, tiled=True
        ).astype(jnp.float32),
        lax.psum_scatter(
            down_bias_grad.astype(jnp.bfloat16), "shard", scatter_dimension=0, tiled=True
        ).astype(jnp.float32),
    )
    summed = (
        lax.psum(front_grad, "rep").astype(jnp.float32),
        lax.psum(up_weight_grad, "rep").astype(jnp.float32),
        lax.psum(down_weight_grad, "rep").astype(jnp.float32),
        lax.psum(vectors[0].astype(jnp.bfloat16), "rep").astype(jnp.float32),
        lax.psum(vectors[1].astype(jnp.bfloat16), "rep").astype(jnp.float32),
        lax.psum(vectors[2].astype(jnp.bfloat16), "rep").astype(jnp.float32),
        lax.psum(vectors[3].astype(jnp.bfloat16), "rep").astype(jnp.float32),
        lax.psum(vectors[4].astype(jnp.bfloat16), "rep").astype(jnp.float32),
        lax.psum(vectors[5].astype(jnp.bfloat16), "rep").astype(jnp.float32),
        lax.psum(vectors[6].astype(jnp.bfloat16), "rep").astype(jnp.float32),
        lax.psum(vectors[7].astype(jnp.bfloat16), "rep").astype(jnp.float32),
        lax.psum(vectors[8].astype(jnp.bfloat16), "rep").astype(jnp.float32),
    )
    front_total = summed[0]
    qkv_weight_grad = front_total[:, : 3 * model_width]
    out_weight_grad = front_total[:, 3 * model_width :]
    return (
        result,
        grad_in,
        summed[3],
        summed[4],
        qkv_weight_grad,
        summed[5],
        summed[6],
        out_weight_grad,
        summed[7],
        summed[8],
        summed[9],
        summed[1],
        summed[10],
        summed[2],
        summed[11],
    )


def solution(mesh):
    return jax.shard_map(
        local,
        mesh=mesh,
        in_specs=(
            P(None, ("rep", "shard"), None),
            P(None, "rep"),
            P("shard"),
            P("shard"),
            P("shard", None),
            P("shard"),
            P("shard"),
            P("shard", None),
            P("shard"),
            P("shard"),
            P("shard"),
            P("shard", None),
            P("shard"),
            P("shard", None),
            P("shard"),
            P(None, ("rep", "shard"), None),
        ),
        out_specs=(
            P(None, ("rep", "shard"), None),
            P(None, ("rep", "shard"), None),
            P("shard"),
            P("shard"),
            P("shard", None),
            P("shard"),
            P("shard"),
            P("shard", None),
            P("shard"),
            P("shard"),
            P("shard"),
            P("shard", None),
            P("shard"),
            P("shard", None),
            P("shard"),
        ),
        check_vma=False,
    )
```

profile of v0, /device:TPU:0, one launch (start us, length us, event | category | flops | bytes accessed | tf_op | source)
XLA Modules:
  0.0 4474.1 jit_solution(2843570770094812183)
XLA Ops:
  27.6 37.2 all-gather.2
  64.8 37.5 all-gather.1
  102.3 34.0 all-gather
  139.1 298.8 %all-gather.15.cloned.1.call-done = bf16[2048,6144]{1,0:T(8,128)(2,1)} async-done(((bf16[512,6144]{1,0:T(8,128)(2,1)}), bf16[2048,6144]{1,0:T(8,128)(2,1)}) %all-gather.15.cloned.1.call-update) | async-done | bytes 25165840 | tf_op jit(solution)/shard_map/all_gather | solution.py:62
  437.8 18.5 add_convert_fusion.1
  477.6 19.3 all-gather.5
  510.9 20.1 all_gather.59
  539.5 68.4 %all-gather.17.cloned.1.call-done = bf16[2,1024,2048]{2,1,0:T(8,128)(2,1)} async-done(((bf16[2,256,2048]{2,1,0:T(8,128)(2,1)}), bf16[2,1024,2048]{2,1,0:T(8,128)(2,1)}) %all-gather.17.cloned.1.call-update) | async-done | bytes 8388624 | tf_op jit(solution)/shard_map/all_gather | solution.py:104
  619.9 137.4 %all-gather.19.cloned.1.call-done = bf16[2,1024,2048]{1,2,0:T(8,128)(2,1)} async-done(((bf16[2,256,2048]{1,2,0:T(8,128)(2,1)}), bf16[2,1024,2048]{1,2,0:T(8,128)(2,1)}) %all-gather.19.cloned.1.call-update) | async-done | bytes 8388624 | tf_op jit(solution)/shard_map/all_gather | solution.py:103
  757.3 18.7 fusion.73
  809.9 96.7 %all-gather.21.cloned.1.call-done = bf16[2048,2048]{1,0:T(8,128)(2,1)} async-done(((bf16[512,2048]{1,0:T(8,128)(2,1)}), bf16[2048,2048]{1,0:T(8,128)(2,1)}) %all-gather.21.cloned.1.call-update) | async-done | bytes 8388624 | tf_op jit(solution)/shard_map/all_gather | solution.py:63
  918.6 549.0 %all-gather.23.cloned.1.call-done = bf16[2048,8192]{1,0:T(8,128)(2,1)} async-done(((bf16[512,8192]{1,0:T(8,128)(2,1)}), bf16[2048,8192]{1,0:T(8,128)(2,1)}) %all-gather.23.cloned.1.call-update) | async-done | bytes 33554448 | tf_op jit(solution)/shard_map/all_gather | solution.py:141
  1467.6 29.8 fusion.65
  1497.4 531.2 %all-gather.25.cloned.1.call-done = bf16[8192,2048]{1,0:T(8,128)(2,1)} async-done(((bf16[2048,2048]{1,0:T(8,128)(2,1)}), bf16[8192,2048]{1,0:T(8,128)(2,1)}) %all-gather.25.cloned.1.call-update) | async-done | bytes 33554448 | tf_op jit(solution)/shard_map/all_gather | solution.py:151
  2028.7 61.3 %fusion.67 = (bf16[8192]{0:T(1024)(128)(2,1)}, bf16[512,8192]{1,0:T(8,128)(2,1)}, f32[512,8192]{1,0:T(8,128)}) fusion(f32[512,8192]{1,0:T(8,128)} %fusion.65, f32[8192]{0:T(1024)S(1)} %convert_element_type.223, bf16[512,2048]{1,0:T(8,128)(2,1)S(1)} %bitcast.118, bf16[8192,2048]{1,0:T(8,128)(2,1)} %all-gather.25.cloned.1.call-done), kind=kOutput, calls=%fused_computation.106 | convolution fusion | flops 17490239488 | bytes 77643776 | tf_op jit(solution)/shard_map/dot_general | solution.py:33
  2090.0 26.7 multiply_reduce_fusion.1
  2133.9 17.5 fusion.31
  2180.3 57.9 %fusion.28 = bf16[2,16,128,1024]{3,2,1,0:T(8,128)(2,1)} fusion(bf16[2,256,16,128]{1,3,2,0:T(8,128)(2,1)} %copy.60, f32[2,16,256,1024]{3,2,1,0:T(8,128)} %fusion.78, f32[2,16,256,1024]{3,2,1,0:T(8,128)} %get-tuple-element.56, f32[2,16,256]{2,1,0:T(8,128)S(1)} %copy-done.10), kind=kOutput, calls=%fused_computation.45 | convolution fusion | flops 2210407424 | bytes 77627392 | tf_op jit(solution)/shard_map/bhqk,bqhd->bkhd/dot_general | solution.py:188
  2250.7 25.2 convolution_convert_fusion.1
  2292.2 25.4 convolution_convert_fusion
  2317.7 58.3 %fusion.75 = (bf16[16,128]{1,0:T(8,128)(2,1)S(1)}, bf16[2,16,128,256]{3,2,1,0:T(8,128)(2,1)}) fusion(bf16[2,1024,16,128]{1,3,2,0:T(8,128)(2,1)} %bitcast.117, f32[2,16,256,1024]{3,2,1,0:T(8,128)} %fusion.78, f32[2,16,256,1024]{3,2,1,0:T(8,128)} %get-tuple-element.56, f32[2,16,256]{2,1,0:T(8,128)S(1)} %copy-done.10), kind=kOutput, calls=%fused_computation.112 | convolution fusion | flops 2208308224 | bytes 77631488 | tf_op jit(solution)/shard_map/bhqk,bkhd->bqhd/dot_general | solution.py:185
  2394.2 59.6 %reduce-scatter.12.cloned.1.call-done = bf16[2,256,2048]{2,1,0:T(8,128)(2,1)} async-done(((bf16[2,1024,2048]{2,1,0:T(8,128)(2,1)}), bf16[2,256,2048]{2,1,0:T(8,128)(2,1)}) %reduce-scatter.12.cloned.1.call-update) | async-done | bytes 2097168 | tf_op jit(solution)/shard_map/reduce_scatter | solution.py:190
  2453.8 19.9 convolution_convert_fusion.2
  2473.7 23.2 pad_maximum_fusion
  2497.1 512.0 %reduce-scatter.18.cloned.1.call-done = bf16[512,8192]{1,0:T(8,128)(2,1)} async-done(((bf16[2048,8192]{1,0:T(8,128)(2,1)}), bf16[512,8192]{1,0:T(8,128)(2,1)}) %reduce-scatter.18.cloned.1.call-update) | async-done | bytes 8388624
  3009.0 555.1 %reduce-scatter.20.cloned.1.call-done = bf16[2048,2048]{1,0:T(8,128)(2,1)} async-done(((bf16[8192,2048]{1,0:T(8,128)(2,1)}), bf16[2048,2048]{1,0:T(8,128)(2,1)}) %reduce-scatter.20.cloned.1.call-update) | async-done | bytes 8388624
  3564.1 555.2 %reduce-scatter.16.cloned.1.call-done = bf16[512,8192]{1,0:T(8,128)(2,1)} async-done(((bf16[2048,8192]{1,0:T(8,128)(2,1)}), bf16[512,8192]{1,0:T(8,128)(2,1)}) %reduce-scatter.16.cloned.1.call-update) | async-done | bytes 8388624
  4134.8 25.8 add_convert_fusion.3
  4162.8 22.5 fusion.66
  4189.0 17.5 all-reduce.14
  4207.1 24.3 all-reduce.12
  4243.4 188.0 %all-reduce.17.cloned.1.call-done = (bf16[512,8192]{1,0:T(8,128)(2,1)}, bf16[512,8192]{1,0:T(8,128)(2,1)}, bf16[2048,2048]{1,0:T(8,128)(2,1)}) async-done(((bf16[512,8192]{1,0:T(8,128)(2,1)}, bf16[512,8192]{1,0:T(8,128)(2,1)}, bf16[2048,2048]{1,0:T(8,128)(2,1)}), (bf16[512,8192]{1,0:T(8,128)(2,1)}, bf16[512,8192]{1,0:T(8,128)(2,1)}, bf16[2048,2048]{1,0:T(8,128)(2,1)})) %all-reduce.17.cloned.1.call-update) | async-done | bytes 25165840 | tf_op jit(solution)/shard_map/psum | solution.py:264
  (208 shorter events, 285.6 us)
Async XLA Ops:
  7.2 430.7 %all-gather.15.cloned.1.call-start = ((), (), s32[]{:S(2)}) async-start(), calls=%async_computation.5 | async-start | bytes 31457280 | tf_op jit(solution)/shard_map/all_gather | solution.py:62
  7.9 599.9 %all-gather.17.cloned.1.call-start = ((), (), s32[]{:S(2)}) async-start(), calls=%async_computation.6 | async-start | bytes 10485760 | tf_op jit(solution)/shard_map/all_gather | solution.py:104
  12.7 123.7 %copy-start.15 = (f32[1,2,2,128]{3,1,2,0:T(2,128)}, f32[1,2,2,128]{3,1,2,0:T(2,128)S(1)}, u32[]{:S(2)}) copy-start(f32[1,2,2,128]{3,1,2,0:T(2,128)S(1)} %copy.68) | copy-start | bytes 6148
  14.0 122.4 %copy-start.17 = (f32[512]{0:T(512)}, f32[512]{0:T(512)S(1)}, u32[]{:S(2)}) copy-start(f32[512]{0:T(512)S(1)} %rsqrt.22) | copy-start | bytes 6148
  459.4 298.0 %all-gather.19.cloned.1.call-start = ((), (), s32[]{:S(2)}) async-start(), calls=%async_computation.7 | async-start | bytes 10485760 | tf_op jit(solution)/shard_map/all_gather | solution.py:103
  463.4 443.2 %all-gather.21.cloned.1.call-start = ((), (), s32[]{:S(2)}) async-start(), calls=%async_computation.8 | async-start | bytes 10485760 | tf_op jit(solution)/shard_map/all_gather | solution.py:63
  464.0 46.9 %copy-start.35 = (bf16[2048]{0:T(1024)(128)(2,1)S(1)}, bf16[2048]{0:T(1024)(128)(2,1)}, u32[]{:S(2)}) copy-start(bf16[2048]{0:T(1024)(128)(2,1)} %param.28) | copy-start | bytes 12292
  464.0 67.3 %copy-start.42 = (s32[2,1]{0,1:T(1,128)S(1)}, s32[2,1]{0,1:T(1,128)}, u32[]{:S(2)}) copy-start(s32[2,1]{0,1:T(1,128)} %param.17) | copy-start | bytes 28
  464.0 1003.6 %all-gather.23.cloned.1.call-start = ((), (), s32[]{:S(2)}) async-start(), calls=%async_computation.9 | async-start | bytes 41943040 | tf_op jit(solution)/shard_map/all_gather | solution.py:141
  464.6 1564.0 %all-gather.25.cloned.1.call-start = ((), (), s32[]{:S(2)}) async-start(), calls=%async_computation.10 | async-start | bytes 41943040 | tf_op jit(solution)/shard_map/all_gather | solution.py:151
  465.2 1929.1 %reduce-scatter.14.cloned.1.call-start = ((), (), s32[]{:S(2)}) async-start(), calls=%async_computation.12 | async-start | bytes 10485760 | tf_op jit(solution)/shard_map/reduce_scatter | solution.py:196
  477.5 990.1 %copy-start.33 = (f32[4,1,512]{2,1,0:T(1,128)}, f32[4,1,512]{2,1,0:T(1,128)S(1)}, u32[]{:S(2)}) copy-start(f32[4,1,512]{2,1,0:T(1,128)S(1)} %convert_element_type.270) | copy-start | bytes 24580
  496.8 970.8 %copy-start.19 = (f32[4,1,512]{2,1,0:T(1,128)}, f32[4,1,512]{2,1,0:T(1,128)S(1)}, u32[]{:S(2)}) copy-start(f32[4,1,512]{2,1,0:T(1,128)S(1)} %convert_element_type.269) | copy-start | bytes 24580
  531.0 1497.6 %copy-start.13 = (f32[8192]{0:T(1024)}, f32[8192]{0:T(1024)S(1)}, u32[]{:S(2)}) copy-start(f32[8192]{0:T(1024)S(1)} %convert_element_type.223) | copy-start | bytes 98308
  914.4 583.1 %copy-start.21 = (f32[512]{0:T(512)}, f32[512]{0:T(512)S(1)}, u32[]{:S(2)}) copy-start(f32[512]{0:T(512)S(1)} %broadcast_multiply_fusion) | copy-start | bytes 6148
  918.0 579.5 %copy-start.23 = (f32[512]{0:T(512)}, f32[512]{0:T(512)S(1)}, u32[]{:S(2)}) copy-start(f32[512]{0:T(512)S(1)} %multiply_reduce_fusion.3) | copy-start | bytes 6148
  918.0 579.4 %copy-start.31 = (f32[512]{0:T(512)}, f32[512]{0:T(512)S(1)}, u32[]{:S(2)}) copy-start(f32[512]{0:T(512)S(1)} %fusion.56) | copy-start | bytes 6148
  1467.6 561.0 %copy-start.5 = (bf16[2,256,2048]{2,1,0:T(8,128)(2,1)S(1)}, bf16[2,256,2048]{2,1,0:T(8,128)(2,1)}, u32[]{:S(2)}) copy-start(bf16[2,256,2048]{2,1,0:T(8,128)(2,1)} %param.31) | copy-start | bytes 6291460
  2028.6 61.4 %copy-start.8 = (f32[512,2048]{1,0:T(8,128)S(1)}, f32[512,2048]{1,0:T(8,128)}, u32[]{:S(2)}) copy-start(f32[512,2048]{1,0:T(8,128)} %copy-done.7) | copy-start | bytes 12582916
  2028.6 61.4 %copy-start.20 = (f32[4,1,512]{2,1,0:T(1,128)S(1)}, f32[4,1,512]{2,1,0:T(1,128)}, u32[]{:S(2)}) copy-start(f32[4,1,512]{2,1,0:T(1,128)} %copy-done.19) | copy-start | bytes 24580
  2028.6 61.3 %copy-start.22 = (f32[512]{0:T(512)S(1)}, f32[512]{0:T(512)}, u32[]{:S(2)}) copy-start(f32[512]{0:T(512)} %copy-done.21) | copy-start | bytes 6148
  2028.7 61.3 %copy-start.32 = (f32[512]{0:T(512)S(1)}, f32[512]{0:T(512)}, u32[]{:S(2)}) copy-start(f32[512]{0:T(512)} %copy-done.31) | copy-start | bytes 6148
  2090.0 26.8 copy-start.24
  2163.2 290.6 %reduce-scatter.12.cloned.1.call-start = ((), (), s32[]{:S(2)}) async-start(), calls=%async_computation.11 | async-start | bytes 10485760 | tf_op jit(solution)/shard_map/reduce_scatter | solution.py:190
  2250.0 759.0 %reduce-scatter.18.cloned.1.call-start = ((), (), s32[]{:S(2)}) async-start(), calls=%async_computation.14 | async-start | bytes 41943040
  2275.9 1288.2 %reduce-scatter.20.cloned.1.call-start = ((), (), s32[]{:S(2)}) async-start(), calls=%async_computation.15 | async-start | bytes 41943040
  2317.6 1801.7 %reduce-scatter.16.cloned.1.call-start = ((), (), s32[]{:S(2)}) async-start(), calls=%async_computation.13 | async-start | bytes 41943040
  2497.0 1934.4 %all-reduce.17.cloned.1.call-start = ((), (), s32[]{:S(2)}) async-start(), calls=%async_computation.16 | async-start | bytes 50331648 | tf_op jit(solution)/shard_map/psum | solution.py:264
  4134.8 27.9 copy-start.2
  4134.8 27.9 copy-start.12
  4134.8 27.8 copy-start.16
  4162.8 73.9 %copy-start.26 = (f32[512]{0:T(512)S(1)}, f32[512]{0:T(512)}, u32[]{:S(2)}) copy-start(f32[512]{0:T(512)} %copy-done.25) | copy-start | bytes 6148
  (26 other events, 234.9 us)
Sparse Core Ops, SparseCore 0:
  9.6 428.2 all-gather.14
  459.5 148.2 all-gather.16
  610.0 147.3 all-gather.18
  758.8 147.7 all-gather.20
  908.0 559.5 all-gather.22
  1469.0 559.5 all-gather.24
  2163.4 142.7 reduce-scatter.13
  2308.5 145.2 reduce-scatter.11
  2456.2 552.8 reduce-scatter.17
  3011.2 552.8 reduce-scatter.19
  3566.4 552.7 reduce-scatter.15
  4123.3 308.0 all-reduce.16
where the time goes:
time: 4480 us; the launch traced here: 4470 us
  waiting for transfers between devices  3550 us (79%)
  matrix products  462 us (10%)
  blocking collectives  242 us (5%)
  other arithmetic  107 us (2%)
  local copies, waits for them, and re-layouts  92 us (2%)
    unnamed x15, waiting for transfers between devices  1620 us
    all_gather x1, waiting for transfers between devices, local(): lax.all_gather(fc1_weight, 'shard', axis=0, tiled=True)  549 us
    all_gather x1, waiting for transfers between devices, local(): lax.all_gather(fc2_weight, 'shard', axis=0, tiled=True)  531 us
    all_gather x1, waiting for transfers between devices, local(): lax.all_gather(qkv_weight, 'shard', axis=0, tiled=True)  299 us
    psum x1, waiting for transfers between devices, local(): lax.psum(front_grad, 'rep').astype(jnp.float32)  188 us
    all_gather x1, waiting for transfers between devices, local(): lax.all_gather(keys_mine, 'shard', axis=1, tiled=True)  137 us
    dot_general x4, matrix products, times_rows(): lax.dot_general(left_side, right_side, (((1,), (1,)), ((), ())), preferre...  115 us
    all_gather x1, waiting for transfers between devices, local(): lax.all_gather(out_weight, 'shard', axis=0, tiled=True)  96.7 us
  transfers between devices with their start and end apart: 12, of which 11 were waited for; matrix products, arithmetic and copies ran while one was open for 10% of the time, Pallas kernels for 0%

commit v1 on v0

v1 whole, which is shorter than its diff:
```python
import math

import jax
import jax.numpy as jnp
import numpy as np
from jax import lax
from jax.experimental import pallas as pl
from jax.experimental.pallas import tpu as pltpu
from jax.sharding import Mesh
from jax.sharding import PartitionSpec as P

HEADS = 16
HEAD_DIM = 128
CORES = 2
EPSILON = 1e-05
MASKED = -1e30
SCALE = 1.0 / math.sqrt(HEAD_DIM)
ALL = ("ch", "co", "sh")
BF = jnp.bfloat16
F32 = jnp.float32


def normalize(values, gain_vec, shift_vec):
    centred = values - jnp.mean(values, axis=-1, keepdims=True)
    spread = jnp.mean(centred * centred, axis=-1, keepdims=True)
    return centred * lax.rsqrt(spread + EPSILON) * gain_vec + shift_vec


def dot(left_side, right_side):
    return jnp.dot(left_side, right_side, preferred_element_type=F32)


def cross_rows(left_side, right_side):
    return lax.dot_general(left_side, right_side, (((0,), (0,)), ((), ())), preferred_element_type=F32)


def times_rows(left_side, right_side):
    return lax.dot_general(left_side, right_side, (((1,), (1,)), ((), ())), preferred_element_type=F32)


def after(value, other):
    return lax.optimization_barrier((value, other))[0]


def place(sources, steps, dest_rows, dest_cols, block, out_shape, out_dtype):
    count = len(steps)
    spans = []
    table = []
    for which in range(len(sources)):
        mine = [i for i, step in enumerate(steps) if step[0] == which]
        first, last = mine[0], mine[-1]
        spans.append((first, last + 1))
        hold = [steps[min(max(i, first), last)] for i in range(count)]
        table.append([step[1] for step in hold])
        table.append([step[2] for step in hold])
    table = jnp.concatenate(
        [jnp.asarray(np.array(table, np.int32)), dest_rows.astype(jnp.int32)[None], dest_cols.astype(jnp.int32)[None]]
    )
    last_row = 2 * len(sources)

    def body(table_ref, *refs):
        step = pl.program_id(0)
        out_ref = refs[-1]
        for which, (first, stop) in enumerate(spans):

            @pl.when((step >= first) & (step < stop))
            def _():
                out_ref[...] = refs[which][...].astype(out_dtype)

    def in_map(which):
        return lambda i, table_ref: (table_ref[2 * which, i], table_ref[2 * which + 1, i])

    return pl.pallas_call(
        body,
        grid_spec=pltpu.PrefetchScalarGridSpec(
            num_scalar_prefetch=1,
            grid=(count,),
            in_specs=[pl.BlockSpec(block, in_map(which)) for which in range(len(sources))],
            out_specs=pl.BlockSpec(block, lambda i, table_ref: (table_ref[last_row, i], table_ref[last_row + 1, i])),
        ),
        out_shape=jax.ShapeDtypeStruct(out_shape, out_dtype),
    )(table, *sources)


def head_parts(scal_ref, q_ref, k_ref, block, rows):
    half = 2 * rows
    core = scal_ref[0]
    prefix = scal_ref[1]
    side = block // 2
    offsets = [pl.multiple_of(core * half, half), pl.multiple_of((1 - core) * half, half)]
    q_off = pl.multiple_of(offsets[side] + (block % 2) * rows, rows)
    queries = q_ref[pl.ds(q_off, rows), :]
    chunks = [(offsets[0], half, 0)]
    if side == 1:
        chunks.append((offsets[1], (block - 1) * rows, half))
    scores = []
    for k_off, count, first in chunks:
        raw = lax.dot_general(
            queries, k_ref[pl.ds(k_off, count), :], (((1,), (1,)), ((), ())), preferred_element_type=F32
        )
        raw = raw * SCALE
        if first + count > block * rows:
            q_pos = block * rows + lax.broadcasted_iota(jnp.int32, raw.shape, 0)
            k_pos = first + lax.broadcasted_iota(jnp.int32, raw.shape, 1)
            raw = jnp.where((k_pos <= q_pos) | (k_pos < prefix), raw, MASKED)
        scores.append(raw)
    top = scores[0].max(axis=-1, keepdims=True)
    for raw in scores[1:]:
        top = jnp.maximum(top, raw.max(axis=-1, keepdims=True))
    terms = [jnp.exp(raw - top) for raw in scores]
    total = terms[0].sum(axis=-1, keepdims=True)
    for term in terms[1:]:
        total = total + term.sum(axis=-1, keepdims=True)
    inverse = 1.0 / total
    return q_off, queries, [(k_off, count, term * inverse) for (k_off, count, _), term in zip(chunks, terms)]


def attend_forward_body(scal_ref, q_ref, k_ref, v_ref, out_ref):
    rows = q_ref.shape[0] // 4
    for block in range(4):
        q_off, _, parts = head_parts(scal_ref, q_ref, k_ref, block, rows)
        total = None
        for k_off, count, soft in parts:
            term = jnp.dot(soft.astype(BF), v_ref[pl.ds(k_off, count), :], preferred_element_type=F32)
            total = term if total is None else total + term
        out_ref[pl.ds(q_off, rows), :] = total.astype(BF)


def attend_backward_body(scal_ref, q_ref, k_ref, v_ref, d_ref, dq_ref, dk_ref, dv_ref, dk_acc, dv_acc):
    rows = q_ref.shape[0] // 4
    dk_acc[...] = jnp.zeros_like(dk_acc)
    dv_acc[...] = jnp.zeros_like(dv_acc)
    for block in range(4):
        q_off, queries, parts = head_parts(scal_ref, q_ref, k_ref, block, rows)
        d_out = d_ref[pl.ds(q_off, rows), :]
        d_softs = []
        row_sum = None
        for k_off, count, soft in parts:
            dv_acc[pl.ds(k_off, count), :] += lax.dot_general(
                soft.astype(BF), d_out, (((0,), (0,)), ((), ())), preferred_element_type=F32
            )
            d_soft = lax.dot_general(
                d_out, v_ref[pl.ds(k_off, count), :], (((1,), (1,)), ((), ())), preferred_element_type=F32
            )
            d_softs.append(d_soft)
            term = jnp.sum(soft * d_soft, axis=-1, keepdims=True)
            row_sum = term if row_sum is None else row_sum + term
        d_queries = None
        for (k_off, count, soft), d_soft in zip(parts, d_softs):
            d_scores = (soft * (d_soft - row_sum) * SCALE).astype(BF)
            term = jnp.dot(d_scores, k_ref[pl.ds(k_off, count), :], preferred_element_type=F32)
            d_queries = term if d_queries is None else d_queries + term
            dk_acc[pl.ds(k_off, count), :] += lax.dot_general(
                d_scores, queries, (((0,), (0,)), ((), ())), preferred_element_type=F32
            )
        dq_ref[pl.ds(q_off, rows), :] = d_queries.astype(BF)
    dk_ref[...] = dk_acc[...].astype(BF)
    dv_ref[...] = dv_acc[...].astype(BF)


def head_specs(rows, heads):
    return [pl.BlockSpec((rows, HEAD_DIM), lambda h, scal_ref, at=at: (0, at * heads + h)) for at in range(3)]


def attend_forward(projected, scalars):
    rows, width = projected.shape
    heads = width // (3 * HEAD_DIM)
    return pl.pallas_call(
        attend_forward_body,
        grid_spec=pltpu.PrefetchScalarGridSpec(
            num_scalar_prefetch=1,
            grid=(heads,),
            in_specs=head_specs(rows, heads),
            out_specs=head_specs(rows, heads)[0],
        ),
        out_shape=jax.ShapeDtypeStruct((rows, width // 3), BF),
    )(scalars, projected, projected, projected)


def attend_backward(projected, d_context, scalars):
    rows, width = projected.shape
    heads = width // (3 * HEAD_DIM)
    one = head_specs(rows, heads)[0]
    return pl.pallas_call(
        attend_backward_body,
        grid_spec=pltpu.PrefetchScalarGridSpec(
            num_scalar_prefetch=1,
            grid=(heads,),
            in_specs=head_specs(rows, heads) + [one],
            out_specs=[one, one, one],
            scratch_shapes=[pltpu.VMEM((rows, HEAD_DIM), F32), pltpu.VMEM((rows, HEAD_DIM), F32)],
        ),
        out_shape=[jax.ShapeDtypeStruct((rows, width // 3), BF)] * 3,
    )(scalars, projected, projected, projected, d_context)


def spread_softmax(queries, keys, q_pos, k_pos, prefix):
    raw = jnp.einsum("qhd,khd->hqk", queries, keys, preferred_element_type=F32) * SCALE
    visible = (k_pos[None, :] <= q_pos[:, None]) | (k_pos[None, :] < prefix)
    raw = jnp.where(visible[None], raw, MASKED)
    terms = jnp.exp(raw - jnp.max(raw, axis=-1, keepdims=True))
    return terms / jnp.sum(terms, axis=-1, keepdims=True)


def spread_backward(queries, keys, values, d_context, soft):
    d_values = jnp.einsum("hqk,qhd->khd", soft.astype(BF), d_context, preferred_element_type=F32)
    d_soft = jnp.einsum("qhd,khd->hqk", d_context, values, preferred_element_type=F32)
    d_scores = (soft * (d_soft - jnp.sum(soft * d_soft, axis=-1, keepdims=True)) * SCALE).astype(BF)
    d_queries = jnp.einsum("hqk,khd->qhd", d_scores, keys, preferred_element_type=F32)
    d_keys = jnp.einsum("hqk,qhd->khd", d_scores, queries, preferred_element_type=F32)
    return d_queries, d_keys, d_values


def local(
    hidden_in,
    prefix,
    ln1_gain,
    ln1_bias,
    qkv_weight,
    q_bias,
    v_bias,
    out_weight,
    out_bias,
    ln2_gain,
    ln2_bias,
    fc1_weight,
    fc1_bias,
    fc2_weight,
    fc2_bias,
    grad_out,
    *,
    chips,
    shards,
):
    micro_count, tok_rows, width = hidden_in.shape
    ff_units = fc1_weight.shape[1]
    piece_rows = width // shards
    rows = micro_count * tok_rows
    parts = shards // (micro_count * CORES)
    ch = lax.axis_index("ch")
    core = lax.axis_index("co")
    shard = lax.axis_index("sh")
    sequence = shard // parts
    micro = sequence // CORES

    def along(value, hop):
        return lax.ppermute(value, "sh", [(i, (i + hop) % shards) for i in range(shards)])

    def plane(value, bit):
        return lax.ppermute(value, "ch", [(i, i ^ bit) for i in range(chips)])

    def swap(value):
        return lax.ppermute(value, "co", [(0, 1), (1, 0)])

    def token_pairs(turn):
        pairs = []
        for c in range(chips):
            for o in range(CORES):
                for s in range(shards):
                    m = (turn + s) % 2
                    slot = s // 2
                    z = (m * CORES + o) * parts + slot // 2
                    pairs.append(((c * CORES + o) * shards + s, (c * CORES + slot % 2) * shards + z))
        return pairs

    def tokens_in(value):
        got = [
            lax.ppermute(lax.dynamic_index_in_dim(value, (turn + shard) % 2, 0, False), ALL, token_pairs(turn))
            for turn in (0, 1)
        ]
        even = micro % 2 == 0
        return jnp.concatenate([jnp.where(even, got[0], got[1]), jnp.where(even, got[1], got[0])])

    def tokens_out(value):
        value = value.reshape(2, tok_rows, width)
        got = [
            lax.ppermute(
                lax.dynamic_index_in_dim(value, (turn + micro) % 2, 0, False),
                ALL,
                [(b, a) for a, b in token_pairs(turn)],
            )
            for turn in (0, 1)
        ]
        even = shard % 2 == 0
        return jnp.stack([jnp.where(even, got[0], got[1]), jnp.where(even, got[1], got[0])])

    def start_pieces(mine, barrier=None):
        cut = mine.shape[1] // chips
        piece = lax.dynamic_slice_in_dim(mine, ch * cut, cut, 1)
        if barrier is not None:
            piece = after(piece, barrier)
        return [along(piece, hop) for hop in range(1, shards)], piece

    def finish_pieces(mine, got, piece, barrier=None):
        height, total = mine.shape
        cut = total // chips
        if chips != 4:
            stacked = jnp.stack([piece] + got)
            everything = lax.all_gather(stacked, "ch")
            everything = jnp.take(everything, (shard - jnp.arange(shards)) % shards, axis=1)
            return everything.transpose(1, 2, 0, 3).reshape(shards * height, total)
        others = jnp.concatenate(got)
        if barrier is not None:
            others = after(others, barrier)
        from_x = plane(others, 1)
        from_y = plane(others, 2)
        tall = (shards - 1, 2, height // 2, cut)
        low_part = plane(from_x.reshape(tall)[:, 0].reshape(-1, cut), 2)
        high_part = plane(from_y.reshape(tall)[:, 1].reshape(-1, cut), 1)
        steps, hops, flips, cols, halves = [], [], [], [], []
        for half in range(2):
            for col in range(chips):
                steps.append((0, half, col))
                hops.append(0), flips.append(-1), cols.append(col), halves.append(half)
        for source, flip in ((1, 0), (2, 1), (3, 2)):
            for hop in range(1, shards):
                for half in range(2):
                    steps.append((source, 2 * (hop - 1) + half, 0))
                    hops.append(hop), flips.append(flip), cols.append(0), halves.append(half)
        for source, half in ((4, 0), (5, 1)):
            for hop in range(1, shards):
                steps.append((source, hop - 1, 0))
                hops.append(hop), flips.append(3), cols.append(0), halves.append(half)
        hops, flips, cols, halves = (np.array(v, np.int32) for v in (hops, flips, cols, halves))
        dest_rows = 2 * ((shard - hops) % shards) + halves
        dest_cols = jnp.where(flips < 0, cols, ch ^ np.maximum(flips, 0))
        return place(
            [mine, others, from_x, from_y, low_part, high_part],
            steps,
            dest_rows,
            dest_cols,
            (height // 2, cut),
            (shards * height, total),
            BF,
        )

    def reduce_grad(left_side, right_side):
        total = right_side.shape[1]
        cut = total // chips
        if chips != 4:
            grads = cross_rows(left_side, right_side).astype(BF)
            grads = grads.reshape(shards, -1, chips, cut).transpose(2, 0, 1, 3)
            mine = lax.psum_scatter(grads, "ch", scatter_dimension=0, tiled=False)
        else:
            middle_at = shards // 2

            def quarter(flip):
                block = lax.dynamic_slice_in_dim(right_side, (ch ^ flip) * cut, cut, 1)
                return cross_rows(left_side, block).astype(BF).reshape(shards, -1, cut)

            far = quarter(3)
            from_y = plane(far[:middle_at], 2)
            from_x = plane(far[middle_at:], 1)
            near_x = quarter(1)
            near_y = quarter(2)
            near_x = jnp.concatenate([near_x[:middle_at] + from_y, near_x[middle_at:]])
            near_y = jnp.concatenate([near_y[:middle_at], near_y[middle_at:] + from_x])
            sum_x = plane(near_x, 1)
            sum_y = plane(near_y, 2)
            mine = (quarter(0).astype(F32) + sum_x.astype(F32) + sum_y.astype(F32)).astype(BF)
        got = [
            along(lax.dynamic_index_in_dim(mine, (shard + hop) % shards, 0, False), hop) for hop in range(1, shards)
        ]
        final = lax.dynamic_index_in_dim(mine, shard, 0, False).astype(F32)
        for member in got:
            final = final + member.astype(F32)
        return final.astype(BF)

    def spread_grad(mine, chunk):
        height, cut = mine.shape
        if chips != 4:
            own = lax.all_gather(mine, "ch", axis=1, tiled=True)
            other = swap(own)
            pair = [jnp.where(core == 0, own, other), jnp.where(core == 0, other, own)]
            if chunk is None:
                return jnp.concatenate(pair).astype(F32)
            wide = jnp.stack([member.reshape(height, -1, chunk) for member in pair], axis=2)
            return wide.reshape(height, -1).astype(F32)
        from_x = plane(mine, 1)
        from_y = plane(mine, 2)
        low_part = plane(from_x[: height // 2], 2)
        high_part = plane(from_y[height // 2 :], 1)
        own = jnp.concatenate([mine, from_x, from_y, low_part, high_part])
        other = swap(own)
        block_cols = cut if chunk is None else min(cut, chunk)
        per = cut // block_cols
        steps, flips, halves, cores, inner = [], [], [], [], []
        for source in range(2):
            for flip in range(4):
                for half in range(2):
                    for at in range(per):
                        steps.append((source, 2 * flip + half, at))
                        flips.append(flip), halves.append(half), cores.append(source), inner.append(at)
        flips, halves, cores, inner = (np.array(v, np.int32) for v in (flips, halves, cores, inner))
        side = core ^ cores
        cols = (ch ^ flips) * per + inner
        if chunk is None:
            dest_rows, dest_cols, shape = 2 * side + halves, cols, (2 * height, chips * cut)
        else:
            step_cols = chunk // block_cols
            dest_rows = jnp.asarray(halves)
            dest_cols = ((cols // step_cols) * 2 + side) * step_cols + cols % step_cols
            shape = (height, 2 * chips * cut)
        return place([own, other], steps, dest_rows, dest_cols, (height // 2, block_cols), shape, F32)

    def take(value, axis):
        return lax.dynamic_index_in_dim(value, core, axis, False)

    qkv_mine = take(qkv_weight.reshape(piece_rows, 3 * shards, CORES, -1), 2).reshape(piece_rows, -1)
    out_mine = take(out_weight.reshape(CORES, piece_rows // CORES, width), 0)
    fc1_mine = take(fc1_weight.reshape(piece_rows, shards, CORES, -1), 2).reshape(piece_rows, -1)
    fc2_mine = take(fc2_weight.reshape(CORES, -1, width), 0)

    vectors = [ln1_gain, ln1_bias, q_bias, v_bias, out_bias, ln2_gain, ln2_bias, fc2_bias, fc1_bias]
    lengths = [v.shape[0] for v in vectors]
    edges = np.cumsum([0] + lengths)
    gathered = lax.all_gather(jnp.concatenate(vectors), "sh").astype(F32)
    vec = [gathered[:, edges[i] : edges[i + 1]] for i in range(len(vectors))]
    gain_one, shift_one, _, _, bias_out, gain_two, shift_two, bias_down, _ = [v.reshape(-1) for v in vec]
    bias_query, bias_value, bias_up = [
        take(vec[i].reshape(shards, CORES, -1), 1).reshape(-1) for i in (2, 3, 8)
    ]

    prefix_pair = [jnp.where(core == 0, a, b) for a, b in ((prefix, swap(prefix)), (swap(prefix), prefix))]
    prefix_len = jnp.concatenate(prefix_pair, axis=1).reshape(-1)[sequence]

    tokens = tokens_in(hidden_in)
    qkv_got, qkv_piece = start_pieces(qkv_mine)
    out_got, out_piece = start_pieces(out_mine, (qkv_got[0], qkv_got[1]))
    fc1_got, fc1_piece = start_pieces(fc1_mine, qkv_got[-1])
    fc2_got, fc2_piece = start_pieces(fc2_mine, fc1_got[-1])
    grads_mine = tokens_in(after(grad_out, fc1_got[-1]))

    hidden_f = tokens.astype(F32)
    normed_own = normalize(hidden_f, gain_one, shift_one).astype(BF)
    normed_one = jnp.concatenate([normed_own, swap(normed_own)])
    qkv_full = finish_pieces(qkv_mine, qkv_got, qkv_piece)
    out_full = finish_pieces(out_mine, out_got, out_piece)
    fc1_full = finish_pieces(fc1_mine, fc1_got, fc1_piece)
    fc2_full = finish_pieces(fc2_mine, fc2_got, fc2_piece)

    half_width = width // CORES
    projected = dot(normed_one, qkv_full) + jnp.concatenate([bias_query, jnp.zeros_like(bias_query), bias_value])
    projected = projected.astype(BF)
    scalars = jnp.stack([core.astype(jnp.int32), prefix_len.astype(jnp.int32)])
    if parts == 1:
        context = attend_forward(projected, scalars)
    else:
        part = shard % parts

        def to_part(value, hop):
            pairs = [(i, i // parts * parts + (i % parts + hop) % parts) for i in range(shards)]
            return lax.ppermute(value, "sh", pairs)

        def positions(which):
            at = jnp.arange(rows)
            return which * CORES * rows + jnp.concatenate([core * rows + at, (1 - core) * rows + at])

        q_four = projected[:, :half_width].reshape(CORES * rows, -1, HEAD_DIM)
        both = projected[:, half_width:]
        held = jnp.concatenate([both] + [to_part(both, hop) for hop in range(1, parts)])
        k_four = held[:, :half_width].reshape(held.shape[0], -1, HEAD_DIM)
        v_four = held[:, half_width:].reshape(held.shape[0], -1, HEAD_DIM)
        k_pos = jnp.concatenate([positions((part - hop) % parts) for hop in range(parts)])
        soft_full = spread_softmax(q_four, k_four, positions(part), k_pos, prefix_len)
        context = jnp.einsum("hqk,khd->qhd", soft_full.astype(BF), v_four, preferred_element_type=F32)
        context = context.reshape(CORES * rows, half_width).astype(BF)

    def own_sum(left_side, product):
        away = swap(product(left_side[rows:]).astype(BF))
        return product(left_side[:rows]) + away.astype(F32)

    middle = hidden_f + (own_sum(context, lambda v: dot(v, out_full)) + bias_out)
    normed_two_own = normalize(middle, gain_two, shift_two).astype(BF)
    normed_two = jnp.concatenate([normed_two_own, swap(normed_two_own)])
    pre_act = dot(normed_two, fc1_full) + bias_up
    below = 0.5 * (1.0 + lax.erf(pre_act * math.sqrt(0.5)))
    density = jnp.exp(-0.5 * pre_act * pre_act) * (1.0 / math.sqrt(2.0 * math.pi))
    activated = (pre_act * below).astype(BF)
    slope = (below + pre_act * density).astype(BF)
    result_own = middle + (own_sum(activated, lambda v: dot(v, fc2_full)) + bias_down)
    result = tokens_out(result_own.astype(BF))

    grad_rows = grads_mine.astype(F32)
    grad_both = jnp.concatenate([grads_mine, swap(grads_mine)])
    down_bias_grad = jnp.sum(grad_rows, axis=0)
    d_pre = (times_rows(grad_both, fc2_full) * slope.astype(F32)).astype(BF)
    fc2_part = reduce_grad(activated, grad_both)
    up_bias_grad = jnp.sum(d_pre, axis=0, dtype=F32)
    fc1_part = reduce_grad(normed_two, d_pre)
    d_normed_two = own_sum(d_pre, lambda v: times_rows(v, fc1_full))
    back_two = jax.vjp(normalize, middle, gain_two, shift_two)[1]
    d_middle, gain_two_grad, shift_two_grad = back_two(d_normed_two)
    d_middle = d_middle + grad_rows
    d_attn_own = d_middle.astype(BF)
    out_bias_grad = jnp.sum(d_attn_own, axis=0, dtype=F32)
    d_attn = jnp.concatenate([d_attn_own, swap(d_attn_own)])
    d_context = times_rows(d_attn, out_full).astype(BF)
    out_part = reduce_grad(context, d_attn)
    if parts == 1:
        d_queries, d_keys, d_values = attend_backward(projected, d_context, scalars)
    else:
        d_four = d_context.reshape(CORES * rows, -1, HEAD_DIM)
        d_queries, d_keys, d_values = spread_backward(q_four, k_four, v_four, d_four, soft_full)
        d_queries = d_queries.reshape(CORES * rows, half_width).astype(BF)
        d_held = jnp.concatenate([d_keys, d_values], axis=1).reshape(parts, CORES * rows, width)
        d_both = d_held[0]
        for hop in range(1, parts):
            d_both = d_both + to_part(d_held[hop].astype(BF), parts - hop).astype(F32)
        d_both = d_both.astype(BF)
        d_keys, d_values = d_both[:, :half_width], d_both[:, half_width:]
    query_bias_grad = jnp.sum(d_queries, axis=0, dtype=F32)
    value_bias_grad = jnp.sum(d_values, axis=0, dtype=F32)
    d_projected = jnp.concatenate([d_queries, d_keys, d_values], axis=1)
    qkv_part = reduce_grad(normed_one, d_projected)
    d_normed_one = own_sum(d_projected, lambda v: times_rows(v, qkv_full))
    back_one = jax.vjp(normalize, hidden_f, gain_one, shift_one)[1]
    d_inputs, gain_one_grad, shift_one_grad = back_one(d_normed_one)
    grad_in = tokens_out((d_middle + d_inputs).astype(BF))

    fc2_weight_grad = spread_grad(fc2_part, None)
    fc1_weight_grad = spread_grad(fc1_part, ff_units // (shards * CORES))
    out_weight_grad = spread_grad(out_part, None)
    qkv_weight_grad = spread_grad(qkv_part, width // (shards * CORES))

    def half_slot(value):
        value = value.reshape(shards, 1, -1)
        mask = lax.broadcasted_iota(jnp.int32, (1, CORES, 1), 1) == core
        return jnp.where(mask, value, 0.0).reshape(shards, -1)

    def full_slot(value):
        return value.reshape(shards, -1)

    packed = jnp.concatenate(
        [
            full_slot(gain_one_grad),
            full_slot(shift_one_grad),
            half_slot(query_bias_grad),
            half_slot(value_bias_grad),
            full_slot(out_bias_grad),
            full_slot(gain_two_grad),
            full_slot(shift_two_grad),
            full_slot(down_bias_grad),
            half_slot(up_bias_grad),
        ],
        axis=1,
    )
    summed = lax.dynamic_index_in_dim(lax.psum(packed, ALL), shard, 0, False)
    sums = [summed[edges[i] : edges[i + 1]] for i in range(len(vectors))]
    return (
        result,
        grad_in,
        sums[0],
        sums[1],
        qkv_weight_grad,
        sums[2],
        sums[3],
        out_weight_grad,
        sums[4],
        sums[5],
        sums[6],
        fc1_weight_grad,
        sums[8],
        fc2_weight_grad,
        sums[7],
    )


def solution(mesh):
    shards = mesh.shape["shard"]
    chips = mesh.shape["rep"] // CORES
    inner = Mesh(mesh.devices.reshape(chips, CORES, shards), ALL)
    token_spec = P(None, ALL, None)
    args = [token_spec, P(None, ("ch", "co"))]
    for dims in (1, 1, 2, 1, 1, 2, 1, 1, 1, 2, 1, 2, 1):
        args.append(P("sh", None) if dims == 2 else P("sh"))
    args.append(token_spec)
    outs = [token_spec, token_spec]
    for dims in (1, 1, 2, 1, 1, 2, 1, 1, 1, 2, 1, 2, 1):
        outs.append(P("sh", None) if dims == 2 else P("sh"))

    def run(*values):
        return local(*values, chips=chips, shards=shards)

    return jax.shard_map(run, mesh=inner, in_specs=tuple(args), out_specs=tuple(outs), check_vma=False)
```

time: 4480 us -> 1850 us (0.41)
  waiting for transfers between devices: 3550 us -> 746 us
  Pallas kernels: 0 us -> 214 us
  starting transfers between devices: 0.48 us -> 203 us
  matrix products: 462 us -> 269 us
  blocking collectives: 242 us -> 109 us
  local copies, waits for them, and re-layouts: 92 us -> 190 us
    all_gather x6 -> x0, waiting for transfers between devices: 1680 us -> none  [the longest x1 549 us: local(): lax.all_gather(fc1_weight, 'shard', axis=0, tiled=True)]
    unnamed x15 -> x1, waiting for transfers between devices: 1620 us -> 0.02 us
    ppermute x0 -> x93, waiting for transfers between devices: none -> 626 us  [the longest x48 355 us: plane(): return lax.ppermute(value, 'ch', [(i, i ^ bit) for i in range(chips)])]
    pallas_call x0 -> x10, Pallas kernels: none -> 214 us  [the longest x8 159 us: place(): pl.pallas_call(body, grid_spec=pltpu.PrefetchScalarGridSpec(num_scalar_pr...]
    ppermute x0 -> x93, starting transfers between devices: none -> 203 us  [the longest x48 50.5 us: plane(): return lax.ppermute(value, 'ch', [(i, i ^ bit) for i in range(chips)])]
    dot_general x10 -> x6, matrix products: 266 us -> 83.1 us  [dot(): return jnp.dot(left_side, right_side, preferred_element_type=F32)]
    all_gather x9 -> x1, blocking collectives: 201 us -> 109 us  [local(): gathered = lax.all_gather(jnp.concatenate(vectors), 'sh').astype(F32)]
    psum x1, waiting for transfers between devices: 188 us -> 120 us  [local(): summed = lax.dynamic_index_in_dim(lax.psum(packed, ALL), shard, 0, False)]
  transfers between devices with their start and end apart: 12 -> 94, of which waited for: 11 -> 34; matrix products, arithmetic and copies ran while one was open for 10% -> 26% of each run, Pallas kernels for 0% -> 10%
where the time goes in v1:
time: 1850 us; the launch traced here: 1840 us
  waiting for transfers between devices  746 us (40%)
  matrix products  269 us (15%)
  Pallas kernels  214 us (12%)
  starting transfers between devices  203 us (11%)
  local copies, waits for them, and re-layouts  190 us (10%)
  blocking collectives  109 us (6%)
  other arithmetic  93.4 us (5%)
    ppermute x48, waiting for transfers between devices, plane(): return lax.ppermute(value, 'ch', [(i, i ^ bit) for i in range(chips)])  355 us
    ppermute x24, waiting for transfers between devices, along(): lax.ppermute(value, 'sh', [(i, (i + hop) % shards) for i in range(shards)])  250 us
    pallas_call x8, Pallas kernels, place(): pl.pallas_call(body, grid_spec=pltpu.PrefetchScalarGridSpec(num_scalar_pr...  159 us
    psum x1, waiting for transfers between devices, local(): summed = lax.dynamic_index_in_dim(lax.psum(packed, ALL), shard, 0, False)  120 us
    all_gather x1, blocking collectives, local(): gathered = lax.all_gather(jnp.concatenate(vectors), 'sh').astype(F32)  109 us
    dot_general x6, matrix products, times_rows(): lax.dot_general(left_side, right_side, (((1,), (1,)), ((), ())), preferre...  97.2 us
    dot_general x16, matrix products, cross_rows(): lax.dot_general(left_side, right_side, (((0,), (0,)), ((), ())), preferre...  88.4 us
    dot_general x6, matrix products, dot(): return jnp.dot(left_side, right_side, preferred_element_type=F32)  83.1 us
  transfers between devices with their start and end apart: 94, of which 34 were waited for; matrix products, arithmetic and copies ran while one was open for 26% of the time, Pallas kernels for 10%

profile of v1, /device:TPU:0, one launch (start us, length us, event | category | flops | bytes accessed | tf_op | source)
XLA Modules:
  0.0 1840.2 jit_solution(10508853754302893176)
XLA Ops:
  41.9 108.8 %all-gather = bf16[24576]{0:T(1024)(128)(2,1)S(1)} all-gather(bf16[6144]{0:T(1024)(128)(2,1)S(1)} %constant_dynamic-update-slice_fusion.44), channel_id=2, replica_groups=mesh['ch'=4,'co'=2,'sh'=4] {'sh'}, dimensions={0}, use_global_device_ids=true | all-gather | bytes 61440 | tf_op jit(solution)/shard_map/all_gather | solution.py:417
  195.1 29.7 %dynamic-slice_reduce_fusion = bf16[512,4,1024]{2,1,0:T(4,128)(2,1)} fusion(bf16[512,4,2,1024]{3,2,1,0:T(2,128)(2,1)} %reshape.290, s32[]{:T(128)S(6)} %select_n.307), kind=kLoop, calls=%fused_computation.17 | loop fusion | bytes 8388612 | tf_op jit(solution)/shard_map/jit(dynamic_index_in_dim)/dynamic_slice | solution.py:407
  265.1 27.6 %collective-permute-done.16.refs_4_ = bf16[384,512]{1,0:T(8,128)(2,1)S(1)} collective-permute-done((bf16[384,512]{1,0:T(8,128)(2,1)S(1)}, bf16[384,512]{1,0:T(8,128)(2,1)S(1)}, u32[]{:S(2)}, u32[]{:S(2)}) %collective-permute-start.16) | collective-permute-done | bytes 393248 | tf_op jit(solution)/shard_map/ppermute | solution.py:250
  293.6 19.1 %shard_map.669 = bf16[1024,2048]{1,0:T(8,128)(2,1)} custom-call(s32[14,32]{1,0:T(8,128)} %pad_add_fusion.table_ref, bf16[256,2048]{1,0:T(8,128)(2,1)} %dynamic-slice_bitcast_fusion.14.refs_0_, bf16[768,512]{1,0:T(8,128)(2,1)} %constant_dynamic-update-slice_fusion.3.refs_1_, bf16[768,512]{1,0:T(8,128)(2,1)} %collective-permute-done.14.refs_2_, ...), custom_call_target="tpu_custom_call" | custom-call | tf_op jit(solution)/shard_map/pallas_call | solution.py:73
  317.0 22.5 %shard_map.667 = bf16[2048,3072]{1,0:T(8,128)(2,1)} custom-call(s32[14,32]{1,0:T(8,128)} %pad_add_fusion.table_ref, bf16[512,3072]{1,0:T(8,128)(2,1)} %copy.116.refs_0_, bf16[1536,768]{1,0:T(8,128)(2,1)} %constant_dynamic-update-slice_fusion.refs_1_, bf16[1536,768]{1,0:T(8,128)(2,1)} %collective-permute-done.7.refs_2_, ...), custom_call_target="tpu_custom_call" | custom-call | tf_op jit(solution)/shard_map/pallas_call | solution.py:73
  341.7 18.4 %add_convert_fusion.q_ref.k_ref.v_ref = bf16[1024,3072]{1,0:T(8,128)(2,1)} fusion(bf16[2048,3072]{1,0:T(8,128)(2,1)} %shard_map.667, f32[3072]{0:T(1024)S(1)} %pad_maximum_fusion.19, bf16[512,2048]{1,0:T(8,128)(2,1)} %collective-permute-done.3, bf16[512,2048]{1,0:T(8,128)(2,1)} %fusion.18), kind=kOutput, calls=%fused_computation.10 | convolution fusion | flops 12899581952 | bytes 23080960 | tf_op jit(solution)/shard_map/dot_general | solution.py:30
  360.1 20.5 %shard_map.668 = bf16[1024,1024]{1,0:T(8,128)(2,1)} custom-call(s32[2]{0:T(128)} %pad_add_fusion.5.scal_ref, bf16[1024,3072]{1,0:T(8,128)(2,1)} %add_convert_fusion.q_ref.k_ref.v_ref, bf16[1024,3072]{1,0:T(8,128)(2,1)} %add_convert_fusion.q_ref.k_ref.v_ref, bf16[1024,3072]{1,0:T(8,128)(2,1)} %add_convert_fusion.q_ref.k_ref.v_ref), custom_call_target="tpu_custom_call" | custom-call | tf_op jit(solution)/shard_map/pallas_call | solution.py:168
  385.8 23.4 %collective-permute-done.21 = bf16[512,1024]{1,0:T(8,128)(2,1)} collective-permute-done((bf16[512,1024]{1,0:T(8,128)(2,1)}, bf16[512,1024]{1,0:T(8,128)(2,1)}, u32[]{:S(2)}, u32[]{:S(2)}) %collective-permute-start.21) | collective-permute-done | bytes 1048608 | tf_op jit(solution)/shard_map/ppermute | solution.py:247
  410.0 32.4 %collective-permute-start.38 = (bf16[256,2048]{1,0:T(8,128)(2,1)S(1)}, bf16[256,2048]{1,0:T(8,128)(2,1)S(1)}, u32[]{:S(2)}, u32[]{:S(2)}) collective-permute-start(bf16[256,2048]{1,0:T(8,128)(2,1)S(1)} %get-tuple-element.83), channel_id=1, source_target_pairs={{0,2},{1,0},{2,6},{3,4},{4,3},{5,1},{6,7},{7,5},{8,10},{9,8},{10,1... | collective-permute-start | bytes 3145736 | tf_op jit(solution)/shard_map/ppermute | solution.py:268
  461.4 37.5 %collective-permute-start.39 = (bf16[512,2048]{1,0:T(8,128)(2,1)S(1)}, bf16[512,2048]{1,0:T(8,128)(2,1)S(1)}, u32[]{:S(2)}, u32[]{:S(2)}) collective-permute-start(bf16[512,2048]{1,0:T(8,128)(2,1)S(1)} %pad_maximum_fusion.13), channel_id=1, source_target_pairs={{0,4},{4,0},{1,5},{5,1},{2,6},{6,2},{3,7},{7,3},{8,12},{12,8},{9,1... | collective-permute-start | bytes 6291464 | tf_op jit(solution)/shard_map/ppermute | solution.py:253
  504.4 20.8 %collective-permute-done.23.refs_2_ = bf16[1536,1024]{1,0:T(8,128)(2,1)S(1)} collective-permute-done((bf16[1536,1024]{1,0:T(8,128)(2,1)S(1)}, bf16[1536,1024]{1,0:T(8,128)(2,1)S(1)}, u32[]{:S(2)}, u32[]{:S(2)}) %collective-permute-start.23) | collective-permute-done | bytes 3145760 | tf_op jit(solution)/shard_map/ppermute | solution.py:250
  529.0 60.9 %collective-permute-done.30.refs_2_ = bf16[3072,512]{1,0:T(8,128)(2,1)S(1)} collective-permute-done((bf16[3072,512]{1,0:T(8,128)(2,1)S(1)}, bf16[3072,512]{1,0:T(8,128)(2,1)S(1)}, u32[]{:S(2)}, u32[]{:S(2)}) %collective-permute-start.30) | collective-permute-done | bytes 3145760 | tf_op jit(solution)/shard_map/ppermute | solution.py:250
  610.4 17.9 collective-permute-done.25.refs_4_
  628.3 24.7 %shard_map.670 = bf16[2048,4096]{1,0:T(8,128)(2,1)} custom-call(s32[14,32]{1,0:T(8,128)} %pad_add_fusion.table_ref, bf16[512,4096]{1,0:T(8,128)(2,1)} %bitcast.219, bf16[1536,1024]{1,0:T(8,128)(2,1)} %copy-done.40, bf16[1536,1024]{1,0:T(8,128)(2,1)} %copy-done.33, bf16[1536,1024]{1,0:T(8,128)(2,1)} %copy-done.35, ...), custom_call_target="tpu_custom_call" | custom-call | tf_op jit(solution)/shard_map/pallas_call | solution.py:73
  659.0 24.7 %shard_map.671 = bf16[4096,2048]{1,0:T(8,128)(2,1)} custom-call(s32[14,32]{1,0:T(8,128)} %pad_add_fusion.table_ref, bf16[1024,2048]{1,0:T(8,128)(2,1)} %dynamic-slice_bitcast_fusion.refs_0_, bf16[3072,512]{1,0:T(8,128)(2,1)} %copy-done.39, bf16[3072,512]{1,0:T(8,128)(2,1)} %copy-done.34, bf16[3072,512]{1,0:T(8,128)(2,1)} %copy-done.36, ...), custom_call_target="tpu_custom_call" | custom-call | tf_op jit(solution)/shard_map/pallas_call | solution.py:73
  683.7 27.9 %multiply_convert_fusion.1 = (bf16[1024,4096]{1,0:T(8,128)(2,1)}, f32[1024,4096]{1,0:T(8,128)}) fusion(f32[4096]{0:T(1024)S(1)} %bitcast.267, bf16[2048,4096]{1,0:T(8,128)(2,1)} %shard_map.670, bf16[512,2048]{1,0:T(8,128)(2,1)} %collective-permute-done.19, bf16[512,2048]{1,0:T(8,128)(2,1)} %add_convert_fusion.3), kind=kOutput, calls=%fused_computation.8 | convolution fusion | flops 17213423616 | bytes 46153728 | tf_op jit(solution)/shard_map/dot_general | solution.py:30
  726.2 32.1 %convert_reduce_fusion = (f32[4096]{0:T(1024)S(1)}, bf16[1024,4096]{1,0:T(8,128)(2,1)}) fusion(f32[1024,4096]{1,0:T(8,128)} %get-tuple-element.127, f32[4096]{0:T(1024)S(1)} %bitcast.268, bf16[4096,2048]{1,0:T(8,128)(2,1)} %shard_map.671, bf16[512,2048]{1,0:T(8,128)(2,1)} %copy-done.53, bf16[256,2048]{1,0:T(8,128)(2,1)S(1)} %copy-done.20, ...), kind=kOutput, calls=%fused_computation.6 | convolution fusion | flops 17255362560 | bytes 46170112 | tf_op jit(solution)/shard_map/dot_general | solution.py:38
  758.2 15.1 fusion.47
  846.9 17.7 multiply_reduce_fusion
  938.2 21.8 %collective-permute-done.36 = bf16[256,2048]{1,0:T(8,128)(2,1)} collective-permute-done((bf16[256,2048]{1,0:T(8,128)(2,1)S(1)}, bf16[256,2048]{1,0:T(8,128)(2,1)}, u32[]{:S(2)}, u32[]{:S(2)}) %collective-permute-start.36) | collective-permute-done | bytes 1048608 | tf_op jit(solution)/shard_map/ppermute | solution.py:277
  970.6 34.3 %shard_map.672 = (bf16[1024,1024]{1,0:T(8,128)(2,1)}, bf16[1024,1024]{1,0:T(8,128)(2,1)}, bf16[1024,1024]{1,0:T(8,128)(2,1)}) custom-call(s32[2]{0:T(128)} %pad_add_fusion.5.scal_ref, bf16[1024,3072]{1,0:T(8,128)(2,1)} %add_convert_fusion.q_ref.k_ref.v_ref, bf16[1024,3072]{1,0:T(8,128)(2,1)} %add_convert_fusion.q_ref.k_ref.v_ref, ...), custom_call_target="tpu_custom_call" | custom-call | tf_op jit(solution)/shard_map/pallas_call | solution.py:184
  1050.6 67.9 %collective-permute-done.57 = bf16[2,256,512]{2,1,0:T(8,128)(2,1)} collective-permute-done((bf16[2,256,512]{2,1,0:T(8,128)(2,1)}, bf16[2,256,512]{2,1,0:T(8,128)(2,1)}, u32[]{:S(2)}, u32[]{:S(2)}) %collective-permute-start.57) | collective-permute-done | bytes 524320 | tf_op jit(solution)/shard_map/ppermute | solution.py:250
  1125.7 18.2 collective-permute-done.60
  1181.1 22.5 %collective-permute-done.47 = bf16[2,512,768]{2,1,0:T(8,128)(2,1)} collective-permute-done((bf16[2,512,768]{2,1,0:T(8,128)(2,1)}, bf16[2,512,768]{2,1,0:T(8,128)(2,1)}, u32[]{:S(2)}, u32[]{:S(2)}) %collective-permute-start.47) | collective-permute-done | bytes 1572896 | tf_op jit(solution)/shard_map/ppermute | solution.py:250
  1215.3 86.6 %collective-permute-done.62 = bf16[256,512]{1,0:T(8,128)(2,1)S(1)} collective-permute-done((bf16[256,512]{1,0:T(8,128)(2,1)S(1)}, bf16[256,512]{1,0:T(8,128)(2,1)S(1)}, u32[]{:S(2)}, u32[]{:S(2)}) %collective-permute-start.62) | collective-permute-done | bytes 262176 | tf_op jit(solution)/shard_map/ppermute | solution.py:247
  1336.8 66.9 %collective-permute-done.86 = bf16[1024,512]{1,0:T(8,128)(2,1)S(1)} collective-permute-done((bf16[1024,512]{1,0:T(8,128)(2,1)S(1)}, bf16[1024,512]{1,0:T(8,128)(2,1)S(1)}, u32[]{:S(2)}, u32[]{:S(2)}) %collective-permute-start.86) | collective-permute-done | bytes 1048608 | tf_op jit(solution)/shard_map/ppermute | solution.py:247
  1432.2 64.3 %collective-permute-done.88 = bf16[1024,512]{1,0:T(8,128)(2,1)} collective-permute-done((bf16[1024,512]{1,0:T(8,128)(2,1)}, bf16[1024,512]{1,0:T(8,128)(2,1)}, u32[]{:S(2)}, u32[]{:S(2)}) %collective-permute-start.88) | collective-permute-done | bytes 1048608 | tf_op jit(solution)/shard_map/ppermute | solution.py:250
  1522.4 46.8 %collective-permute-done.50 = bf16[512,768]{1,0:T(8,128)(2,1)S(1)} collective-permute-done((bf16[512,768]{1,0:T(8,128)(2,1)S(1)}, bf16[512,768]{1,0:T(8,128)(2,1)S(1)}, u32[]{:S(2)}, u32[]{:S(2)}) %collective-permute-start.50) | collective-permute-done | bytes 786464 | tf_op jit(solution)/shard_map/ppermute | solution.py:247
  1638.5 119.8 %all-reduce.2.cloned.1.call-done = f32[4,6144]{1,0:T(4,128)} async-done(((f32[4,6144]{1,0:T(4,128)}), f32[4,6144]{1,0:T(4,128)}) %all-reduce.2.cloned.1.call-update) | async-done | bytes 98320 | tf_op jit(solution)/shard_map/psum | solution.py:548
  1775.2 14.6 shard_map.676
  1789.9 14.6 shard_map.675
  1804.5 28.4 %shard_map.673 = f32[512,6144]{1,0:T(8,128)} custom-call(s32[6,48]{1,0:T(8,128)} %pad_add_fusion.3.table_ref, bf16[2048,768]{1,0:T(8,128)(2,1)} %constant_dynamic-update-slice_fusion.24.refs_0_, bf16[2048,768]{1,0:T(8,128)(2,1)} %collective-permute-done.56.refs_1_), custom_call_target="tpu_custom_call" | custom-call | tf_op jit(solution)/shard_map/pallas_call | solution.py:73
  (633 shorter events, 635.5 us)
Async XLA Ops:
  7.2 1751.2 %all-reduce.2.cloned.1.call-start = ((), (), s32[]{:S(2)}) async-start(), calls=%async_computation | async-start | bytes 196608 | tf_op jit(solution)/shard_map/psum | solution.py:548
  26.6 138.8 %collective-permute-start.4 = (bf16[512,768]{1,0:T(8,128)(2,1)}, bf16[512,768]{1,0:T(8,128)(2,1)}, u32[]{:S(2)}, u32[]{:S(2)}) collective-permute-start(bf16[512,768]{1,0:T(8,128)(2,1)} %constant_dynamic-slice_fusion.5), channel_id=1, source_target_pairs={{0,1},{1,2},{2,3},{3,0},{4,5},{5,6},{6,7},{7,4},{8,9},{9,10},{10,1... | collective-permute-start | bytes 2359304 | tf_op jit(solution)/shard_map/ppermute | solution.py:247
  29.7 135.8 %collective-permute-start.5 = (bf16[512,768]{1,0:T(8,128)(2,1)}, bf16[512,768]{1,0:T(8,128)(2,1)}, u32[]{:S(2)}, u32[]{:S(2)}) collective-permute-start(bf16[512,768]{1,0:T(8,128)(2,1)} %constant_dynamic-slice_fusion.5), channel_id=1, source_target_pairs={{0,2},{1,3},{2,0},{3,1},{4,6},{5,7},{6,4},{7,5},{8,10},{9,11},{10,... | collective-permute-start | bytes 2359304 | tf_op jit(solution)/shard_map/ppermute | solution.py:247
  32.2 140.2 %collective-permute-start.6 = (bf16[512,768]{1,0:T(8,128)(2,1)}, bf16[512,768]{1,0:T(8,128)(2,1)}, u32[]{:S(2)}, u32[]{:S(2)}) collective-permute-start(bf16[512,768]{1,0:T(8,128)(2,1)} %constant_dynamic-slice_fusion.5), channel_id=1, source_target_pairs={{0,3},{1,0},{2,1},{3,2},{4,7},{5,4},{6,5},{7,6},{8,11},{9,8},{10,9... | collective-permute-start | bytes 2359304 | tf_op jit(solution)/shard_map/ppermute | solution.py:247
  36.7 151.8 %collective-permute-start = (bf16[256,2048]{1,0:T(8,128)(2,1)}, bf16[256,2048]{1,0:T(8,128)(2,1)S(1)}, u32[]{:S(2)}, u32[]{:S(2)}) collective-permute-start(bf16[256,2048]{1,0:T(8,128)(2,1)} %get-tuple-element.90), channel_id=1, source_target_pairs={{0,0},{1,2},{2,4},{3,6},{4,1},{5,3},{6,5},{7,7},{8,8},{9,10},{10,1... | collective-permute-start | bytes 3145736 | tf_op jit(solution)/shard_map/ppermute | solution.py:268
  38.6 150.9 %collective-permute-start.1 = (bf16[256,2048]{1,0:T(8,128)(2,1)}, bf16[256,2048]{1,0:T(8,128)(2,1)}, u32[]{:S(2)}, u32[]{:S(2)}) collective-permute-start(bf16[256,2048]{1,0:T(8,128)(2,1)} %get-tuple-element.91), channel_id=1, source_target_pairs={{0,2},{1,0},{2,6},{3,4},{4,3},{5,1},{6,7},{7,5},{8,10},{9,8},{10,1... | collective-permute-start | bytes 3145736 | tf_op jit(solution)/shard_map/ppermute | solution.py:268
  195.0 144.5 %collective-permute-start.3 = (bf16[512,2048]{1,0:T(8,128)(2,1)}, bf16[512,2048]{1,0:T(8,128)(2,1)}, u32[]{:S(2)}, u32[]{:S(2)}) collective-permute-start(bf16[512,2048]{1,0:T(8,128)(2,1)} %fusion.18), channel_id=1, source_target_pairs={{0,4},{4,0},{1,5},{5,1},{2,6},{6,2},{3,7},{7,3},{8,12},{12,8},{9,1... | collective-permute-start | bytes 6291464 | tf_op jit(solution)/shard_map/ppermute | solution.py:253
  292.7 116.5 %collective-permute-start.21 = (bf16[512,1024]{1,0:T(8,128)(2,1)}, bf16[512,1024]{1,0:T(8,128)(2,1)}, u32[]{:S(2)}, u32[]{:S(2)}) collective-permute-start(bf16[512,1024]{1,0:T(8,128)(2,1)} %constant_dynamic-slice_fusion.2), channel_id=1, source_target_pairs={{0,2},{1,3},{2,0},{3,1},{4,6},{5,7},{6,4},{7,5},{8,10},{9,11},{10,... | collective-permute-start | bytes 3145736 | tf_op jit(solution)/shard_map/ppermute | solution.py:247
  316.3 137.9 %collective-permute-start.28 = (bf16[1024,512]{1,0:T(8,128)(2,1)}, bf16[1024,512]{1,0:T(8,128)(2,1)}, u32[]{:S(2)}, u32[]{:S(2)}) collective-permute-start(bf16[1024,512]{1,0:T(8,128)(2,1)} %dynamic-slice_bitcast_fusion.13), channel_id=1, source_target_pairs={{0,2},{1,3},{2,0},{3,1},{4,6},{5,7},{6,4},{7,5},{8,10},{9,11},{10,... | collective-permute-start | bytes 3145736 | tf_op jit(solution)/shard_map/ppermute | solution.py:247
  339.5 116.5 %collective-permute-start.29 = (bf16[1024,512]{1,0:T(8,128)(2,1)}, bf16[1024,512]{1,0:T(8,128)(2,1)}, u32[]{:S(2)}, u32[]{:S(2)}) collective-permute-start(bf16[1024,512]{1,0:T(8,128)(2,1)} %dynamic-slice_bitcast_fusion.13), channel_id=1, source_target_pairs={{0,3},{1,0},{2,1},{3,2},{4,7},{5,4},{6,5},{7,6},{8,11},{9,8},{10,9... | collective-permute-start | bytes 3145736 | tf_op jit(solution)/shard_map/ppermute | solution.py:247
  458.0 131.9 %collective-permute-start.30 = (bf16[3072,512]{1,0:T(8,128)(2,1)S(1)}, bf16[3072,512]{1,0:T(8,128)(2,1)S(1)}, u32[]{:S(2)}, u32[]{:S(2)}) collective-permute-start(bf16[3072,512]{1,0:T(8,128)(2,1)S(1)} %constant_dynamic-update-slice_fusion.9.refs_1_), channel_id=1, source_target_pairs={{0,8},{8,0},{16,24},{24,16},{1,9},{9,1},{17,25},{25,17},{2,10},{10... | collective-permute-start | bytes 9437192 | tf_op jit(solution)/shard_map/ppermute | solution.py:250
  459.5 135.0 %collective-permute-start.31 = (bf16[3072,512]{1,0:T(8,128)(2,1)S(1)}, bf16[3072,512]{1,0:T(8,128)(2,1)S(1)}, u32[]{:S(2)}, u32[]{:S(2)}) collective-permute-start(bf16[3072,512]{1,0:T(8,128)(2,1)S(1)} %constant_dynamic-update-slice_fusion.9.refs_1_), channel_id=1, source_target_pairs={{0,16},{8,24},{16,0},{24,8},{1,17},{9,25},{17,1},{25,9},{2,18},{10... | collective-permute-start | bytes 9437192 | tf_op jit(solution)/shard_map/ppermute | solution.py:250
  461.4 135.4 %collective-permute-start.39 = (bf16[512,2048]{1,0:T(8,128)(2,1)S(1)}, bf16[512,2048]{1,0:T(8,128)(2,1)S(1)}, u32[]{:S(2)}, u32[]{:S(2)}) collective-permute-start(bf16[512,2048]{1,0:T(8,128)(2,1)S(1)} %pad_maximum_fusion.13), channel_id=1, source_target_pairs={{0,4},{4,0},{1,5},{5,1},{2,6},{6,2},{3,7},{7,3},{8,12},{12,8},{9,1... | collective-permute-start | bytes 6291464 | tf_op jit(solution)/shard_map/ppermute | solution.py:253
  525.2 158.6 %collective-permute-start.19 = (bf16[512,2048]{1,0:T(8,128)(2,1)}, bf16[512,2048]{1,0:T(8,128)(2,1)}, u32[]{:S(2)}, u32[]{:S(2)}) collective-permute-start(bf16[512,2048]{1,0:T(8,128)(2,1)} %add_convert_fusion.3), channel_id=1, source_target_pairs={{0,4},{4,0},{1,5},{5,1},{2,6},{6,2},{3,7},{7,3},{8,12},{12,8},{9,1... | collective-permute-start | bytes 6291464 | tf_op jit(solution)/shard_map/ppermute | solution.py:253
  527.1 101.2 %collective-permute-start.25 = (bf16[768,1024]{1,0:T(8,128)(2,1)}, bf16[768,1024]{1,0:T(8,128)(2,1)}, u32[]{:S(2)}, u32[]{:S(2)}) collective-permute-start(bf16[768,1024]{1,0:T(8,128)(2,1)} %bitcast.21), channel_id=1, source_target_pairs={{0,16},{8,24},{16,0},{24,8},{1,17},{9,25},{17,1},{25,9},{2,18},{10... | collective-permute-start | bytes 4718600 | tf_op jit(solution)/shard_map/ppermute | solution.py:250
  726.2 145.2 %collective-permute-start.34 = (bf16[512,2048]{1,0:T(8,128)(2,1)}, bf16[512,2048]{1,0:T(8,128)(2,1)}, u32[]{:S(2)}, u32[]{:S(2)}) collective-permute-start(bf16[512,2048]{1,0:T(8,128)(2,1)} %fusion.44), channel_id=1, source_target_pairs={{0,4},{4,0},{1,5},{5,1},{2,6},{6,2},{3,7},{7,3},{8,12},{12,8},{9,1... | collective-permute-start | bytes 6291464 | tf_op jit(solution)/shard_map/ppermute | solution.py:253
  822.8 101.0 %collective-permute-start.83 = (bf16[2,1024,512]{2,1,0:T(8,128)(2,1)}, bf16[2,1024,512]{2,1,0:T(8,128)(2,1)}, u32[]{:S(2)}, u32[]{:S(2)}) collective-permute-start(bf16[2,1024,512]{2,1,0:T(8,128)(2,1)} %bitcast.95), channel_id=1, source_target_pairs={{0,8},{8,0},{16,24},{24,16},{1,9},{9,1},{17,25},{25,17},{2,10},{10... | collective-permute-start | bytes 6291464 | tf_op jit(solution)/shard_map/ppermute | solution.py:250
  923.8 245.6 %collective-permute-start.72 = (bf16[4,512,1024]{2,1,0:T(8,128)(2,1)}, bf16[4,512,1024]{2,1,0:T(8,128)(2,1)}, u32[]{:S(2)}, u32[]{:S(2)}) collective-permute-start(bf16[4,512,1024]{2,1,0:T(8,128)(2,1)} %pad_maximum_fusion.6), channel_id=1, source_target_pairs={{0,16},{8,24},{16,0},{24,8},{1,17},{9,25},{17,1},{25,9},{2,18},{10... | collective-permute-start | bytes 12582920 | tf_op jit(solution)/shard_map/ppermute | solution.py:250
  929.4 241.7 %collective-permute-start.70 = (bf16[4,512,1024]{2,1,0:T(8,128)(2,1)}, bf16[4,512,1024]{2,1,0:T(8,128)(2,1)}, u32[]{:S(2)}, u32[]{:S(2)}) collective-permute-start(bf16[4,512,1024]{2,1,0:T(8,128)(2,1)} %pad_maximum_fusion.5), channel_id=1, source_target_pairs={{0,8},{8,0},{16,24},{24,16},{1,9},{9,1},{17,25},{25,17},{2,10},{10... | collective-permute-start | bytes 12582920 | tf_op jit(solution)/shard_map/ppermute | solution.py:250
  937.3 268.4 %collective-permute-start.84 = (bf16[4,1024,512]{2,1,0:T(8,128)(2,1)}, bf16[4,1024,512]{2,1,0:T(8,128)(2,1)}, u32[]{:S(2)}, u32[]{:S(2)}) collective-permute-start(bf16[4,1024,512]{2,1,0:T(8,128)(2,1)} %pad_maximum_fusion.8), channel_id=1, source_target_pairs={{0,16},{8,24},{16,0},{24,8},{1,17},{9,25},{17,1},{25,9},{2,18},{10... | collective-permute-start | bytes 12582920 | tf_op jit(solution)/shard_map/ppermute | solution.py:250
  1047.9 157.8 %collective-permute-start.82 = (bf16[4,1024,512]{2,1,0:T(8,128)(2,1)S(1)}, bf16[4,1024,512]{2,1,0:T(8,128)(2,1)}, u32[]{:S(2)}, u32[]{:S(2)}) collective-permute-start(bf16[4,1024,512]{2,1,0:T(8,128)(2,1)S(1)} %copy-done.43), channel_id=1, source_target_pairs={{0,8},{8,0},{16,24},{24,16},{1,9},{9,1},{17,25},{25,17},{2,10},{10... | collective-permute-start | bytes 12582920 | tf_op jit(solution)/shard_map/ppermute | solution.py:250
  1203.6 101.0 %collective-permute-start.75 = (bf16[512,1024]{1,0:T(8,128)(2,1)}, bf16[512,1024]{1,0:T(8,128)(2,1)S(1)}, u32[]{:S(2)}, u32[]{:S(2)}) collective-permute-start(bf16[512,1024]{1,0:T(8,128)(2,1)} %get-tuple-element.58), channel_id=1, source_target_pairs={{0,3},{1,0},{2,1},{3,2},{4,7},{5,4},{6,5},{7,6},{8,11},{9,8},{10,9... | collective-permute-start | bytes 3145736 | tf_op jit(solution)/shard_map/ppermute | solution.py:247
  1204.5 102.9 %collective-permute-start.74 = (bf16[512,1024]{1,0:T(8,128)(2,1)}, bf16[512,1024]{1,0:T(8,128)(2,1)S(1)}, u32[]{:S(2)}, u32[]{:S(2)}) collective-permute-start(bf16[512,1024]{1,0:T(8,128)(2,1)} %get-tuple-element.59), channel_id=1, source_target_pairs={{0,2},{1,3},{2,0},{3,1},{4,6},{5,7},{6,4},{7,5},{8,10},{9,11},{10,... | collective-permute-start | bytes 3145736 | tf_op jit(solution)/shard_map/ppermute | solution.py:247
  1204.5 103.5 %collective-permute-start.73 = (bf16[512,1024]{1,0:T(8,128)(2,1)}, bf16[512,1024]{1,0:T(8,128)(2,1)}, u32[]{:S(2)}, u32[]{:S(2)}) collective-permute-start(bf16[512,1024]{1,0:T(8,128)(2,1)} %get-tuple-element.57), channel_id=1, source_target_pairs={{0,1},{1,2},{2,3},{3,0},{4,5},{5,6},{6,7},{7,4},{8,9},{9,10},{10,1... | collective-permute-start | bytes 3145736 | tf_op jit(solution)/shard_map/ppermute | solution.py:247
  1205.7 202.2 %collective-permute-start.42 = (bf16[512,2048]{1,0:T(8,128)(2,1)}, bf16[512,2048]{1,0:T(8,128)(2,1)}, u32[]{:S(2)}, u32[]{:S(2)}) collective-permute-start(bf16[512,2048]{1,0:T(8,128)(2,1)} %fusion.41), channel_id=1, source_target_pairs={{0,4},{4,0},{1,5},{5,1},{2,6},{6,2},{3,7},{7,3},{8,12},{12,8},{9,1... | collective-permute-start | bytes 6291464 | tf_op jit(solution)/shard_map/ppermute | solution.py:253
  1334.9 166.1 %collective-permute-start.48 = (bf16[4,512,768]{2,1,0:T(8,128)(2,1)}, bf16[4,512,768]{2,1,0:T(8,128)(2,1)S(1)}, u32[]{:S(2)}, u32[]{:S(2)}) collective-permute-start(bf16[4,512,768]{2,1,0:T(8,128)(2,1)} %pad_maximum_fusion.10), channel_id=1, source_target_pairs={{0,16},{8,24},{16,0},{24,8},{1,17},{9,25},{17,1},{25,9},{2,18},{10... | collective-permute-start | bytes 9437192 | tf_op jit(solution)/shard_map/ppermute | solution.py:250
  1403.7 97.4 %collective-permute-start.46 = (bf16[4,512,768]{2,1,0:T(8,128)(2,1)}, bf16[4,512,768]{2,1,0:T(8,128)(2,1)S(1)}, u32[]{:S(2)}, u32[]{:S(2)}) collective-permute-start(bf16[4,512,768]{2,1,0:T(8,128)(2,1)} %pad_maximum_fusion.9), channel_id=1, source_target_pairs={{0,8},{8,0},{16,24},{24,16},{1,9},{9,1},{17,25},{25,17},{2,10},{10... | collective-permute-start | bytes 9437192 | tf_op jit(solution)/shard_map/ppermute | solution.py:250
  1522.4 267.5 %collective-permute-start.80 = (bf16[2048,1024]{1,0:T(8,128)(2,1)}, bf16[2048,1024]{1,0:T(8,128)(2,1)}, u32[]{:S(2)}, u32[]{:S(2)}) collective-permute-start(bf16[2048,1024]{1,0:T(8,128)(2,1)} %constant_dynamic-update-slice_fusion.34.refs_0_), channel_id=1, source_target_pairs={{0,4},{4,0},{1,5},{5,1},{2,6},{6,2},{3,7},{7,3},{8,12},{12,8},{9,1... | collective-permute-start | bytes 12582920 | tf_op jit(solution)/shard_map/ppermute | solution.py:253
  1572.3 202.9 %collective-permute-start.92 = (bf16[4096,512]{1,0:T(8,128)(2,1)}, bf16[4096,512]{1,0:T(8,128)(2,1)}, u32[]{:S(2)}, u32[]{:S(2)}) collective-permute-start(bf16[4096,512]{1,0:T(8,128)(2,1)} %constant_dynamic-update-slice_fusion.39.refs_0_), channel_id=1, source_target_pairs={{0,4},{4,0},{1,5},{5,1},{2,6},{6,2},{3,7},{7,3},{8,12},{12,8},{9,1... | collective-permute-start | bytes 12582920 | tf_op jit(solution)/shard_map/ppermute | solution.py:253
  1606.0 198.6 %collective-permute-start.56 = (bf16[2048,768]{1,0:T(8,128)(2,1)}, bf16[2048,768]{1,0:T(8,128)(2,1)}, u32[]{:S(2)}, u32[]{:S(2)}) collective-permute-start(bf16[2048,768]{1,0:T(8,128)(2,1)} %constant_dynamic-update-slice_fusion.24.refs_0_), channel_id=1, source_target_pairs={{0,4},{4,0},{1,5},{5,1},{2,6},{6,2},{3,7},{7,3},{8,12},{12,8},{9,1... | collective-permute-start | bytes 9437192 | tf_op jit(solution)/shard_map/ppermute | solution.py:253
  1617.5 143.9 %collective-permute-start.44 = (bf16[256,2048]{1,0:T(8,128)(2,1)}, bf16[256,2048]{1,0:T(8,128)(2,1)}, u32[]{:S(2)}, u32[]{:S(2)}) collective-permute-start(bf16[256,2048]{1,0:T(8,128)(2,1)} %get-tuple-element.79), channel_id=1, source_target_pairs={{2,0},{0,1},{6,2},{4,3},{3,4},{1,5},{7,6},{5,7},{10,8},{8,9},{14,1... | collective-permute-start | bytes 3145736 | tf_op jit(solution)/shard_map/ppermute | solution.py:277
  1624.5 140.0 %collective-permute-start.68 = (bf16[1024,512]{1,0:T(8,128)(2,1)}, bf16[1024,512]{1,0:T(8,128)(2,1)}, u32[]{:S(2)}, u32[]{:S(2)}) collective-permute-start(bf16[1024,512]{1,0:T(8,128)(2,1)} %constant_dynamic-update-slice_fusion.29.refs_0_), channel_id=1, source_target_pairs={{0,4},{4,0},{1,5},{5,1},{2,6},{6,2},{3,7},{7,3},{8,12},{12,8},{9,1... | collective-permute-start | bytes 3145736 | tf_op jit(solution)/shard_map/ppermute | solution.py:253
  (180 other events, 6761.9 us)
Sparse Core Ops, SparseCore 0:
  1620.9 137.4 all-reduce.1

commit v2 on v1

--- a/solution.py
+++ b/solution.py
@@ -42,7 +42,7 @@
     return lax.optimization_barrier((value, other))[0]
 
 
-def place(sources, steps, dest_rows, dest_cols, block, out_shape, out_dtype):
+def place(sources, steps, dest_rows, dest_cols, block, out_shape, out_dtype, offset=None):
     count = len(steps)
     spans = []
     table = []
@@ -53,8 +53,12 @@
         hold = [steps[min(max(i, first), last)] for i in range(count)]
         table.append([step[1] for step in hold])
         table.append([step[2] for step in hold])
+    fixed = jnp.asarray(np.array(table, np.int32))
+    if offset is not None:
+        mask = lax.broadcasted_iota(jnp.int32, (fixed.shape[0], 1), 0)
+        fixed = fixed + jnp.where(mask == 0, offset[0], jnp.where(mask == 1, offset[1], 0))
     table = jnp.concatenate(
-        [jnp.asarray(np.array(table, np.int32)), dest_rows.astype(jnp.int32)[None], dest_cols.astype(jnp.int32)[None]]
+        [fixed, dest_rows.astype(jnp.int32)[None], dest_cols.astype(jnp.int32)[None]]
     )
     last_row = 2 * len(sources)
 
@@ -284,138 +288,141 @@
         even = shard % 2 == 0
         return jnp.stack([jnp.where(even, got[0], got[1]), jnp.where(even, got[1], got[0])])
 
-    def start_pieces(mine, barrier=None):
-        cut = mine.shape[1] // chips
-        piece = lax.dynamic_slice_in_dim(mine, ch * cut, cut, 1)
-        if barrier is not None:
-            piece = after(piece, barrier)
-        return [along(piece, hop) for hop in range(1, shards)], piece
-
-    def finish_pieces(mine, got, piece, barrier=None):
-        height, total = mine.shape
-        cut = total // chips
-        if chips != 4:
-            stacked = jnp.stack([piece] + got)
-            everything = lax.all_gather(stacked, "ch")
-            everything = jnp.take(everything, (shard - jnp.arange(shards)) % shards, axis=1)
-            return everything.transpose(1, 2, 0, 3).reshape(shards * height, total)
-        others = jnp.concatenate(got)
-        if barrier is not None:
-            others = after(others, barrier)
+    def gather_shards(piece):
+        held = lax.all_gather(piece, "sh")
+        return [lax.dynamic_index_in_dim(held, (shard - hop) % shards, 0, False) for hop in range(1, shards)]
+
+    def spread_others(others):
         from_x = plane(others, 1)
         from_y = plane(others, 2)
-        tall = (shards - 1, 2, height // 2, cut)
-        low_part = plane(from_x.reshape(tall)[:, 0].reshape(-1, cut), 2)
-        high_part = plane(from_y.reshape(tall)[:, 1].reshape(-1, cut), 1)
+        tall = (shards - 1, 2, others.shape[0] // (2 * (shards - 1)), others.shape[1])
+        low_cut = from_x.reshape(tall)[:, 0].reshape(-1, tall[3])
+        high_cut = from_y.reshape(tall)[:, 1].reshape(-1, tall[3])
+        return from_x, from_y, low_cut, high_cut
+
+    def whole_weight(source, offset, col_step, height, others, from_x, from_y, low_part, high_part):
+        cut = others.shape[1]
         steps, hops, flips, cols, halves = [], [], [], [], []
         for half in range(2):
             for col in range(chips):
-                steps.append((0, half, col))
+                steps.append((0, half, col * col_step))
                 hops.append(0), flips.append(-1), cols.append(col), halves.append(half)
-        for source, flip in ((1, 0), (2, 1), (3, 2)):
+        for which, flip in ((1, 0), (2, 1), (3, 2)):
             for hop in range(1, shards):
                 for half in range(2):
-                    steps.append((source, 2 * (hop - 1) + half, 0))
+                    steps.append((which, 2 * (hop - 1) + half, 0))
                     hops.append(hop), flips.append(flip), cols.append(0), halves.append(half)
-        for source, half in ((4, 0), (5, 1)):
+        for which, half in ((4, 0), (5, 1)):
             for hop in range(1, shards):
-                steps.append((source, hop - 1, 0))
+                steps.append((which, hop - 1, 0))
                 hops.append(hop), flips.append(3), cols.append(0), halves.append(half)
         hops, flips, cols, halves = (np.array(v, np.int32) for v in (hops, flips, cols, halves))
-        dest_rows = 2 * ((shard - hops) % shards) + halves
-        dest_cols = jnp.where(flips < 0, cols, ch ^ np.maximum(flips, 0))
         return place(
-            [mine, others, from_x, from_y, low_part, high_part],
+            [source, others, from_x, from_y, low_part, high_part],
             steps,
-            dest_rows,
-            dest_cols,
+            2 * ((shard - hops) % shards) + halves,
+            jnp.where(flips < 0, cols, ch ^ np.maximum(flips, 0)),
             (height // 2, cut),
-            (shards * height, total),
+            (shards * height, chips * cut),
             BF,
+            offset,
         )
 
-    def reduce_grad(left_side, right_side):
-        total = right_side.shape[1]
-        cut = total // chips
-        if chips != 4:
-            grads = cross_rows(left_side, right_side).astype(BF)
-            grads = grads.reshape(shards, -1, chips, cut).transpose(2, 0, 1, 3)
-            mine = lax.psum_scatter(grads, "ch", scatter_dimension=0, tiled=False)
-        else:
-            middle_at = shards // 2
-
-            def quarter(flip):
-                block = lax.dynamic_slice_in_dim(right_side, (ch ^ flip) * cut, cut, 1)
-                return cross_rows(left_side, block).astype(BF).reshape(shards, -1, cut)
-
-            far = quarter(3)
-            from_y = plane(far[:middle_at], 2)
-            from_x = plane(far[middle_at:], 1)
-            near_x = quarter(1)
-            near_y = quarter(2)
-            near_x = jnp.concatenate([near_x[:middle_at] + from_y, near_x[middle_at:]])
-            near_y = jnp.concatenate([near_y[:middle_at], near_y[middle_at:] + from_x])
-            sum_x = plane(near_x, 1)
-            sum_y = plane(near_y, 2)
-            mine = (quarter(0).astype(F32) + sum_x.astype(F32) + sum_y.astype(F32)).astype(BF)
-        got = [
-            along(lax.dynamic_index_in_dim(mine, (shard + hop) % shards, 0, False), hop) for hop in range(1, shards)
-        ]
-        final = lax.dynamic_index_in_dim(mine, shard, 0, False).astype(F32)
-        for member in got:
-            final = final + member.astype(F32)
-        return final.astype(BF)
-
-    def spread_grad(mine, chunk):
-        height, cut = mine.shape
-        if chips != 4:
-            own = lax.all_gather(mine, "ch", axis=1, tiled=True)
-            other = swap(own)
-            pair = [jnp.where(core == 0, own, other), jnp.where(core == 0, other, own)]
-            if chunk is None:
-                return jnp.concatenate(pair).astype(F32)
-            wide = jnp.stack([member.reshape(height, -1, chunk) for member in pair], axis=2)
-            return wide.reshape(height, -1).astype(F32)
+    def whole_weight_any(piece):
+        everything = lax.all_gather(lax.all_gather(piece, "sh"), "ch")
+        return everything.transpose(1, 2, 0, 3).reshape(-1, chips * piece.shape[1])
+
+    def grad_block(left_side, right_side, flip, half=None):
+        cut = right_side.shape[1] // chips
+        block = lax.dynamic_slice_in_dim(right_side, (ch ^ flip) * cut, cut, 1)
+        if half is not None:
+            width_half = left_side.shape[1] // 2
+            left_side = left_side[:, half * width_half : (half + 1) * width_half]
+        return cross_rows(left_side, block).astype(BF)
+
+    def sum_shards(mine):
+        return lax.psum_scatter(mine, "sh", scatter_dimension=0, tiled=True)
+
+    def sum_any(left_side, right_side):
+        cut = right_side.shape[1] // chips
+        grads = cross_rows(left_side, right_side).astype(BF).reshape(-1, chips, cut).transpose(1, 0, 2)
+        return sum_shards(lax.psum_scatter(grads, "ch", scatter_dimension=0))
+
+    def spread_any(mine, chunk):
+        height = mine.shape[0]
+        own = lax.all_gather(mine, "ch", axis=1, tiled=True)
+        other = swap(own)
+        pair = [jnp.where(core == 0, own, other), jnp.where(core == 0, other, own)]
+        if chunk is None:
+            return jnp.concatenate(pair).astype(F32)
+        wide = jnp.stack([member.reshape(height, -1, chunk) for member in pair], axis=2)
+        return wide.reshape(height, -1).astype(F32)
+
+    def spread_first(mine):
         from_x = plane(mine, 1)
         from_y = plane(mine, 2)
-        low_part = plane(from_x[: height // 2], 2)
-        high_part = plane(from_y[height // 2 :], 1)
+        return mine, from_x, from_y
+
+    def spread_second(mine, from_x, from_y):
+        middle_row = mine.shape[0] // 2
+        low_part = plane(from_x[:middle_row], 2)
+        high_part = plane(from_y[middle_row:], 1)
         own = jnp.concatenate([mine, from_x, from_y, low_part, high_part])
-        other = swap(own)
-        block_cols = cut if chunk is None else min(cut, chunk)
+        return own, swap(own)
+
+    def spread_last(own, other, chunk):
+        height, cut = own.shape[0] // 4, own.shape[1]
+        block_cols = cut if chunk is None else chunk
         per = cut // block_cols
-        steps, flips, halves, cores, inner = [], [], [], [], []
+        steps, flips, cores, inner = [], [], [], []
         for source in range(2):
             for flip in range(4):
-                for half in range(2):
-                    for at in range(per):
-                        steps.append((source, 2 * flip + half, at))
-                        flips.append(flip), halves.append(half), cores.append(source), inner.append(at)
-        flips, halves, cores, inner = (np.array(v, np.int32) for v in (flips, halves, cores, inner))
+                for at in range(per):
+                    steps.append((source, flip, at))
+                    flips.append(flip), cores.append(source), inner.append(at)
+        flips, cores, inner = (np.array(v, np.int32) for v in (flips, cores, inner))
         side = core ^ cores
         cols = (ch ^ flips) * per + inner
         if chunk is None:
-            dest_rows, dest_cols, shape = 2 * side + halves, cols, (2 * height, chips * cut)
+            dest_rows, dest_cols, shape = side, cols, (2 * height, chips * cut)
         else:
-            step_cols = chunk // block_cols
-            dest_rows = jnp.asarray(halves)
-            dest_cols = ((cols // step_cols) * 2 + side) * step_cols + cols % step_cols
-            shape = (height, 2 * chips * cut)
-        return place([own, other], steps, dest_rows, dest_cols, (height // 2, block_cols), shape, F32)
+            dest_rows, dest_cols, shape = 0 * side, cols * 2 + side, (height, 2 * chips * cut)
+        return place([own, other], steps, dest_rows, dest_cols, (height, block_cols), shape, F32)
 
     def take(value, axis):
         return lax.dynamic_index_in_dim(value, core, axis, False)
 
-    qkv_mine = take(qkv_weight.reshape(piece_rows, 3 * shards, CORES, -1), 2).reshape(piece_rows, -1)
-    out_mine = take(out_weight.reshape(CORES, piece_rows // CORES, width), 0)
-    fc1_mine = take(fc1_weight.reshape(piece_rows, shards, CORES, -1), 2).reshape(piece_rows, -1)
-    fc2_mine = take(fc2_weight.reshape(CORES, -1, width), 0)
+    qkv_chunk = width // (shards * CORES)
+    fc1_chunk = ff_units // (shards * CORES)
+
+    def col_chunks(value, chunk, first, count):
+        cuts = [lax.dynamic_slice_in_dim(value, ((first + i) * CORES + core) * chunk, chunk, 1) for i in range(count)]
+        return cuts[0] if count == 1 else jnp.concatenate(cuts, axis=1)
+
+    def col_piece(value, chunk):
+        per = value.shape[1] // (CORES * chips * chunk)
+        return col_chunks(value, chunk, ch * per, per)
+
+    def row_piece(value):
+        height, cut = value.shape[0] // CORES, value.shape[1] // chips
+        return lax.dynamic_slice(value, (core * height, ch * cut), (height, cut))
+
+    qkv_piece = col_piece(qkv_weight, qkv_chunk)
+    fc1_piece = col_piece(fc1_weight, fc1_chunk)
+    out_piece = row_piece(out_weight)
+    fc2_piece = row_piece(fc2_weight)
 
     vectors = [ln1_gain, ln1_bias, q_bias, v_bias, out_bias, ln2_gain, ln2_bias, fc2_bias, fc1_bias]
     lengths = [v.shape[0] for v in vectors]
     edges = np.cumsum([0] + lengths)
-    gathered = lax.all_gather(jnp.concatenate(vectors), "sh").astype(F32)
-    vec = [gathered[:, edges[i] : edges[i + 1]] for i in range(len(vectors))]
+    square = chips == 4
+    small = jnp.concatenate(vectors)
+    if square:
+        qkv_others = jnp.concatenate(gather_shards(qkv_piece))
+        small = after(small, qkv_others)
+    ring = [small] + [along(small, hop) for hop in range(shards - 1, 0, -1)]
+    gathered = lax.dynamic_slice_in_dim(jnp.stack(ring + ring), (shards - shard) % shards, shards, 0)
+    vec = [gathered[:, edges[i] : edges[i + 1]].astype(F32) for i in range(len(vectors))]
     gain_one, shift_one, _, _, bias_out, gain_two, shift_two, bias_down, _ = [v.reshape(-1) for v in vec]
     bias_query, bias_value, bias_up = [
         take(vec[i].reshape(shards, CORES, -1), 1).reshape(-1) for i in (2, 3, 8)
@@ -424,20 +431,53 @@
     prefix_pair = [jnp.where(core == 0, a, b) for a, b in ((prefix, swap(prefix)), (swap(prefix), prefix))]
     prefix_len = jnp.concatenate(prefix_pair, axis=1).reshape(-1)[sequence]
 
-    tokens = tokens_in(hidden_in)
-    qkv_got, qkv_piece = start_pieces(qkv_mine)
-    out_got, out_piece = start_pieces(out_mine, (qkv_got[0], qkv_got[1]))
-    fc1_got, fc1_piece = start_pieces(fc1_mine, qkv_got[-1])
-    fc2_got, fc2_piece = start_pieces(fc2_mine, fc1_got[-1])
-    grads_mine = tokens_in(after(grad_out, fc1_got[-1]))
+    tokens = lax.optimization_barrier(tokens_in(after(hidden_in, small)))
+    if square:
+        out_others = jnp.concatenate(gather_shards(out_piece))
+        fc1_others = jnp.concatenate(gather_shards(fc1_piece))
+        fc2_others = jnp.concatenate(gather_shards(fc2_piece))
+        qkv_x, qkv_y, qkv_low, qkv_high = spread_others(qkv_others)
+        out_others = after(out_others, (qkv_x, qkv_y))
+        out_x, out_y, out_low, out_high = spread_others(out_others)
+        fc1_others = after(fc1_others, (qkv_low, qkv_high, out_others))
+        fc1_x, fc1_y, fc1_low, fc1_high = spread_others(fc1_others)
+        fc2_others = after(fc2_others, (fc1_low, fc1_high))
+        fc2_x, fc2_y, fc2_low, fc2_high = spread_others(fc2_others)
 
     hidden_f = tokens.astype(F32)
     normed_own = normalize(hidden_f, gain_one, shift_one).astype(BF)
     normed_one = jnp.concatenate([normed_own, swap(normed_own)])
-    qkv_full = finish_pieces(qkv_mine, qkv_got, qkv_piece)
-    out_full = finish_pieces(out_mine, out_got, out_piece)
-    fc1_full = finish_pieces(fc1_mine, fc1_got, fc1_piece)
-    fc2_full = finish_pieces(fc2_mine, fc2_got, fc2_piece)
+    none = jnp.zeros((), jnp.int32)
+    if square:
+        normed_one = after(normed_one, fc1_others)
+        qkv_mine = col_chunks(qkv_weight, qkv_chunk, 0, 3 * shards)
+        qkv_full = whole_weight(
+            qkv_mine, None, 1, piece_rows, qkv_others, qkv_x, qkv_y, plane(qkv_low, 2), plane(qkv_high, 1)
+        )
+        out_full = whole_weight(
+            out_weight, (2 * core, none), 1, piece_rows // 2, out_others, out_x, out_y, plane(out_low, 2), plane(out_high, 1)
+        )
+        fc1_full = whole_weight(
+            fc1_weight, (none, core), 2, piece_rows, fc1_others, fc1_x, fc1_y, plane(fc1_low, 2), plane(fc1_high, 1)
+        )
+        fc2_full = whole_weight(
+            fc2_weight,
+            (2 * core, none),
+            1,
+            fc2_weight.shape[0] // 2,
+            fc2_others,
+            fc2_x,
+            fc2_y,
+            plane(fc2_low, 2),
+            plane(fc2_high, 1),
+        )
+        grads_mine = tokens_in(after(grad_out, fc1_others))
+    else:
+        qkv_full, out_full, fc1_full, fc2_full = [
+            whole_weight_any(piece) for piece in (qkv_piece, out_piece, fc1_piece, fc2_piece)
+        ]
+        grads_mine = tokens_in(grad_out)
+    grads_mine = lax.optimization_barrier(grads_mine)
 
     half_width = width // CORES
     projected = dot(normed_one, qkv_full) + jnp.concatenate([bias_query, jnp.zeros_like(bias_query), bias_value])
@@ -466,6 +506,9 @@
         context = jnp.einsum("hqk,khd->qhd", soft_full.astype(BF), v_four, preferred_element_type=F32)
         context = context.reshape(CORES * rows, half_width).astype(BF)
 
+    if square:
+        context = after(context, (fc1_low, fc1_high))
+
     def own_sum(left_side, product):
         away = swap(product(left_side[rows:]).astype(BF))
         return product(left_side[:rows]) + away.astype(F32)
@@ -478,16 +521,47 @@
     density = jnp.exp(-0.5 * pre_act * pre_act) * (1.0 / math.sqrt(2.0 * math.pi))
     activated = (pre_act * below).astype(BF)
     slope = (below + pre_act * density).astype(BF)
-    result_own = middle + (own_sum(activated, lambda v: dot(v, fc2_full)) + bias_down)
-    result = tokens_out(result_own.astype(BF))
 
     grad_rows = grads_mine.astype(F32)
     grad_both = jnp.concatenate([grads_mine, swap(grads_mine)])
     down_bias_grad = jnp.sum(grad_rows, axis=0)
+
+    class Reduction:
+        def __init__(self, left_side, right_side):
+            self.sides = (left_side, right_side)
+            far_low = grad_block(left_side, right_side, 3, 0)
+            far_high = grad_block(left_side, right_side, 3, 1)
+            self.far = (plane(far_low, 2), plane(far_high, 1))
+            right_side = after(right_side, (far_low, far_high))
+            self.x_high = plane(grad_block(left_side, right_side, 1, 1), 1)
+            self.y_low = plane(grad_block(left_side, right_side, 2, 0), 2)
+            self.near = [grad_block(left_side, right_side, 1, 0), grad_block(left_side, right_side, 2, 1)]
+
+        def second(self, barrier=None):
+            far = self.far if barrier is None else tuple(after(value, barrier) for value in self.far)
+            self.sent = [self.near[0] + far[0], self.near[1] + far[1]]
+            self.x_low = plane(self.sent[0], 1)
+            self.y_high = plane(self.sent[1], 2)
+
+        def third(self, barrier=None):
+            x_low, y_high = self.x_low, self.y_high
+            if barrier is not None:
+                x_low, y_high = after(x_low, barrier), after(y_high, barrier)
+            low_part = grad_block(*self.sides, 0, 0).astype(F32) + x_low.astype(F32) + self.y_low.astype(F32)
+            high_part = grad_block(*self.sides, 0, 1).astype(F32) + self.x_high.astype(F32) + y_high.astype(F32)
+            self.mine = jnp.concatenate([low_part.astype(BF), high_part.astype(BF)])
+            return sum_shards(self.mine)
+
+    if square:
+        fc2_red = Reduction(activated, after(grad_both, (fc2_low, fc2_high)))
     d_pre = (times_rows(grad_both, fc2_full) * slope.astype(F32)).astype(BF)
-    fc2_part = reduce_grad(activated, grad_both)
     up_bias_grad = jnp.sum(d_pre, axis=0, dtype=F32)
-    fc1_part = reduce_grad(normed_two, d_pre)
+    if square:
+        fc1_red = Reduction(normed_two, d_pre)
+        fc2_red.second()
+        activated = after(activated, fc1_red.near)
+    result_own = middle + (own_sum(activated, lambda v: dot(v, fc2_full)) + bias_down)
+    result = tokens_out(result_own.astype(BF))
     d_normed_two = own_sum(d_pre, lambda v: times_rows(v, fc1_full))
     back_two = jax.vjp(normalize, middle, gain_two, shift_two)[1]
     d_middle, gain_two_grad, shift_two_grad = back_two(d_normed_two)
@@ -495,8 +569,12 @@
     d_attn_own = d_middle.astype(BF)
     out_bias_grad = jnp.sum(d_attn_own, axis=0, dtype=F32)
     d_attn = jnp.concatenate([d_attn_own, swap(d_attn_own)])
+    if square:
+        fc1_red.second(fc2_red.sent)
+        out_red = Reduction(context, d_attn)
     d_context = times_rows(d_attn, out_full).astype(BF)
-    out_part = reduce_grad(context, d_attn)
+    if square:
+        d_context = after(d_context, fc1_red.sent)
     if parts == 1:
         d_queries, d_keys, d_values = attend_backward(projected, d_context, scalars)
     else:
@@ -509,19 +587,21 @@
             d_both = d_both + to_part(d_held[hop].astype(BF), parts - hop).astype(F32)
         d_both = d_both.astype(BF)
         d_keys, d_values = d_both[:, :half_width], d_both[:, half_width:]
-    query_bias_grad = jnp.sum(d_queries, axis=0, dtype=F32)
-    value_bias_grad = jnp.sum(d_values, axis=0, dtype=F32)
     d_projected = jnp.concatenate([d_queries, d_keys, d_values], axis=1)
-    qkv_part = reduce_grad(normed_one, d_projected)
+    if square:
+        fc2_part = fc2_red.third()
+        d_projected = after(d_projected, (fc2_red.mine, result))
+        qkv_red = Reduction(normed_one, d_projected)
+        out_red.second()
+        fc1_part = fc1_red.third(qkv_red.near)
+        qkv_red.second((fc1_red.mine, out_red.sent))
+        d_projected = after(d_projected, qkv_red.sent)
+    query_bias_grad = jnp.sum(d_projected[:, :half_width], axis=0, dtype=F32)
+    value_bias_grad = jnp.sum(d_projected[:, width:], axis=0, dtype=F32)
     d_normed_one = own_sum(d_projected, lambda v: times_rows(v, qkv_full))
     back_one = jax.vjp(normalize, hidden_f, gain_one, shift_one)[1]
     d_inputs, gain_one_grad, shift_one_grad = back_one(d_normed_one)
-    grad_in = tokens_out((d_middle + d_inputs).astype(BF))
-
-    fc2_weight_grad = spread_grad(fc2_part, None)
-    fc1_weight_grad = spread_grad(fc1_part, ff_units // (shards * CORES))
-    out_weight_grad = spread_grad(out_part, None)
-    qkv_weight_grad = spread_grad(qkv_part, width // (shards * CORES))
+    grad_in_own = (d_middle + d_inputs).astype(BF)
 
     def half_slot(value):
         value = value.reshape(shards, 1, -1)
@@ -545,7 +625,44 @@
         ],
         axis=1,
     )
-    summed = lax.dynamic_index_in_dim(lax.psum(packed, ALL), shard, 0, False)
+    grad_in = tokens_out(grad_in_own)
+
+    def sum_plane(values, bits):
+        for bit in bits:
+            values = values + plane(values, 1 << bit)
+        return values
+
+    def sum_line(values):
+        total = lax.dynamic_index_in_dim(values, shard, 0, False)
+        for hop in range(1, shards):
+            total = total + along(lax.dynamic_index_in_dim(values, (shard + hop) % shards, 0, False), hop)
+        return total
+
+    packed = packed + swap(packed)
+    if square:
+        out_part = out_red.third((qkv_red.sent, qkv_red.x_high, qkv_red.y_low))
+        fc2_first = spread_first(after(fc2_part, (qkv_red.sent, out_red.mine)))
+        qkv_part = qkv_red.third(grad_in_own)
+        packed = sum_plane(packed, [0])
+        fc1_first = spread_first(after(fc1_part, (fc2_first[1:], qkv_red.mine, packed, grad_in)))
+        fc2_pair = spread_second(*fc2_first)
+        packed = sum_plane(packed, [1])
+        out_first = spread_first(after(out_part, (fc1_first[1:], fc2_pair[0], packed)))
+        summed = sum_line(after(packed, grad_in))
+        fc1_pair = spread_second(*fc1_first)
+        fc2_weight_grad = spread_last(*fc2_pair, None)
+        fc1_weight_grad = spread_last(*fc1_pair, fc1_chunk)
+        out_pair = spread_second(*out_first)
+        qkv_first = spread_first(after(qkv_part, (out_pair[0], fc1_pair[0], fc2_weight_grad, summed)))
+        out_weight_grad = spread_last(*out_pair, None)
+        qkv_own, qkv_other = spread_second(*after(qkv_first, (fc1_weight_grad, out_pair[1])))
+        qkv_weight_grad = spread_last(qkv_own, after(qkv_other, out_weight_grad), qkv_chunk)
+    else:
+        summed = sum_line(sum_plane(packed, range(chips.bit_length() - 1)))
+        fc2_weight_grad = spread_any(sum_any(activated, grad_both), None)
+        fc1_weight_grad = spread_any(sum_any(normed_two, d_pre), fc1_chunk)
+        out_weight_grad = spread_any(sum_any(context, d_attn), None)
+        qkv_weight_grad = spread_any(sum_any(normed_one, d_projected), qkv_chunk)
     sums = [summed[edges[i] : edges[i + 1]] for i in range(len(vectors))]
     return (
         result,

time: 1850 us -> 1370 us (0.74)
  waiting for transfers between devices: 746 us -> 555 us
  local copies, waits for them, and re-layouts: 190 us -> 79.7 us
  blocking collectives: 109 us -> 0 us
  starting transfers between devices: 203 us -> 137 us
  Pallas kernels: 214 us -> 193 us
    ppermute x24 -> x6, waiting for transfers between devices: 250 us -> 83.6 us  [along(): lax.ppermute(value, 'sh', [(i, (i + hop) % shards) for i in range(shards)])]
    psum x1 -> x0, waiting for transfers between devices: 120 us -> none  [local(): summed = lax.dynamic_index_in_dim(lax.psum(packed, ALL), shard, 0, False)]
    all_gather x1 -> x0, blocking collectives: 109 us -> none  [local(): gathered = lax.all_gather(jnp.concatenate(vectors), 'sh').astype(F32)]
    ppermute x4, waiting for transfers between devices: 21.9 us -> 115 us  [tokens_out(): lax.ppermute(lax.dynamic_index_in_dim(value, (turn + micro) % 2, 0, False...]
    ppermute x48 -> x58, waiting for transfers between devices: 355 us -> 276 us  [plane(): return lax.ppermute(value, 'ch', [(i, i ^ bit) for i in range(chips)])]
    all_gather x0 -> x4, waiting for transfers between devices: none -> 60.1 us  [gather_shards(): held = lax.all_gather(piece, 'sh')]
    ppermute x24 -> x6, starting transfers between devices: 38.4 us -> 2.92 us  [along(): lax.ppermute(value, 'sh', [(i, (i + hop) % shards) for i in range(shards)])]
    dynamic_slice x4 -> x2, local copies, waits for them, and re-layouts: 33.5 us -> 0.03 us  [take(): return lax.dynamic_index_in_dim(value, core, axis, False)]
  transfers between devices with their start and end apart: 94 -> 94, of which waited for: 34 -> 31; matrix products, arithmetic and copies ran while one was open for 26% -> 32% of each run, Pallas kernels for 10% -> 13%
where the time goes in v2:
time: 1370 us; the launch traced here: 1350 us
  waiting for transfers between devices  555 us (41%)
  matrix products  280 us (20%)
  Pallas kernels  193 us (14%)
  starting transfers between devices  137 us (10%)
  other arithmetic  92.3 us (7%)
  local copies, waits for them, and re-layouts  79.7 us (6%)
  between operations  16.4 us (1%)
    ppermute x58, waiting for transfers between devices, plane(): return lax.ppermute(value, 'ch', [(i, i ^ bit) for i in range(chips)])  276 us
    pallas_call x8, Pallas kernels, place(): pl.pallas_call(body, grid_spec=pltpu.PrefetchScalarGridSpec(num_scalar_pr...  138 us
    ppermute x4, waiting for transfers between devices, tokens_out(): lax.ppermute(lax.dynamic_index_in_dim(value, (turn + micro) % 2, 0, False...  115 us
    dot_general x32, matrix products, cross_rows(): lax.dot_general(left_side, right_side, (((0,), (0,)), ((), ())), preferre...  108 us
    dot_general x6, matrix products, times_rows(): lax.dot_general(left_side, right_side, (((1,), (1,)), ((), ())), preferre...  92.3 us
    ppermute x6, waiting for transfers between devices, along(): lax.ppermute(value, 'sh', [(i, (i + hop) % shards) for i in range(shards)])  83.6 us
    dot_general x6, matrix products, dot(): return jnp.dot(left_side, right_side, preferred_element_type=F32)  79.2 us
    ppermute x58, starting transfers between devices, plane(): return lax.ppermute(value, 'ch', [(i, i ^ bit) for i in range(chips)])  61.5 us
  transfers between devices with their start and end apart: 94, of which 31 were waited for; matrix products, arithmetic and copies ran while one was open for 32% of the time, Pallas kernels for 13%

profile of v2, /device:TPU:0, one launch (start us, length us, event | category | flops | bytes accessed | tf_op | source)
XLA Modules:
  0.0 1353.2 jit_solution(16784129613404754189)
XLA Ops:
  26.9 60.0 %all-gather.9.cloned.1.call-done = bf16[2048,768]{1,0:T(8,128)(2,1)} async-done(((bf16[512,768]{1,0:T(8,128)(2,1)}), bf16[2048,768]{1,0:T(8,128)(2,1)}) %all-gather.9.cloned.1.call-update) | async-done | bytes 3145744 | tf_op jit(solution)/shard_map/all_gather | solution.py:292
  100.3 35.3 %collective-permute-done.3 = bf16[6144]{0:T(1024)(128)(2,1)S(1)} collective-permute-done((bf16[6144]{0:T(1024)(128)(2,1)S(1)}, bf16[6144]{0:T(1024)(128)(2,1)S(1)}, u32[]{:S(2)}, u32[]{:S(2)}) %collective-permute-start.3) | collective-permute-done | bytes 12320 | tf_op jit(solution)/shard_map/ppermute | solution.py:251
  135.7 12.9 collective-permute-start.2
  148.6 44.1 %collective-permute-done.4 = bf16[6144]{0:T(1024)(128)(2,1)S(1)} collective-permute-done((bf16[6144]{0:T(1024)(128)(2,1)S(1)}, bf16[6144]{0:T(1024)(128)(2,1)S(1)}, u32[]{:S(2)}, u32[]{:S(2)}) %collective-permute-start.4) | collective-permute-done | bytes 12320 | tf_op jit(solution)/shard_map/ppermute | solution.py:251
  202.6 40.7 %collective-permute-done.7.refs_2_ = bf16[1536,768]{1,0:T(8,128)(2,1)} collective-permute-done((bf16[1536,768]{1,0:T(8,128)(2,1)}, bf16[1536,768]{1,0:T(8,128)(2,1)}, u32[]{:S(2)}, u32[]{:S(2)}) %collective-permute-start.7) | collective-permute-done | bytes 2359328 | tf_op jit(solution)/shard_map/ppermute | solution.py:254
  275.4 16.2 %collective-permute-done.9.refs_4_ = bf16[768,768]{1,0:T(8,128)(2,1)} collective-permute-done((bf16[768,768]{1,0:T(8,128)(2,1)}, bf16[768,768]{1,0:T(8,128)(2,1)}, u32[]{:S(2)}, u32[]{:S(2)}) %collective-permute-start.9) | collective-permute-done | bytes 1179680 | tf_op jit(solution)/shard_map/ppermute | solution.py:254
  293.5 22.5 %shard_map.631 = bf16[2048,3072]{1,0:T(8,128)(2,1)} custom-call(s32[14,32]{1,0:T(8,128)} %get-tuple-element.166.table_ref, bf16[512,3072]{1,0:T(8,128)(2,1)} %copy-done.27, bf16[1536,768]{1,0:T(8,128)(2,1)} %pad_maximum_fusion.11.refs_1_, bf16[1536,768]{1,0:T(8,128)(2,1)} %collective-permute-done.7.refs_2_, ...), custom_call_target="tpu_custom_call" | custom-call | tf_op jit(solution)/shard_map/pallas_call | solution.py:77
  315.9 18.4 %add_convert_fusion.q_ref.k_ref.v_ref = bf16[1024,3072]{1,0:T(8,128)(2,1)} fusion(bf16[1024,2048]{1,0:T(8,128)(2,1)} %pad_maximum_fusion.4, bf16[2048,3072]{1,0:T(8,128)(2,1)} %shard_map.631, f32[3072]{0:T(1024)S(1)} %pad_maximum_fusion.19), kind=kOutput, calls=%fused_computation.10 | convolution fusion | flops 12891193344 | bytes 23080960 | tf_op jit(solution)/shard_map/dot_general | solution.py:30
  334.4 20.5 %shard_map.632 = bf16[1024,1024]{1,0:T(8,128)(2,1)} custom-call(s32[2]{0:T(128)} %pad_add_fusion.10.scal_ref, bf16[1024,3072]{1,0:T(8,128)(2,1)} %add_convert_fusion.q_ref.k_ref.v_ref, bf16[1024,3072]{1,0:T(8,128)(2,1)} %add_convert_fusion.q_ref.k_ref.v_ref, bf16[1024,3072]{1,0:T(8,128)(2,1)} %add_convert_fusion.q_ref.k_ref.v_ref), custom_call_target="tpu_custom_call" | custom-call | tf_op jit(solution)/shard_map/pallas_call | solution.py:172
  355.6 19.1 %shard_map.633 = bf16[1024,2048]{1,0:T(8,128)(2,1)} custom-call(s32[14,32]{1,0:T(8,128)} %get-tuple-element.165.table_ref, bf16[512,2048]{1,0:T(8,128)(2,1)} %refs_0_.3, bf16[768,512]{1,0:T(8,128)(2,1)} %copy-done.28, bf16[768,512]{1,0:T(8,128)(2,1)} %collective-permute-done.13.refs_2_, bf16[768,512]{1,0:T(8,128)(2,1)} %collective-permute-done.14.refs_3_, ...), custom_call_target="tpu_custom_call" | custom-call | tf_op jit(solution)/shard_map/pallas_call | solution.py:77
  387.3 12.3 collective-permute-start.22
  404.0 19.0 %collective-permute-done.22 = bf16[256,2048]{1,0:T(8,128)(2,1)} collective-permute-done((bf16[256,2048]{1,0:T(8,128)(2,1)}, bf16[256,2048]{1,0:T(8,128)(2,1)}, u32[]{:S(2)}, u32[]{:S(2)}) %collective-permute-start.22) | collective-permute-done | bytes 1048608 | tf_op jit(solution)/shard_map/ppermute | solution.py:272
  424.6 21.0 %collective-permute-start.23 = (bf16[512,2048]{1,0:T(8,128)(2,1)S(1)}, bf16[512,2048]{1,0:T(8,128)(2,1)S(1)}, u32[]{:S(2)}, u32[]{:S(2)}) collective-permute-start(bf16[512,2048]{1,0:T(8,128)(2,1)S(1)} %pad_maximum_fusion.13), channel_id=1, source_target_pairs={{0,4},{4,0},{1,5},{5,1},{2,6},{6,2},{3,7},{7,3},{8,12},{12,8},{9,1... | collective-permute-start | bytes 6291464 | tf_op jit(solution)/shard_map/ppermute | solution.py:257
  463.2 86.6 %collective-permute-done.19.refs_4_ = bf16[768,1024]{1,0:T(8,128)(2,1)} collective-permute-done((bf16[768,1024]{1,0:T(8,128)(2,1)}, bf16[768,1024]{1,0:T(8,128)(2,1)}, u32[]{:S(2)}, u32[]{:S(2)}) %collective-permute-start.19) | collective-permute-done | bytes 1572896 | tf_op jit(solution)/shard_map/ppermute | solution.py:254
  549.8 24.7 %shard_map.634 = bf16[2048,4096]{1,0:T(8,128)(2,1)} custom-call(s32[14,32]{1,0:T(8,128)} %get-tuple-element.164.table_ref, bf16[512,8192]{1,0:T(8,128)(2,1)} %refs_0_.4, bf16[1536,1024]{1,0:T(8,128)(2,1)} %pad_maximum_fusion.8.refs_1_, bf16[1536,1024]{1,0:T(8,128)(2,1)} %collective-permute-done.11.refs_2_, ...), custom_call_target="tpu_custom_call" | custom-call | tf_op jit(solution)/shard_map/pallas_call | solution.py:77
  583.2 27.9 %multiply_convert_fusion.1 = (bf16[1024,4096]{1,0:T(8,128)(2,1)}, f32[1024,4096]{1,0:T(8,128)}) fusion(f32[4096]{0:T(1024)S(1)} %bitcast.184, bf16[2048,4096]{1,0:T(8,128)(2,1)} %shard_map.634, bf16[512,2048]{1,0:T(8,128)(2,1)} %collective-permute-done.18, bf16[512,2048]{1,0:T(8,128)(2,1)} %add_convert_fusion.7), kind=kOutput, calls=%fused_computation.8 | convolution fusion | flops 17213423616 | bytes 46153728 | tf_op jit(solution)/shard_map/dot_general | solution.py:30
  644.4 24.7 %shard_map.635 = bf16[4096,2048]{1,0:T(8,128)(2,1)} custom-call(s32[14,32]{1,0:T(8,128)} %get-tuple-element.165.table_ref, bf16[2048,2048]{1,0:T(8,128)(2,1)} %refs_0_.5, bf16[3072,512]{1,0:T(8,128)(2,1)} %pad_maximum_fusion.9.refs_1_, bf16[3072,512]{1,0:T(8,128)(2,1)} %collective-permute-done.24.refs_2_, bf16[3072,512]{1,0:T(8,128)(2,1)} %collective-permute-done.25.refs_3_, ...), custom_call_target="tpu_custom_call" | custom-call | tf_op jit(solution)/shard_map/pallas_call | solution.py:77
  669.1 29.6 %convert_reduce_fusion = (f32[4096]{0:T(1024)}, bf16[1024,4096]{1,0:T(8,128)(2,1)}) fusion(f32[1024,4096]{1,0:T(8,128)} %get-tuple-element.175, f32[4096]{0:T(1024)S(1)} %bitcast.185, bf16[4096,2048]{1,0:T(8,128)(2,1)} %shard_map.635, bf16[512,2048]{1,0:T(8,128)(2,1)} %copy-done.33, bf16[512,2048]{1,0:T(8,128)(2,1)S(1)} %copy-done.8), kind=kOutput, calls=%fused_computation.6 | convolution fusion | flops 17251168256 | bytes 46170112 | tf_op jit(solution)/shard_map/dot_general | solution.py:38
  726.6 14.8 %fusion.39 = bf16[512,2048]{1,0:T(8,128)(2,1)} fusion(bf16[2048,4096]{1,0:T(8,128)(2,1)} %shard_map.634, bf16[1024,4096]{1,0:T(8,128)(2,1)} %get-tuple-element.62), kind=kOutput, calls=%fused_computation.88 | convolution fusion | flops 8590983168 | bytes 23068672 | tf_op jit(solution)/shard_map/dot_general | solution.py:38
  757.9 13.8 %add_convert_fusion.6 = bf16[512,2048]{1,0:T(8,128)(2,1)S(1)} fusion(f32[512,2048]{1,0:T(8,128)S(1)} %copy-done.3, bf16[512,2048]{1,0:T(8,128)(2,1)S(1)} %collective-permute-done.28, bf16[4096,2048]{1,0:T(8,128)(2,1)} %shard_map.635, bf16[1024,4096]{1,0:T(8,128)(2,1)} %get-tuple-element.63, f32[2048]{0:T(1024)S(1)} %bitcast.188), kind=kOutput, calls=%fused_computation.61 | convolution fusion | flops 8595177472 | bytes 29368320 | tf_op jit(solution)/shard_map/dot_general | solution.py:30
  774.3 27.2 %collective-permute-done.40 = bf16[2048,512]{1,0:T(8,128)(2,1)S(1)} collective-permute-done((bf16[2048,512]{1,0:T(8,128)(2,1)S(1)}, bf16[2048,512]{1,0:T(8,128)(2,1)S(1)}, u32[]{:S(2)}, u32[]{:S(2)}) %collective-permute-start.40) | collective-permute-done | bytes 2097184 | tf_op jit(solution)/shard_map/ppermute | solution.py:254
  819.7 18.0 %multiply_reduce_fusion = (f32[2048]{0:T(1024)S(1)}, f32[512]{0:T(512)S(1)}, f32[2048]{0:T(1024)S(1)}, f32[512,2048]{1,0:T(8,128)}) fusion(f32[512,2048]{1,0:T(8,128)} %copy-done.2, f32[512]{0:T(512)S(1)} %copy-done.66, f32[512]{0:T(512)S(1)} %copy-done.61, f32[2048]{0:T(1024)S(1)} %bitcast.175, bf16[512,2048]{1,0:T(8,128)(2,1)} %collective-permute-done.31, ...), kind=kOutput, calls=%fused_computation.49 | convolution fusion | flops 8600416256 | bytes 31488000 | tf_op jit(solution)/shard_map/dot_general | solution.py:38
  870.7 55.5 %collective-permute-done.30 = bf16[256,2048]{1,0:T(8,128)(2,1)} collective-permute-done((bf16[256,2048]{1,0:T(8,128)(2,1)S(1)}, bf16[256,2048]{1,0:T(8,128)(2,1)}, u32[]{:S(2)}, u32[]{:S(2)}) %collective-permute-start.30) | collective-permute-done | bytes 1048608 | tf_op jit(solution)/shard_map/ppermute | solution.py:281
  937.2 34.4 %shard_map.636 = (bf16[1024,1024]{1,0:T(8,128)(2,1)}, bf16[1024,1024]{1,0:T(8,128)(2,1)}, bf16[1024,1024]{1,0:T(8,128)(2,1)}) custom-call(s32[2]{0:T(128)} %pad_add_fusion.10.scal_ref, bf16[1024,3072]{1,0:T(8,128)(2,1)} %add_convert_fusion.q_ref.k_ref.v_ref, bf16[1024,3072]{1,0:T(8,128)(2,1)} %add_convert_fusion.q_ref.k_ref.v_ref, ...), custom_call_target="tpu_custom_call" | custom-call | tf_op jit(solution)/shard_map/pallas_call | solution.py:188
  1066.0 17.7 %collective-permute-done.62 = bf16[512,512]{1,0:T(8,128)(2,1)} collective-permute-done((bf16[512,512]{1,0:T(8,128)(2,1)}, bf16[512,512]{1,0:T(8,128)(2,1)}, u32[]{:S(2)}, u32[]{:S(2)}) %collective-permute-start.62) | collective-permute-done | bytes 524320 | tf_op jit(solution)/shard_map/ppermute | solution.py:254
  1089.8 12.9 fusion.168
  1133.1 20.1 %collective-permute-done.53 = f32[4,6144]{1,0:T(4,128)S(1)} collective-permute-done((f32[4,6144]{1,0:T(4,128)S(1)}, f32[4,6144]{1,0:T(4,128)S(1)}, u32[]{:S(2)}, u32[]{:S(2)}) %collective-permute-start.53) | collective-permute-done | bytes 98336 | tf_op jit(solution)/shard_map/ppermute | solution.py:254
  1153.2 59.2 %collective-permute-done.51 = bf16[256,2048]{1,0:T(8,128)(2,1)} collective-permute-done((bf16[256,2048]{1,0:T(8,128)(2,1)}, bf16[256,2048]{1,0:T(8,128)(2,1)}, u32[]{:S(2)}, u32[]{:S(2)}) %collective-permute-start.51) | collective-permute-done | bytes 1048608 | tf_op jit(solution)/shard_map/ppermute | solution.py:281
  1223.1 13.8 %collective-permute-done.70 = bf16[512,512]{1,0:T(8,128)(2,1)S(1)} collective-permute-done((bf16[512,512]{1,0:T(8,128)(2,1)S(1)}, bf16[512,512]{1,0:T(8,128)(2,1)S(1)}, u32[]{:S(2)}, u32[]{:S(2)}) %collective-permute-start.70) | collective-permute-done | bytes 524320 | tf_op jit(solution)/shard_map/ppermute | solution.py:254
  1280.4 11.7 shard_map.637
  1294.5 11.7 shard_map.638
  1329.5 16.6 %shard_map.640 = f32[512,6144]{1,0:T(8,128)} custom-call(s32[6,24]{1,0:T(8,128)} %pad_add_fusion.8.table_ref, bf16[2048,768]{1,0:T(8,128)(2,1)} %copy-done.19, bf16[2048,768]{1,0:T(8,128)(2,1)} %collective-permute-done.85.refs_1_), custom_call_target="tpu_custom_call" | custom-call | tf_op jit(solution)/shard_map/pallas_call | solution.py:77
  (626 shorter events, 474.1 us)
Async XLA Ops:
  20.6 180.8 %all-gather.13.cloned.1.call-start = ((), (), s32[]{:S(2)}) async-start(), calls=%async_computation.10 | async-start | bytes 1310720 | tf_op jit(solution)/shard_map/all_gather | solution.py:292
  22.5 233.2 %all-gather.11.cloned.1.call-start = ((), (), s32[]{:S(2)}) async-start(), calls=%async_computation.9 | async-start | bytes 5242880 | tf_op jit(solution)/shard_map/all_gather | solution.py:292
  24.9 374.8 %all-gather.15.cloned.1.call-start = ((), (), s32[]{:S(2)}) async-start(), calls=%async_computation.11 | async-start | bytes 5242880 | tf_op jit(solution)/shard_map/all_gather | solution.py:292
  91.6 104.6 %collective-permute-start = (bf16[256,2048]{1,0:T(8,128)(2,1)}, bf16[256,2048]{1,0:T(8,128)(2,1)S(1)}, u32[]{:S(2)}, u32[]{:S(2)}) collective-permute-start(bf16[256,2048]{1,0:T(8,128)(2,1)} %get-tuple-element.137), channel_id=1, source_target_pairs={{0,0},{1,2},{2,4},{3,6},{4,1},{5,3},{6,5},{7,7},{8,8},{9,10},{10,1... | collective-permute-start | bytes 3145736 | tf_op jit(solution)/shard_map/ppermute | solution.py:272
  93.5 102.8 %collective-permute-start.1 = (bf16[256,2048]{1,0:T(8,128)(2,1)S(1)}, bf16[256,2048]{1,0:T(8,128)(2,1)S(1)}, u32[]{:S(2)}, u32[]{:S(2)}) collective-permute-start(bf16[256,2048]{1,0:T(8,128)(2,1)S(1)} %get-tuple-element.138), channel_id=1, source_target_pairs={{0,2},{1,0},{2,6},{3,4},{4,3},{5,1},{6,7},{7,5},{8,10},{9,8},{10,1... | collective-permute-start | bytes 3145736 | tf_op jit(solution)/shard_map/ppermute | solution.py:272
  98.1 1030.9 %reduce-scatter.11.cloned.1.call-start = ((), (), s32[]{:S(2)}) async-start(), calls=%async_computation.7 | async-start | bytes 5242880 | tf_op jit(solution)/shard_map/reduce_scatter | solution.py:344
  99.2 93.5 %collective-permute-start.4 = (bf16[6144]{0:T(1024)(128)(2,1)S(1)}, bf16[6144]{0:T(1024)(128)(2,1)S(1)}, u32[]{:S(2)}, u32[]{:S(2)}) collective-permute-start(bf16[6144]{0:T(1024)(128)(2,1)S(1)} %constant_dynamic-update-slice_fusion.29), channel_id=1, source_target_pairs={{0,2},{1,3},{2,0},{3,1},{4,6},{5,7},{6,4},{7,5},{8,10},{9,11},{10,... | collective-permute-start | bytes 36872 | tf_op jit(solution)/shard_map/ppermute | solution.py:251
  99.5 94.7 %collective-permute-start.5 = (bf16[6144]{0:T(1024)(128)(2,1)S(1)}, bf16[6144]{0:T(1024)(128)(2,1)S(1)}, u32[]{:S(2)}, u32[]{:S(2)}) collective-permute-start(bf16[6144]{0:T(1024)(128)(2,1)S(1)} %constant_dynamic-update-slice_fusion.29), channel_id=1, source_target_pairs={{0,1},{1,2},{2,3},{3,0},{4,5},{5,6},{6,7},{7,4},{8,9},{9,10},{10,1... | collective-permute-start | bytes 36872 | tf_op jit(solution)/shard_map/ppermute | solution.py:251
  266.1 108.6 %collective-permute-start.11 = (bf16[1536,1024]{1,0:T(8,128)(2,1)}, bf16[1536,1024]{1,0:T(8,128)(2,1)}, u32[]{:S(2)}, u32[]{:S(2)}) collective-permute-start(bf16[1536,1024]{1,0:T(8,128)(2,1)} %pad_maximum_fusion.8.refs_1_), channel_id=1, source_target_pairs={{0,8},{8,0},{16,24},{24,16},{1,9},{9,1},{17,25},{25,17},{2,10},{10... | collective-permute-start | bytes 9437192 | tf_op jit(solution)/shard_map/ppermute | solution.py:254
  267.3 110.3 %collective-permute-start.12 = (bf16[1536,1024]{1,0:T(8,128)(2,1)}, bf16[1536,1024]{1,0:T(8,128)(2,1)}, u32[]{:S(2)}, u32[]{:S(2)}) collective-permute-start(bf16[1536,1024]{1,0:T(8,128)(2,1)} %pad_maximum_fusion.8.refs_1_), channel_id=1, source_target_pairs={{0,16},{8,24},{16,0},{24,8},{1,17},{9,25},{17,1},{25,9},{2,18},{10... | collective-permute-start | bytes 9437192 | tf_op jit(solution)/shard_map/ppermute | solution.py:254
  269.9 85.0 %collective-permute-start.15 = (bf16[384,512]{1,0:T(8,128)(2,1)S(1)}, bf16[384,512]{1,0:T(8,128)(2,1)S(1)}, u32[]{:S(2)}, u32[]{:S(2)}) collective-permute-start(bf16[384,512]{1,0:T(8,128)(2,1)S(1)} %bitcast.166), channel_id=1, source_target_pairs={{0,16},{8,24},{16,0},{24,8},{1,17},{9,25},{17,1},{25,9},{2,18},{10... | collective-permute-start | bytes 1179656 | tf_op jit(solution)/shard_map/ppermute | solution.py:254
  445.6 128.9 %collective-permute-start.24 = (bf16[3072,512]{1,0:T(8,128)(2,1)}, bf16[3072,512]{1,0:T(8,128)(2,1)}, u32[]{:S(2)}, u32[]{:S(2)}) collective-permute-start(bf16[3072,512]{1,0:T(8,128)(2,1)} %pad_maximum_fusion.9.refs_1_), channel_id=1, source_target_pairs={{0,8},{8,0},{16,24},{24,16},{1,9},{9,1},{17,25},{25,17},{2,10},{10... | collective-permute-start | bytes 9437192 | tf_op jit(solution)/shard_map/ppermute | solution.py:254
  445.6 133.2 %collective-permute-start.25 = (bf16[3072,512]{1,0:T(8,128)(2,1)}, bf16[3072,512]{1,0:T(8,128)(2,1)}, u32[]{:S(2)}, u32[]{:S(2)}) collective-permute-start(bf16[3072,512]{1,0:T(8,128)(2,1)} %pad_maximum_fusion.9.refs_1_), channel_id=1, source_target_pairs={{0,16},{8,24},{16,0},{24,8},{1,17},{9,25},{17,1},{25,9},{2,18},{10... | collective-permute-start | bytes 9437192 | tf_op jit(solution)/shard_map/ppermute | solution.py:254
  454.5 128.7 %collective-permute-start.18 = (bf16[512,2048]{1,0:T(8,128)(2,1)}, bf16[512,2048]{1,0:T(8,128)(2,1)}, u32[]{:S(2)}, u32[]{:S(2)}) collective-permute-start(bf16[512,2048]{1,0:T(8,128)(2,1)} %add_convert_fusion.7), channel_id=1, source_target_pairs={{0,4},{4,0},{1,5},{5,1},{2,6},{6,2},{3,7},{7,3},{8,12},{12,8},{9,1... | collective-permute-start | bytes 6291464 | tf_op jit(solution)/shard_map/ppermute | solution.py:257
  454.5 95.3 %collective-permute-start.19 = (bf16[768,1024]{1,0:T(8,128)(2,1)}, bf16[768,1024]{1,0:T(8,128)(2,1)}, u32[]{:S(2)}, u32[]{:S(2)}) collective-permute-start(bf16[768,1024]{1,0:T(8,128)(2,1)} %bitcast.24), channel_id=1, source_target_pairs={{0,16},{8,24},{16,0},{24,8},{1,17},{9,25},{17,1},{25,9},{2,18},{10... | collective-permute-start | bytes 4718600 | tf_op jit(solution)/shard_map/ppermute | solution.py:254
  456.5 93.3 %collective-permute-start.20 = (bf16[768,1024]{1,0:T(8,128)(2,1)}, bf16[768,1024]{1,0:T(8,128)(2,1)}, u32[]{:S(2)}, u32[]{:S(2)}) collective-permute-start(bf16[768,1024]{1,0:T(8,128)(2,1)} %bitcast.26), channel_id=1, source_target_pairs={{0,8},{8,0},{16,24},{24,16},{1,9},{9,1},{17,25},{25,17},{2,10},{10... | collective-permute-start | bytes 4718600 | tf_op jit(solution)/shard_map/ppermute | solution.py:254
  621.5 131.4 %collective-permute-start.34 = (bf16[2048,512]{1,0:T(8,128)(2,1)}, bf16[2048,512]{1,0:T(8,128)(2,1)}, u32[]{:S(2)}, u32[]{:S(2)}) collective-permute-start(bf16[2048,512]{1,0:T(8,128)(2,1)} %convolution_convert_fusion.7), channel_id=1, source_target_pairs={{0,16},{8,24},{16,0},{24,8},{1,17},{9,25},{17,1},{25,9},{2,18},{10... | collective-permute-start | bytes 6291464 | tf_op jit(solution)/shard_map/ppermute | solution.py:254
  621.8 125.1 %collective-permute-start.35 = (bf16[2048,512]{1,0:T(8,128)(2,1)}, bf16[2048,512]{1,0:T(8,128)(2,1)}, u32[]{:S(2)}, u32[]{:S(2)}) collective-permute-start(bf16[2048,512]{1,0:T(8,128)(2,1)} %convolution_convert_fusion.6), channel_id=1, source_target_pairs={{0,8},{8,0},{16,24},{24,16},{1,9},{9,1},{17,25},{25,17},{2,10},{10... | collective-permute-start | bytes 6291464 | tf_op jit(solution)/shard_map/ppermute | solution.py:254
  629.5 143.3 %collective-permute-start.39 = (bf16[2048,512]{1,0:T(8,128)(2,1)}, bf16[2048,512]{1,0:T(8,128)(2,1)}, u32[]{:S(2)}, u32[]{:S(2)}) collective-permute-start(bf16[2048,512]{1,0:T(8,128)(2,1)} %convolution_convert_fusion), channel_id=1, source_target_pairs={{0,8},{8,0},{16,24},{24,16},{1,9},{9,1},{17,25},{25,17},{2,10},{10... | collective-permute-start | bytes 6291464 | tf_op jit(solution)/shard_map/ppermute | solution.py:254
  642.7 161.6 %collective-permute-start.38 = (bf16[2048,512]{1,0:T(8,128)(2,1)}, bf16[2048,512]{1,0:T(8,128)(2,1)}, u32[]{:S(2)}, u32[]{:S(2)}) collective-permute-start(bf16[2048,512]{1,0:T(8,128)(2,1)} %convolution_convert_fusion.2), channel_id=1, source_target_pairs={{0,16},{8,24},{16,0},{24,8},{1,17},{9,25},{17,1},{25,9},{2,18},{10... | collective-permute-start | bytes 6291464 | tf_op jit(solution)/shard_map/ppermute | solution.py:254
  772.8 86.5 %collective-permute-start.33 = (bf16[1024,1024]{1,0:T(8,128)(2,1)}, bf16[1024,1024]{1,0:T(8,128)(2,1)}, u32[]{:S(2)}, u32[]{:S(2)}) collective-permute-start(bf16[1024,1024]{1,0:T(8,128)(2,1)} %convolution_convert_fusion.15), channel_id=1, source_target_pairs={{0,16},{8,24},{16,0},{24,8},{1,17},{9,25},{17,1},{25,9},{2,18},{10... | collective-permute-start | bytes 6291464 | tf_op jit(solution)/shard_map/ppermute | solution.py:254
  813.8 112.4 %collective-permute-start.30 = (bf16[256,2048]{1,0:T(8,128)(2,1)S(1)}, bf16[256,2048]{1,0:T(8,128)(2,1)}, u32[]{:S(2)}, u32[]{:S(2)}) collective-permute-start(bf16[256,2048]{1,0:T(8,128)(2,1)S(1)} %get-tuple-element.130), channel_id=1, source_target_pairs={{2,0},{0,1},{6,2},{4,3},{3,4},{1,5},{7,6},{5,7},{10,8},{8,9},{14,1... | collective-permute-start | bytes 3145736 | tf_op jit(solution)/shard_map/ppermute | solution.py:281
  819.0 396.6 %reduce-scatter.9.cloned.1.call-start = ((), (), s32[]{:S(2)}) async-start(), calls=%async_computation.6 | async-start | bytes 5242880 | tf_op jit(solution)/shard_map/reduce_scatter | solution.py:344
  844.5 85.5 %collective-permute-start.32 = (bf16[512,2048]{1,0:T(8,128)(2,1)S(1)}, bf16[512,2048]{1,0:T(8,128)(2,1)S(1)}, u32[]{:S(2)}, u32[]{:S(2)}) collective-permute-start(bf16[512,2048]{1,0:T(8,128)(2,1)S(1)} %get-tuple-element.103), channel_id=1, source_target_pairs={{0,4},{4,0},{1,5},{5,1},{2,6},{6,2},{3,7},{7,3},{8,12},{12,8},{9,1... | collective-permute-start | bytes 6291464 | tf_op jit(solution)/shard_map/ppermute | solution.py:257
  859.3 128.8 %collective-permute-start.44 = (bf16[1024,1024]{1,0:T(8,128)(2,1)}, bf16[1024,1024]{1,0:T(8,128)(2,1)}, u32[]{:S(2)}, u32[]{:S(2)}) collective-permute-start(bf16[1024,1024]{1,0:T(8,128)(2,1)} %convolution_convert_fusion.9), channel_id=1, source_target_pairs={{0,8},{8,0},{16,24},{24,16},{1,9},{9,1},{17,25},{25,17},{2,10},{10... | collective-permute-start | bytes 6291464 | tf_op jit(solution)/shard_map/ppermute | solution.py:254
  864.8 127.2 %collective-permute-start.43 = (bf16[1024,1024]{1,0:T(8,128)(2,1)}, bf16[1024,1024]{1,0:T(8,128)(2,1)}, u32[]{:S(2)}, u32[]{:S(2)}) collective-permute-start(bf16[1024,1024]{1,0:T(8,128)(2,1)} %convolution_convert_fusion.10), channel_id=1, source_target_pairs={{0,16},{8,24},{16,0},{24,8},{1,17},{9,25},{17,1},{25,9},{2,18},{10... | collective-permute-start | bytes 6291464 | tf_op jit(solution)/shard_map/ppermute | solution.py:254
  868.7 119.4 %collective-permute-start.45 = (bf16[1024,1024]{1,0:T(8,128)(2,1)}, bf16[1024,1024]{1,0:T(8,128)(2,1)}, u32[]{:S(2)}, u32[]{:S(2)}) collective-permute-start(bf16[1024,1024]{1,0:T(8,128)(2,1)} %add.665), channel_id=1, source_target_pairs={{0,16},{8,24},{16,0},{24,8},{1,17},{9,25},{17,1},{25,9},{2,18},{10... | collective-permute-start | bytes 6291464 | tf_op jit(solution)/shard_map/ppermute | solution.py:254
  998.2 262.1 %reduce-scatter.7.cloned.1.call-start = ((), (), s32[]{:S(2)}) async-start(), calls=%async_computation.5 | async-start | bytes 1310720 | tf_op jit(solution)/shard_map/reduce_scatter | solution.py:344
  1089.7 202.4 %reduce-scatter.5.cloned.1.call-start = ((), (), s32[]{:S(2)}) async-start(), calls=%async_computation.4 | async-start | bytes 3932160 | tf_op jit(solution)/shard_map/reduce_scatter | solution.py:344
  1122.0 90.4 %collective-permute-start.51 = (bf16[256,2048]{1,0:T(8,128)(2,1)}, bf16[256,2048]{1,0:T(8,128)(2,1)}, u32[]{:S(2)}, u32[]{:S(2)}) collective-permute-start(bf16[256,2048]{1,0:T(8,128)(2,1)} %get-tuple-element.126), channel_id=1, source_target_pairs={{2,0},{0,1},{6,2},{4,3},{3,4},{1,5},{7,6},{5,7},{10,8},{8,9},{14,1... | collective-permute-start | bytes 3145736 | tf_op jit(solution)/shard_map/ppermute | solution.py:281
  1129.0 86.6 %collective-permute-start.66 = (bf16[1024,512]{1,0:T(8,128)(2,1)}, bf16[1024,512]{1,0:T(8,128)(2,1)S(1)}, u32[]{:S(2)}, u32[]{:S(2)}) collective-permute-start(bf16[1024,512]{1,0:T(8,128)(2,1)} %reduce-scatter.11.cloned.1.call-done), channel_id=1, source_target_pairs={{0,8},{8,0},{16,24},{24,16},{1,9},{9,1},{17,25},{25,17},{2,10},{10... | collective-permute-start | bytes 3145736 | tf_op jit(solution)/shard_map/ppermute | solution.py:254
  1130.5 85.1 %collective-permute-start.67 = (bf16[1024,512]{1,0:T(8,128)(2,1)}, bf16[1024,512]{1,0:T(8,128)(2,1)S(1)}, u32[]{:S(2)}, u32[]{:S(2)}) collective-permute-start(bf16[1024,512]{1,0:T(8,128)(2,1)} %reduce-scatter.11.cloned.1.call-done), channel_id=1, source_target_pairs={{0,16},{8,24},{16,0},{24,8},{1,17},{9,25},{17,1},{25,9},{2,18},{10... | collective-permute-start | bytes 3145736 | tf_op jit(solution)/shard_map/ppermute | solution.py:254
  (168 other events, 3805.1 us)
Sparse Core Ops, SparseCore 0:
  20.7 66.1 all-gather.8
  89.0 44.1 all-gather.12
  135.4 90.5 all-gather.10
  227.5 81.4 all-gather.14
  819.1 97.3 reduce-scatter.10
  998.4 73.9 reduce-scatter.8
  1089.8 25.9 reduce-scatter.6
  1129.0 76.7 reduce-scatter.4

commit v3 on v2

--- a/solution.py
+++ b/solution.py
@@ -417,10 +417,8 @@
     edges = np.cumsum([0] + lengths)
     square = chips == 4
     small = jnp.concatenate(vectors)
-    if square:
-        qkv_others = jnp.concatenate(gather_shards(qkv_piece))
-        small = after(small, qkv_others)
     ring = [small] + [along(small, hop) for hop in range(shards - 1, 0, -1)]
+    qkv_piece, *ring = lax.optimization_barrier((qkv_piece, *ring))
     gathered = lax.dynamic_slice_in_dim(jnp.stack(ring + ring), (shards - shard) % shards, shards, 0)
     vec = [gathered[:, edges[i] : edges[i + 1]].astype(F32) for i in range(len(vectors))]
     gain_one, shift_one, _, _, bias_out, gain_two, shift_two, bias_down, _ = [v.reshape(-1) for v in vec]
@@ -431,34 +429,40 @@
     prefix_pair = [jnp.where(core == 0, a, b) for a, b in ((prefix, swap(prefix)), (swap(prefix), prefix))]
     prefix_len = jnp.concatenate(prefix_pair, axis=1).reshape(-1)[sequence]
 
-    tokens = lax.optimization_barrier(tokens_in(after(hidden_in, small)))
-    if square:
-        out_others = jnp.concatenate(gather_shards(out_piece))
+    tokens_from = hidden_in
+    if square:
+        qkv_others = jnp.concatenate(gather_shards(qkv_piece))
+        tokens_from = after(hidden_in, qkv_others)
+        out_got = gather_shards(out_piece)
+        out_others = jnp.concatenate(out_got)
         fc1_others = jnp.concatenate(gather_shards(fc1_piece))
-        fc2_others = jnp.concatenate(gather_shards(fc2_piece))
+        fc2_got = gather_shards(after(fc2_piece, out_got[0]))
+        fc2_others = jnp.concatenate(fc2_got)
         qkv_x, qkv_y, qkv_low, qkv_high = spread_others(qkv_others)
-        out_others = after(out_others, (qkv_x, qkv_y))
+        qkv_ends = plane(qkv_low, 2), plane(qkv_high, 1)
+        out_others = after(out_others, (qkv_low, qkv_high))
         out_x, out_y, out_low, out_high = spread_others(out_others)
-        fc1_others = after(fc1_others, (qkv_low, qkv_high, out_others))
+        fc1_others = after(fc1_others, (qkv_ends, out_others))
         fc1_x, fc1_y, fc1_low, fc1_high = spread_others(fc1_others)
-        fc2_others = after(fc2_others, (fc1_low, fc1_high))
+        fc1_ends = plane(fc1_low, 2), plane(fc1_high, 1)
+        fc2_others = after(fc2_others, fc1_ends)
         fc2_x, fc2_y, fc2_low, fc2_high = spread_others(fc2_others)
 
+    tokens = lax.optimization_barrier(tokens_in(tokens_from))
     hidden_f = tokens.astype(F32)
     normed_own = normalize(hidden_f, gain_one, shift_one).astype(BF)
     normed_one = jnp.concatenate([normed_own, swap(normed_own)])
     none = jnp.zeros((), jnp.int32)
     if square:
-        normed_one = after(normed_one, fc1_others)
         qkv_mine = col_chunks(qkv_weight, qkv_chunk, 0, 3 * shards)
         qkv_full = whole_weight(
-            qkv_mine, None, 1, piece_rows, qkv_others, qkv_x, qkv_y, plane(qkv_low, 2), plane(qkv_high, 1)
+            qkv_mine, None, 1, piece_rows, qkv_others, qkv_x, qkv_y, *qkv_ends
         )
         out_full = whole_weight(
             out_weight, (2 * core, none), 1, piece_rows // 2, out_others, out_x, out_y, plane(out_low, 2), plane(out_high, 1)
         )
         fc1_full = whole_weight(
-            fc1_weight, (none, core), 2, piece_rows, fc1_others, fc1_x, fc1_y, plane(fc1_low, 2), plane(fc1_high, 1)
+            fc1_weight, (none, core), 2, piece_rows, fc1_others, fc1_x, fc1_y, *fc1_ends
         )
         fc2_full = whole_weight(
             fc2_weight,
@@ -471,7 +475,7 @@
             plane(fc2_low, 2),
             plane(fc2_high, 1),
         )
-        grads_mine = tokens_in(after(grad_out, fc1_others))
+        grads_mine = tokens_in(after(grad_out, fc2_others))
     else:
         qkv_full, out_full, fc1_full, fc2_full = [
             whole_weight_any(piece) for piece in (qkv_piece, out_piece, fc1_piece, fc2_piece)
@@ -507,7 +511,7 @@
         context = context.reshape(CORES * rows, half_width).astype(BF)
 
     if square:
-        context = after(context, (fc1_low, fc1_high))
+        context = after(context, fc1_ends)
 
     def own_sum(left_side, product):
         away = swap(product(left_side[rows:]).astype(BF))
@@ -516,6 +520,9 @@
     middle = hidden_f + (own_sum(context, lambda v: dot(v, out_full)) + bias_out)
     normed_two_own = normalize(middle, gain_two, shift_two).astype(BF)
     normed_two = jnp.concatenate([normed_two_own, swap(normed_two_own)])
+    grads_mine = after(grads_mine, normed_two)
+    if square:
+        normed_two = after(normed_two, (fc2_low, fc2_high))
     pre_act = dot(normed_two, fc1_full) + bias_up
     below = 0.5 * (1.0 + lax.erf(pre_act * math.sqrt(0.5)))
     density = jnp.exp(-0.5 * pre_act * pre_act) * (1.0 / math.sqrt(2.0 * math.pi))
@@ -527,12 +534,12 @@
     down_bias_grad = jnp.sum(grad_rows, axis=0)
 
     class Reduction:
-        def __init__(self, left_side, right_side):
+        def __init__(self, left_side, right_side, barrier=()):
             self.sides = (left_side, right_side)
             far_low = grad_block(left_side, right_side, 3, 0)
             far_high = grad_block(left_side, right_side, 3, 1)
             self.far = (plane(far_low, 2), plane(far_high, 1))
-            right_side = after(right_side, (far_low, far_high))
+            right_side = after(right_side, (far_low, far_high, *barrier))
             self.x_high = plane(grad_block(left_side, right_side, 1, 1), 1)
             self.y_low = plane(grad_block(left_side, right_side, 2, 0), 2)
             self.near = [grad_block(left_side, right_side, 1, 0), grad_block(left_side, right_side, 2, 1)]
@@ -557,11 +564,14 @@
     d_pre = (times_rows(grad_both, fc2_full) * slope.astype(F32)).astype(BF)
     up_bias_grad = jnp.sum(d_pre, axis=0, dtype=F32)
     if square:
-        fc1_red = Reduction(normed_two, d_pre)
         fc2_red.second()
+        d_pre = after(d_pre, (fc2_red.sent, fc2_red.x_high, fc2_red.y_low))
+        fc1_red = Reduction(normed_two, d_pre, (fc2_red.x_low, fc2_red.y_high))
         activated = after(activated, fc1_red.near)
     result_own = middle + (own_sum(activated, lambda v: dot(v, fc2_full)) + bias_down)
     result = tokens_out(result_own.astype(BF))
+    if square:
+        d_pre = after(d_pre, result_own)
     d_normed_two = own_sum(d_pre, lambda v: times_rows(v, fc1_full))
     back_two = jax.vjp(normalize, middle, gain_two, shift_two)[1]
     d_middle, gain_two_grad, shift_two_grad = back_two(d_normed_two)
@@ -590,7 +600,7 @@
     d_projected = jnp.concatenate([d_queries, d_keys, d_values], axis=1)
     if square:
         fc2_part = fc2_red.third()
-        d_projected = after(d_projected, (fc2_red.mine, result))
+        d_projected = after(d_projected, (fc2_red.mine, result, fc1_red.x_high, fc1_red.y_low))
         qkv_red = Reduction(normed_one, d_projected)
         out_red.second()
         fc1_part = fc1_red.third(qkv_red.near)
@@ -625,8 +635,6 @@
         ],
         axis=1,
     )
-    grad_in = tokens_out(grad_in_own)
-
     def sum_plane(values, bits):
         for bit in bits:
             values = values + plane(values, 1 << bit)
@@ -643,21 +651,23 @@
         out_part = out_red.third((qkv_red.sent, qkv_red.x_high, qkv_red.y_low))
         fc2_first = spread_first(after(fc2_part, (qkv_red.sent, out_red.mine)))
         qkv_part = qkv_red.third(grad_in_own)
+        grad_in = tokens_out(after(grad_in_own, qkv_part))
         packed = sum_plane(packed, [0])
-        fc1_first = spread_first(after(fc1_part, (fc2_first[1:], qkv_red.mine, packed, grad_in)))
+        fc1_first = spread_first(after(fc1_part, (fc2_first[1:], qkv_red.mine, packed)))
         fc2_pair = spread_second(*fc2_first)
         packed = sum_plane(packed, [1])
         out_first = spread_first(after(out_part, (fc1_first[1:], fc2_pair[0], packed)))
-        summed = sum_line(after(packed, grad_in))
+        summed = sum_line(after(packed, qkv_part))
         fc1_pair = spread_second(*fc1_first)
         fc2_weight_grad = spread_last(*fc2_pair, None)
         fc1_weight_grad = spread_last(*fc1_pair, fc1_chunk)
         out_pair = spread_second(*out_first)
-        qkv_first = spread_first(after(qkv_part, (out_pair[0], fc1_pair[0], fc2_weight_grad, summed)))
+        qkv_first = spread_first(after(qkv_part, (out_pair[0], fc1_pair[0], fc2_weight_grad)))
         out_weight_grad = spread_last(*out_pair, None)
         qkv_own, qkv_other = spread_second(*after(qkv_first, (fc1_weight_grad, out_pair[1])))
-        qkv_weight_grad = spread_last(qkv_own, after(qkv_other, out_weight_grad), qkv_chunk)
+        qkv_weight_grad = spread_last(qkv_own, after(qkv_other, (out_weight_grad, grad_in)), qkv_chunk)
     else:
+        grad_in = tokens_out(grad_in_own)
         summed = sum_line(sum_plane(packed, range(chips.bit_length() - 1)))
         fc2_weight_grad = spread_any(sum_any(activated, grad_both), None)
         fc1_weight_grad = spread_any(sum_any(normed_two, d_pre), fc1_chunk)

time: 1370 us -> 1340 us (0.978)
  waiting for transfers between devices: 555 us -> 508 us
  local copies, waits for them, and re-layouts: 79.7 us -> 107 us
    all_gather x4, waiting for transfers between devices: 60.1 us -> 159 us  [gather_shards(): held = lax.all_gather(piece, 'sh')]
    ppermute x6, waiting for transfers between devices: 83.6 us -> 15.6 us  [along(): lax.ppermute(value, 'sh', [(i, (i + hop) % shards) for i in range(shards)])]
    ppermute x4, waiting for transfers between devices: 115 us -> 60.4 us  [tokens_out(): lax.ppermute(lax.dynamic_index_in_dim(value, (turn + micro) % 2, 0, False...]
    ppermute x6, starting transfers between devices: 2.92 us -> 42.6 us  [along(): lax.ppermute(value, 'sh', [(i, (i + hop) % shards) for i in range(shards)])]
    ppermute x14, starting transfers between devices: 34.7 us -> 1.98 us  [swap(): return lax.ppermute(value, 'co', [(0, 1), (1, 0)])]
    ppermute x4, waiting for transfers between devices: 19 us -> 0.01 us  [tokens_in(): lax.ppermute(lax.dynamic_index_in_dim(value, (turn + shard) % 2, 0, False...]
    unnamed x265 -> x238, local copies, waits for them, and re-layouts: 36.8 us -> 55.5 us
  transfers between devices with their start and end apart: 94 -> 94, of which waited for: 31 -> 30; matrix products, arithmetic and copies ran while one was open for 32% -> 33% of each run, Pallas kernels for 13% -> 13%
where the time goes in v3:
time: 1340 us; the launch traced here: 1320 us
  waiting for transfers between devices  508 us (38%)
  matrix products  290 us (22%)
  Pallas kernels  193 us (14%)
  starting transfers between devices  130 us (10%)
  local copies, waits for them, and re-layouts  107 us (8%)
  other arithmetic  80.8 us (6%)
  between operations  15.8 us (1%)
    ppermute x58, waiting for transfers between devices, plane(): return lax.ppermute(value, 'ch', [(i, i ^ bit) for i in range(chips)])  272 us
    all_gather x4, waiting for transfers between devices, gather_shards(): held = lax.all_gather(piece, 'sh')  159 us
    pallas_call x8, Pallas kernels, place(): pl.pallas_call(body, grid_spec=pltpu.PrefetchScalarGridSpec(num_scalar_pr...  138 us
    dot_general x32, matrix products, cross_rows(): lax.dot_general(left_side, right_side, (((0,), (0,)), ((), ())), preferre...  121 us
    dot_general x6, matrix products, times_rows(): lax.dot_general(left_side, right_side, (((1,), (1,)), ((), ())), preferre...  91.7 us
    dot_general x6, matrix products, dot(): return jnp.dot(left_side, right_side, preferred_element_type=F32)  77.1 us
    ppermute x58, starting transfers between devices, plane(): return lax.ppermute(value, 'ch', [(i, i ^ bit) for i in range(chips)])  60.8 us
    ppermute x4, waiting for transfers between devices, tokens_out(): lax.ppermute(lax.dynamic_index_in_dim(value, (turn + micro) % 2, 0, False...  60.4 us
  transfers between devices with their start and end apart: 94, of which 30 were waited for; matrix products, arithmetic and copies ran while one was open for 33% of the time, Pallas kernels for 13%

profile of v3, /device:TPU:0, one launch (start us, length us, event | category | flops | bytes accessed | tf_op | source)
XLA Modules:
  0.0 1324.6 jit_solution(15158668425083286978)
XLA Ops:
  47.3 57.7 %all-gather.9.cloned.1.call-done = bf16[2048,768]{1,0:T(8,128)(2,1)} async-done(((bf16[512,768]{1,0:T(8,128)(2,1)}), bf16[2048,768]{1,0:T(8,128)(2,1)}) %all-gather.9.cloned.1.call-update) | async-done | bytes 3145744 | tf_op jit(solution)/shard_map/all_gather | solution.py:292
  113.1 9.5 collective-permute-start.3
  123.6 25.0 %all-gather.13.cloned.1.call-done = bf16[1024,512]{1,0:T(8,128)(2,1)} async-done(((bf16[256,512]{1,0:T(8,128)(2,1)}), bf16[1024,512]{1,0:T(8,128)(2,1)}) %all-gather.13.cloned.1.call-update) | async-done | bytes 1048592 | tf_op jit(solution)/shard_map/all_gather | solution.py:292
  149.9 10.1 collective-permute-done.8.refs_3_
  169.9 76.0 %all-gather.11.cloned.1.call-done = bf16[2048,1024]{1,0:T(8,128)(2,1)} async-done(((bf16[512,1024]{1,0:T(8,128)(2,1)}), bf16[2048,1024]{1,0:T(8,128)(2,1)}) %all-gather.11.cloned.1.call-update) | async-done | bytes 4194320 | tf_op jit(solution)/shard_map/all_gather | solution.py:292
  263.9 73.2 %collective-permute-done.16.refs_3_ = bf16[768,512]{1,0:T(8,128)(2,1)} collective-permute-done((bf16[768,512]{1,0:T(8,128)(2,1)S(1)}, bf16[768,512]{1,0:T(8,128)(2,1)}, u32[]{:S(2)}, u32[]{:S(2)}) %collective-permute-start.16) | collective-permute-done | bytes 786464 | tf_op jit(solution)/shard_map/ppermute | solution.py:254
  340.7 22.5 %shard_map.631 = bf16[2048,3072]{1,0:T(8,128)(2,1)} custom-call(s32[14,32]{1,0:T(8,128)} %get-tuple-element.184.table_ref, bf16[512,3072]{1,0:T(8,128)(2,1)} %get-tuple-element.124.refs_0_, bf16[1536,768]{1,0:T(8,128)(2,1)} %copy-done.13, bf16[1536,768]{1,0:T(8,128)(2,1)} %collective-permute-done.7.refs_2_, ...), custom_call_target="tpu_custom_call" | custom-call | tf_op jit(solution)/shard_map/pallas_call | solution.py:77
  371.3 18.4 %add_convert_fusion.q_ref.k_ref.v_ref = bf16[1024,3072]{1,0:T(8,128)(2,1)} fusion(bf16[2048,3072]{1,0:T(8,128)(2,1)} %shard_map.631, f32[3072]{0:T(1024)S(1)} %copy-done.63, bf16[512,2048]{1,0:T(8,128)(2,1)} %collective-permute-done.6, bf16[512,2048]{1,0:T(8,128)(2,1)} %fusion.12), kind=kOutput, calls=%fused_computation.10 | convolution fusion | flops 12899581952 | bytes 23080960 | tf_op jit(solution)/shard_map/dot_general | solution.py:30
  389.7 20.5 %shard_map.632 = bf16[1024,1024]{1,0:T(8,128)(2,1)} custom-call(s32[2]{0:T(128)} %pad_add_fusion.10.scal_ref, bf16[1024,3072]{1,0:T(8,128)(2,1)} %add_convert_fusion.q_ref.k_ref.v_ref, bf16[1024,3072]{1,0:T(8,128)(2,1)} %add_convert_fusion.q_ref.k_ref.v_ref, bf16[1024,3072]{1,0:T(8,128)(2,1)} %add_convert_fusion.q_ref.k_ref.v_ref), custom_call_target="tpu_custom_call" | custom-call | tf_op jit(solution)/shard_map/pallas_call | solution.py:172
  411.0 19.1 %shard_map.633 = bf16[1024,2048]{1,0:T(8,128)(2,1)} custom-call(s32[14,32]{1,0:T(8,128)} %get-tuple-element.183.table_ref, bf16[512,2048]{1,0:T(8,128)(2,1)} %refs_0_.3, bf16[768,512]{1,0:T(8,128)(2,1)} %copy-done.24, bf16[768,512]{1,0:T(8,128)(2,1)} %collective-permute-done.15.refs_2_, bf16[768,512]{1,0:T(8,128)(2,1)} %collective-permute-done.16.refs_3_, ...), custom_call_target="tpu_custom_call" | custom-call | tf_op jit(solution)/shard_map/pallas_call | solution.py:77
  457.3 24.9 %shard_map.634 = bf16[2048,4096]{1,0:T(8,128)(2,1)} custom-call(s32[14,32]{1,0:T(8,128)} %get-tuple-element.182.table_ref, bf16[512,8192]{1,0:T(8,128)(2,1)} %refs_0_.4, bf16[1536,1024]{1,0:T(8,128)(2,1)} %pad_maximum_fusion.7.refs_1_, bf16[1536,1024]{1,0:T(8,128)(2,1)} %collective-permute-done.11.refs_2_, ...), custom_call_target="tpu_custom_call" | custom-call | tf_op jit(solution)/shard_map/pallas_call | solution.py:77
  483.8 27.3 %collective-permute-done.22.refs_3_ = bf16[3072,512]{1,0:T(8,128)(2,1)} collective-permute-done((bf16[3072,512]{1,0:T(8,128)(2,1)}, bf16[3072,512]{1,0:T(8,128)(2,1)}, u32[]{:S(2)}, u32[]{:S(2)}) %collective-permute-start.22) | collective-permute-done | bytes 3145760 | tf_op jit(solution)/shard_map/ppermute | solution.py:254
  522.7 21.9 %multiply_convert_fusion.1 = (bf16[1024,4096]{1,0:T(8,128)(2,1)}, f32[1024,4096]{1,0:T(8,128)}) fusion(f32[4096]{0:T(1024)S(1)} %bitcast.185, bf16[1024,2048]{1,0:T(8,128)(2,1)S(1)} %pad_maximum_fusion.4, bf16[2048,4096]{1,0:T(8,128)(2,1)S(1)} %copy-done.12), kind=kOutput, calls=%fused_computation.8 | convolution fusion | flops 17205035008 | bytes 46153728 | tf_op jit(solution)/shard_map/dot_general | solution.py:30
  560.6 24.9 %shard_map.635 = bf16[4096,2048]{1,0:T(8,128)(2,1)} custom-call(s32[14,32]{1,0:T(8,128)} %get-tuple-element.183.table_ref, bf16[2048,2048]{1,0:T(8,128)(2,1)} %refs_0_.5, bf16[3072,512]{1,0:T(8,128)(2,1)} %pad_maximum_fusion.8.refs_1_, bf16[3072,512]{1,0:T(8,128)(2,1)} %collective-permute-done.21.refs_2_, bf16[3072,512]{1,0:T(8,128)(2,1)} %collective-permute-done.22.refs_3_, ...), custom_call_target="tpu_custom_call" | custom-call | tf_op jit(solution)/shard_map/pallas_call | solution.py:77
  614.4 28.4 %convert_reduce_fusion = (f32[4096]{0:T(1024)}, bf16[1024,4096]{1,0:T(8,128)(2,1)}) fusion(f32[1024,4096]{1,0:T(8,128)} %get-tuple-element.193, f32[4096]{0:T(1024)S(1)} %bitcast.186, bf16[1024,2048]{1,0:T(8,128)(2,1)} %constant_dynamic-update-slice_fusion, bf16[4096,2048]{1,0:T(8,128)(2,1)S(1)} %bitcast.160), kind=kOutput, calls=%fused_computation.6 | convolution fusion | flops 17242779648 | bytes 46170112 | tf_op jit(solution)/shard_map/dot_general | solution.py:38
  662.9 33.9 %collective-permute-done.32 = bf16[2048,512]{1,0:T(8,128)(2,1)} collective-permute-done((bf16[2048,512]{1,0:T(8,128)(2,1)}, bf16[2048,512]{1,0:T(8,128)(2,1)}, u32[]{:S(2)}, u32[]{:S(2)}) %collective-permute-start.32) | collective-permute-done | bytes 2097184 | tf_op jit(solution)/shard_map/ppermute | solution.py:254
  704.3 12.2 fusion.37
  729.2 14.1 %add_add_fusion.2 = bf16[512,2048]{1,0:T(8,128)(2,1)S(1)} fusion(f32[512,2048]{1,0:T(8,128)S(1)} %copy-done.3, bf16[512,2048]{1,0:T(8,128)(2,1)} %copy-done.78, bf16[4096,2048]{1,0:T(8,128)(2,1)} %shard_map.635, bf16[1024,4096]{1,0:T(8,128)(2,1)} %get-tuple-element.81, f32[2048]{0:T(1024)S(1)} %bitcast.190), kind=kOutput, calls=%fused_computation.59 | convolution fusion | flops 8595177472 | bytes 29368320 | tf_op jit(solution)/shard_map/dot_general | solution.py:30
  743.3 15.0 %fusion.40 = bf16[512,2048]{1,0:T(8,128)(2,1)} fusion(bf16[2048,4096]{1,0:T(8,128)(2,1)} %shard_map.634, bf16[1024,4096]{1,0:T(8,128)(2,1)} %get-tuple-element.82), kind=kOutput, calls=%fused_computation.86 | convolution fusion | flops 8590983168 | bytes 23068672 | tf_op jit(solution)/shard_map/dot_general | solution.py:38
  778.9 18.4 %multiply_reduce_fusion = (f32[2048]{0:T(1024)S(1)}, f32[512]{0:T(512)S(1)}, f32[2048]{0:T(1024)S(1)}, f32[512,2048]{1,0:T(8,128)}) fusion(f32[512,2048]{1,0:T(8,128)} %copy-done.2, f32[512]{0:T(512)S(1)} %copy-done.59, f32[512]{0:T(512)S(1)} %copy-done.52, f32[2048]{0:T(1024)S(1)} %bitcast.176, bf16[512,2048]{1,0:T(8,128)(2,1)} %collective-permute-done.37, ...), kind=kOutput, calls=%fused_computation.43 | convolution fusion | flops 8600416256 | bytes 31488000 | tf_op jit(solution)/shard_map/dot_general | solution.py:38
  831.9 60.4 %collective-permute-done.36 = bf16[256,2048]{1,0:T(8,128)(2,1)} collective-permute-done((bf16[256,2048]{1,0:T(8,128)(2,1)}, bf16[256,2048]{1,0:T(8,128)(2,1)}, u32[]{:S(2)}, u32[]{:S(2)}) %collective-permute-start.36) | collective-permute-done | bytes 1048608 | tf_op jit(solution)/shard_map/ppermute | solution.py:281
  903.2 34.3 %shard_map.636 = (bf16[1024,1024]{1,0:T(8,128)(2,1)}, bf16[1024,1024]{1,0:T(8,128)(2,1)}, bf16[1024,1024]{1,0:T(8,128)(2,1)}) custom-call(s32[2]{0:T(128)} %pad_add_fusion.10.scal_ref, bf16[1024,3072]{1,0:T(8,128)(2,1)} %add_convert_fusion.q_ref.k_ref.v_ref, bf16[1024,3072]{1,0:T(8,128)(2,1)} %add_convert_fusion.q_ref.k_ref.v_ref, ...), custom_call_target="tpu_custom_call" | custom-call | tf_op jit(solution)/shard_map/pallas_call | solution.py:188
  985.8 18.8 %collective-permute-done.46 = bf16[512,512]{1,0:T(8,128)(2,1)S(1)} collective-permute-done((bf16[512,512]{1,0:T(8,128)(2,1)S(1)}, bf16[512,512]{1,0:T(8,128)(2,1)S(1)}, u32[]{:S(2)}, u32[]{:S(2)}) %collective-permute-start.46) | collective-permute-done | bytes 524320 | tf_op jit(solution)/shard_map/ppermute | solution.py:254
  1014.6 11.1 fusion.34
  1035.3 17.7 %collective-permute-done.65 = bf16[512,512]{1,0:T(8,128)(2,1)} collective-permute-done((bf16[512,512]{1,0:T(8,128)(2,1)}, bf16[512,512]{1,0:T(8,128)(2,1)}, u32[]{:S(2)}, u32[]{:S(2)}) %collective-permute-start.65) | collective-permute-done | bytes 524320 | tf_op jit(solution)/shard_map/ppermute | solution.py:254
  1061.0 12.9 fusion.167
  1121.4 25.7 %collective-permute-done.70 = bf16[512,512]{1,0:T(8,128)(2,1)S(1)} collective-permute-done((bf16[512,512]{1,0:T(8,128)(2,1)S(1)}, bf16[512,512]{1,0:T(8,128)(2,1)S(1)}, u32[]{:S(2)}, u32[]{:S(2)}) %collective-permute-start.70) | collective-permute-done | bytes 524320 | tf_op jit(solution)/shard_map/ppermute | solution.py:254
  1187.3 11.7 shard_map.637
  1200.7 11.7 shard_map.638
  1246.2 14.4 %collective-permute-done.61 = f32[6144]{0:T(1024)S(1)} collective-permute-done((f32[6144]{0:T(1024)S(1)}, f32[6144]{0:T(1024)S(1)}, u32[]{:S(2)}, u32[]{:S(2)}) %collective-permute-start.61) | collective-permute-done | bytes 24608 | tf_op jit(solution)/shard_map/ppermute | solution.py:251
  1260.6 28.8 %collective-permute-start.60 = (f32[6144]{0:T(1024)S(1)}, f32[6144]{0:T(1024)S(1)}, u32[]{:S(2)}, u32[]{:S(2)}) collective-permute-start(f32[6144]{0:T(1024)S(1)} %bitcast.182), channel_id=1, source_target_pairs={{0,2},{1,3},{2,0},{3,1},{4,6},{5,7},{6,4},{7,5},{8,10},{9,11},{10,... | collective-permute-start | bytes 73736 | tf_op jit(solution)/shard_map/ppermute | solution.py:251
  1301.0 16.6 %shard_map.640 = f32[512,6144]{1,0:T(8,128)} custom-call(s32[6,24]{1,0:T(8,128)} %pad_add_fusion.8.table_ref, bf16[2048,768]{1,0:T(8,128)(2,1)} %constant_dynamic-update-slice_fusion.26.refs_0_, bf16[2048,768]{1,0:T(8,128)(2,1)} %collective-permute-done.85.refs_1_), custom_call_target="tpu_custom_call" | custom-call | tf_op jit(solution)/shard_map/pallas_call | solution.py:77
  (598 shorter events, 491.6 us)
Async XLA Ops:
  7.2 97.8 %all-gather.9.cloned.1.call-start = ((), (), s32[]{:S(2)}) async-start(), calls=%async_computation.8 | async-start | bytes 3932160 | tf_op jit(solution)/shard_map/all_gather | solution.py:292
  43.1 105.5 %all-gather.13.cloned.1.call-start = ((), (), s32[]{:S(2)}) async-start(), calls=%async_computation.10 | async-start | bytes 1310720 | tf_op jit(solution)/shard_map/all_gather | solution.py:292
  44.9 201.1 %all-gather.11.cloned.1.call-start = ((), (), s32[]{:S(2)}) async-start(), calls=%async_computation.9 | async-start | bytes 5242880 | tf_op jit(solution)/shard_map/all_gather | solution.py:292
  47.2 389.2 %all-gather.15.cloned.1.call-start = ((), (), s32[]{:S(2)}) async-start(), calls=%async_computation.11 | async-start | bytes 5242880 | tf_op jit(solution)/shard_map/all_gather | solution.py:292
  162.4 87.5 %collective-permute-start.10 = (bf16[768,768]{1,0:T(8,128)(2,1)}, bf16[768,768]{1,0:T(8,128)(2,1)}, u32[]{:S(2)}, u32[]{:S(2)}) collective-permute-start(bf16[768,768]{1,0:T(8,128)(2,1)} %bitcast.12), channel_id=1, source_target_pairs={{0,8},{8,0},{16,24},{24,16},{1,9},{9,1},{17,25},{25,17},{2,10},{10... | collective-permute-start | bytes 3538952 | tf_op jit(solution)/shard_map/ppermute | solution.py:254
  166.3 83.7 %collective-permute-start.9 = (bf16[768,768]{1,0:T(8,128)(2,1)}, bf16[768,768]{1,0:T(8,128)(2,1)}, u32[]{:S(2)}, u32[]{:S(2)}) collective-permute-start(bf16[768,768]{1,0:T(8,128)(2,1)} %bitcast.10), channel_id=1, source_target_pairs={{0,16},{8,24},{16,0},{24,8},{1,17},{9,25},{17,1},{25,9},{2,18},{10... | collective-permute-start | bytes 3538952 | tf_op jit(solution)/shard_map/ppermute | solution.py:254
  249.9 113.2 %collective-permute-start.13 = (bf16[1536,1024]{1,0:T(8,128)(2,1)}, bf16[1536,1024]{1,0:T(8,128)(2,1)}, u32[]{:S(2)}, u32[]{:S(2)}) collective-permute-start(bf16[1536,1024]{1,0:T(8,128)(2,1)} %pad_maximum_fusion.7.refs_1_), channel_id=1, source_target_pairs={{0,16},{8,24},{16,0},{24,8},{1,17},{9,25},{17,1},{25,9},{2,18},{10... | collective-permute-start | bytes 9437192 | tf_op jit(solution)/shard_map/ppermute | solution.py:254
  250.6 116.6 %collective-permute-start.11 = (bf16[1536,1024]{1,0:T(8,128)(2,1)}, bf16[1536,1024]{1,0:T(8,128)(2,1)}, u32[]{:S(2)}, u32[]{:S(2)}) collective-permute-start(bf16[1536,1024]{1,0:T(8,128)(2,1)} %pad_maximum_fusion.7.refs_1_), channel_id=1, source_target_pairs={{0,8},{8,0},{16,24},{24,16},{1,9},{9,1},{17,25},{25,17},{2,10},{10... | collective-permute-start | bytes 9437192 | tf_op jit(solution)/shard_map/ppermute | solution.py:254
  254.3 117.0 %collective-permute-start.6 = (bf16[512,2048]{1,0:T(8,128)(2,1)}, bf16[512,2048]{1,0:T(8,128)(2,1)}, u32[]{:S(2)}, u32[]{:S(2)}) collective-permute-start(bf16[512,2048]{1,0:T(8,128)(2,1)} %fusion.12), channel_id=1, source_target_pairs={{0,4},{4,0},{1,5},{5,1},{2,6},{6,2},{3,7},{7,3},{8,12},{12,8},{9,1... | collective-permute-start | bytes 6291464 | tf_op jit(solution)/shard_map/ppermute | solution.py:257
  257.3 802.2 %reduce-scatter.11.cloned.1.call-start = ((), (), s32[]{:S(2)}) async-start(), calls=%async_computation.7 | async-start | bytes 5242880 | tf_op jit(solution)/shard_map/reduce_scatter | solution.py:344
  257.9 79.3 %collective-permute-start.16 = (bf16[768,512]{1,0:T(8,128)(2,1)S(1)}, bf16[768,512]{1,0:T(8,128)(2,1)}, u32[]{:S(2)}, u32[]{:S(2)}) collective-permute-start(bf16[768,512]{1,0:T(8,128)(2,1)S(1)} %pad_maximum_fusion.17.refs_1_), channel_id=1, source_target_pairs={{0,16},{8,24},{16,0},{24,8},{1,17},{9,25},{17,1},{25,9},{2,18},{10... | collective-permute-start | bytes 2359304 | tf_op jit(solution)/shard_map/ppermute | solution.py:254
  259.2 79.7 %collective-permute-start.15 = (bf16[768,512]{1,0:T(8,128)(2,1)S(1)}, bf16[768,512]{1,0:T(8,128)(2,1)}, u32[]{:S(2)}, u32[]{:S(2)}) collective-permute-start(bf16[768,512]{1,0:T(8,128)(2,1)S(1)} %pad_maximum_fusion.17.refs_1_), channel_id=1, source_target_pairs={{0,8},{8,0},{16,24},{24,16},{1,9},{9,1},{17,25},{25,17},{2,10},{10... | collective-permute-start | bytes 2359304 | tf_op jit(solution)/shard_map/ppermute | solution.py:254
  338.2 72.0 %collective-permute-start.18 = (bf16[384,512]{1,0:T(8,128)(2,1)S(1)}, bf16[384,512]{1,0:T(8,128)(2,1)}, u32[]{:S(2)}, u32[]{:S(2)}) collective-permute-start(bf16[384,512]{1,0:T(8,128)(2,1)S(1)} %bitcast.167), channel_id=1, source_target_pairs={{0,8},{8,0},{16,24},{24,16},{1,9},{9,1},{17,25},{25,17},{2,10},{10... | collective-permute-start | bytes 1179656 | tf_op jit(solution)/shard_map/ppermute | solution.py:254
  339.9 70.3 %collective-permute-start.17 = (bf16[384,512]{1,0:T(8,128)(2,1)S(1)}, bf16[384,512]{1,0:T(8,128)(2,1)S(1)}, u32[]{:S(2)}, u32[]{:S(2)}) collective-permute-start(bf16[384,512]{1,0:T(8,128)(2,1)S(1)} %bitcast.168), channel_id=1, source_target_pairs={{0,16},{8,24},{16,0},{24,8},{1,17},{9,25},{17,1},{25,9},{2,18},{10... | collective-permute-start | bytes 1179656 | tf_op jit(solution)/shard_map/ppermute | solution.py:254
  365.9 64.3 %collective-permute-start.14 = (bf16[768,1024]{1,0:T(8,128)(2,1)}, bf16[768,1024]{1,0:T(8,128)(2,1)}, u32[]{:S(2)}, u32[]{:S(2)}) collective-permute-start(bf16[768,1024]{1,0:T(8,128)(2,1)} %bitcast.26), channel_id=1, source_target_pairs={{0,8},{8,0},{16,24},{24,16},{1,9},{9,1},{17,25},{25,17},{2,10},{10... | collective-permute-start | bytes 4718600 | tf_op jit(solution)/shard_map/ppermute | solution.py:254
  440.3 70.8 %collective-permute-start.22 = (bf16[3072,512]{1,0:T(8,128)(2,1)}, bf16[3072,512]{1,0:T(8,128)(2,1)}, u32[]{:S(2)}, u32[]{:S(2)}) collective-permute-start(bf16[3072,512]{1,0:T(8,128)(2,1)} %pad_maximum_fusion.8.refs_1_), channel_id=1, source_target_pairs={{0,16},{8,24},{16,0},{24,8},{1,17},{9,25},{17,1},{25,9},{2,18},{10... | collective-permute-start | bytes 9437192 | tf_op jit(solution)/shard_map/ppermute | solution.py:254
  440.9 73.6 %collective-permute-start.21 = (bf16[3072,512]{1,0:T(8,128)(2,1)}, bf16[3072,512]{1,0:T(8,128)(2,1)}, u32[]{:S(2)}, u32[]{:S(2)}) collective-permute-start(bf16[3072,512]{1,0:T(8,128)(2,1)} %pad_maximum_fusion.8.refs_1_), channel_id=1, source_target_pairs={{0,8},{8,0},{16,24},{24,16},{1,9},{9,1},{17,25},{25,17},{2,10},{10... | collective-permute-start | bytes 9437192 | tf_op jit(solution)/shard_map/ppermute | solution.py:254
  449.1 69.6 %collective-permute-start.20 = (bf16[512,2048]{1,0:T(8,128)(2,1)S(1)}, bf16[512,2048]{1,0:T(8,128)(2,1)}, u32[]{:S(2)}, u32[]{:S(2)}) collective-permute-start(bf16[512,2048]{1,0:T(8,128)(2,1)S(1)} %add_convert_fusion.6), channel_id=1, source_target_pairs={{0,4},{4,0},{1,5},{5,1},{2,6},{6,2},{3,7},{7,3},{8,12},{12,8},{9,1... | collective-permute-start | bytes 6291464 | tf_op jit(solution)/shard_map/ppermute | solution.py:257
  605.4 91.5 %collective-permute-start.32 = (bf16[2048,512]{1,0:T(8,128)(2,1)}, bf16[2048,512]{1,0:T(8,128)(2,1)}, u32[]{:S(2)}, u32[]{:S(2)}) collective-permute-start(bf16[2048,512]{1,0:T(8,128)(2,1)} %fusion.52), channel_id=1, source_target_pairs={{0,8},{8,0},{16,24},{24,16},{1,9},{9,1},{17,25},{25,17},{2,10},{10... | collective-permute-start | bytes 6291464 | tf_op jit(solution)/shard_map/ppermute | solution.py:254
  613.2 83.6 %collective-permute-start.33 = (bf16[2048,512]{1,0:T(8,128)(2,1)}, bf16[2048,512]{1,0:T(8,128)(2,1)}, u32[]{:S(2)}, u32[]{:S(2)}) collective-permute-start(bf16[2048,512]{1,0:T(8,128)(2,1)} %fusion.55), channel_id=1, source_target_pairs={{0,16},{8,24},{16,0},{24,8},{1,17},{9,25},{17,1},{25,9},{2,18},{10... | collective-permute-start | bytes 6291464 | tf_op jit(solution)/shard_map/ppermute | solution.py:254
  720.5 92.3 %collective-permute-start.39 = (bf16[1024,1024]{1,0:T(8,128)(2,1)}, bf16[1024,1024]{1,0:T(8,128)(2,1)}, u32[]{:S(2)}, u32[]{:S(2)}) collective-permute-start(bf16[1024,1024]{1,0:T(8,128)(2,1)} %convolution_convert_fusion.15), channel_id=1, source_target_pairs={{0,16},{8,24},{16,0},{24,8},{1,17},{9,25},{17,1},{25,9},{2,18},{10... | collective-permute-start | bytes 6291464 | tf_op jit(solution)/shard_map/ppermute | solution.py:254
  721.2 91.5 %collective-permute-start.40 = (bf16[1024,1024]{1,0:T(8,128)(2,1)}, bf16[1024,1024]{1,0:T(8,128)(2,1)}, u32[]{:S(2)}, u32[]{:S(2)}) collective-permute-start(bf16[1024,1024]{1,0:T(8,128)(2,1)} %convolution_convert_fusion.14), channel_id=1, source_target_pairs={{0,8},{8,0},{16,24},{24,16},{1,9},{9,1},{17,25},{25,17},{2,10},{10... | collective-permute-start | bytes 6291464 | tf_op jit(solution)/shard_map/ppermute | solution.py:254
  773.2 338.5 %reduce-scatter.9.cloned.1.call-start = ((), (), s32[]{:S(2)}) async-start(), calls=%async_computation.6 | async-start | bytes 5242880 | tf_op jit(solution)/shard_map/reduce_scatter | solution.py:344
  776.6 115.7 %collective-permute-start.36 = (bf16[256,2048]{1,0:T(8,128)(2,1)}, bf16[256,2048]{1,0:T(8,128)(2,1)}, u32[]{:S(2)}, u32[]{:S(2)}) collective-permute-start(bf16[256,2048]{1,0:T(8,128)(2,1)} %get-tuple-element.148), channel_id=1, source_target_pairs={{2,0},{0,1},{6,2},{4,3},{3,4},{1,5},{7,6},{5,7},{10,8},{8,9},{14,1... | collective-permute-start | bytes 3145736 | tf_op jit(solution)/shard_map/ppermute | solution.py:281
  804.2 91.8 %collective-permute-start.38 = (bf16[512,2048]{1,0:T(8,128)(2,1)S(1)}, bf16[512,2048]{1,0:T(8,128)(2,1)S(1)}, u32[]{:S(2)}, u32[]{:S(2)}) collective-permute-start(bf16[512,2048]{1,0:T(8,128)(2,1)S(1)} %get-tuple-element.121), channel_id=1, source_target_pairs={{0,4},{4,0},{1,5},{5,1},{2,6},{6,2},{3,7},{7,3},{8,12},{12,8},{9,1... | collective-permute-start | bytes 6291464 | tf_op jit(solution)/shard_map/ppermute | solution.py:257
  820.7 133.0 %collective-permute-start.44 = (bf16[1024,1024]{1,0:T(8,128)(2,1)}, bf16[1024,1024]{1,0:T(8,128)(2,1)}, u32[]{:S(2)}, u32[]{:S(2)}) collective-permute-start(bf16[1024,1024]{1,0:T(8,128)(2,1)} %add.664), channel_id=1, source_target_pairs={{0,8},{8,0},{16,24},{24,16},{1,9},{9,1},{17,25},{25,17},{2,10},{10... | collective-permute-start | bytes 6291464 | tf_op jit(solution)/shard_map/ppermute | solution.py:254
  825.6 115.6 %collective-permute-start.41 = (bf16[1024,1024]{1,0:T(8,128)(2,1)}, bf16[1024,1024]{1,0:T(8,128)(2,1)}, u32[]{:S(2)}, u32[]{:S(2)}) collective-permute-start(bf16[1024,1024]{1,0:T(8,128)(2,1)} %convolution_convert_fusion.10), channel_id=1, source_target_pairs={{0,8},{8,0},{16,24},{24,16},{1,9},{9,1},{17,25},{25,17},{2,10},{10... | collective-permute-start | bytes 6291464 | tf_op jit(solution)/shard_map/ppermute | solution.py:254
  830.3 110.9 %collective-permute-start.42 = (bf16[1024,1024]{1,0:T(8,128)(2,1)}, bf16[1024,1024]{1,0:T(8,128)(2,1)}, u32[]{:S(2)}, u32[]{:S(2)}) collective-permute-start(bf16[1024,1024]{1,0:T(8,128)(2,1)} %convolution_convert_fusion.9), channel_id=1, source_target_pairs={{0,16},{8,24},{16,0},{24,8},{1,17},{9,25},{17,1},{25,9},{2,18},{10... | collective-permute-start | bytes 6291464 | tf_op jit(solution)/shard_map/ppermute | solution.py:254
  963.7 206.7 %reduce-scatter.7.cloned.1.call-start = ((), (), s32[]{:S(2)}) async-start(), calls=%async_computation.5 | async-start | bytes 1310720 | tf_op jit(solution)/shard_map/reduce_scatter | solution.py:344
  1059.4 139.6 %reduce-scatter.5.cloned.1.call-start = ((), (), s32[]{:S(2)}) async-start(), calls=%async_computation.4 | async-start | bytes 3932160 | tf_op jit(solution)/shard_map/reduce_scatter | solution.py:344
  1233.5 67.5 %collective-permute-start.85 = (bf16[2048,768]{1,0:T(8,128)(2,1)}, bf16[2048,768]{1,0:T(8,128)(2,1)}, u32[]{:S(2)}, u32[]{:S(2)}) collective-permute-start(bf16[2048,768]{1,0:T(8,128)(2,1)} %constant_dynamic-update-slice_fusion.26.refs_0_), channel_id=1, source_target_pairs={{0,4},{4,0},{1,5},{5,1},{2,6},{6,2},{3,7},{7,3},{8,12},{12,8},{9,1... | collective-permute-start | bytes 9437192 | tf_op jit(solution)/shard_map/ppermute | solution.py:257
  1234.7 64.7 %collective-permute-start.54 = (bf16[256,2048]{1,0:T(8,128)(2,1)}, bf16[256,2048]{1,0:T(8,128)(2,1)S(1)}, u32[]{:S(2)}, u32[]{:S(2)}) collective-permute-start(bf16[256,2048]{1,0:T(8,128)(2,1)} %get-tuple-element.143), channel_id=1, source_target_pairs={{0,0},{2,1},{4,2},{6,3},{1,4},{3,5},{5,6},{7,7},{8,8},{10,9},{12,1... | collective-permute-start | bytes 3145736 | tf_op jit(solution)/shard_map/ppermute | solution.py:281
  (154 other events, 3965.3 us)
Sparse Core Ops, SparseCore 0:
  43.2 61.7 all-gather.8
  107.2 41.4 all-gather.12
  150.2 95.6 all-gather.10
  257.4 80.2 all-gather.14
  773.3 108.0 reduce-scatter.10
  963.8 74.2 reduce-scatter.8
  1059.5 30.8 reduce-scatter.6
  1098.0 63.3 reduce-scatter.4

commit v4 on v3

--- a/solution.py
+++ b/solution.py
@@ -289,8 +289,12 @@
         return jnp.stack([jnp.where(even, got[0], got[1]), jnp.where(even, got[1], got[0])])
 
     def gather_shards(piece):
-        held = lax.all_gather(piece, "sh")
-        return [lax.dynamic_index_in_dim(held, (shard - hop) % shards, 0, False) for hop in range(1, shards)]
+        return lax.all_gather(piece, "sh")
+
+    def others_of(held):
+        return jnp.concatenate(
+            [lax.dynamic_index_in_dim(held, (shard - hop) % shards, 0, False) for hop in range(1, shards)]
+        )
 
     def spread_others(others):
         from_x = plane(others, 1)
@@ -332,13 +336,12 @@
         everything = lax.all_gather(lax.all_gather(piece, "sh"), "ch")
         return everything.transpose(1, 2, 0, 3).reshape(-1, chips * piece.shape[1])
 
-    def grad_block(left_side, right_side, flip, half=None):
+    def grad_block(left_side, right_side, flips, half):
         cut = right_side.shape[1] // chips
-        block = lax.dynamic_slice_in_dim(right_side, (ch ^ flip) * cut, cut, 1)
-        if half is not None:
-            width_half = left_side.shape[1] // 2
-            left_side = left_side[:, half * width_half : (half + 1) * width_half]
-        return cross_rows(left_side, block).astype(BF)
+        blocks = [lax.dynamic_slice_in_dim(right_side, (ch ^ flip) * cut, cut, 1) for flip in flips]
+        block = blocks[0] if len(flips) == 1 else jnp.concatenate(blocks, axis=1)
+        width_half = left_side.shape[1] // 2
+        return cross_rows(left_side[:, half * width_half : (half + 1) * width_half], block).astype(BF)
 
     def sum_shards(mine):
         return lax.psum_scatter(mine, "sh", scatter_dimension=0, tiled=True)
@@ -431,22 +434,15 @@
 
     tokens_from = hidden_in
     if square:
-        qkv_others = jnp.concatenate(gather_shards(qkv_piece))
+        qkv_others = others_of(gather_shards(qkv_piece))
         tokens_from = after(hidden_in, qkv_others)
         out_got = gather_shards(out_piece)
-        out_others = jnp.concatenate(out_got)
-        fc1_others = jnp.concatenate(gather_shards(fc1_piece))
-        fc2_got = gather_shards(after(fc2_piece, out_got[0]))
-        fc2_others = jnp.concatenate(fc2_got)
+        fc1_got = gather_shards(fc1_piece)
+        fc2_got = gather_shards(after(fc2_piece, out_got))
         qkv_x, qkv_y, qkv_low, qkv_high = spread_others(qkv_others)
         qkv_ends = plane(qkv_low, 2), plane(qkv_high, 1)
-        out_others = after(out_others, (qkv_low, qkv_high))
+        out_others = others_of(after(out_got, (qkv_low, qkv_high)))
         out_x, out_y, out_low, out_high = spread_others(out_others)
-        fc1_others = after(fc1_others, (qkv_ends, out_others))
-        fc1_x, fc1_y, fc1_low, fc1_high = spread_others(fc1_others)
-        fc1_ends = plane(fc1_low, 2), plane(fc1_high, 1)
-        fc2_others = after(fc2_others, fc1_ends)
-        fc2_x, fc2_y, fc2_low, fc2_high = spread_others(fc2_others)
 
     tokens = lax.optimization_barrier(tokens_in(tokens_from))
     hidden_f = tokens.astype(F32)
@@ -461,6 +457,21 @@
         out_full = whole_weight(
             out_weight, (2 * core, none), 1, piece_rows // 2, out_others, out_x, out_y, plane(out_low, 2), plane(out_high, 1)
         )
+    else:
+        qkv_full, out_full, fc1_full, fc2_full = [
+            whole_weight_any(piece) for piece in (qkv_piece, out_piece, fc1_piece, fc2_piece)
+        ]
+        grads_mine = tokens_in(grad_out)
+
+    half_width = width // CORES
+    projected = dot(normed_one, qkv_full) + jnp.concatenate([bias_query, jnp.zeros_like(bias_query), bias_value])
+    projected = projected.astype(BF)
+    if square:
+        fc1_others = others_of(after(fc1_got, (projected, out_low, out_high)))
+        fc1_x, fc1_y, fc1_low, fc1_high = spread_others(fc1_others)
+        fc1_ends = plane(fc1_low, 2), plane(fc1_high, 1)
+        fc2_others = others_of(after(fc2_got, fc1_ends))
+        fc2_x, fc2_y, fc2_low, fc2_high = spread_others(fc2_others)
         fc1_full = whole_weight(
             fc1_weight, (none, core), 2, piece_rows, fc1_others, fc1_x, fc1_y, *fc1_ends
         )
@@ -476,16 +487,7 @@
             plane(fc2_high, 1),
         )
         grads_mine = tokens_in(after(grad_out, fc2_others))
-    else:
-        qkv_full, out_full, fc1_full, fc2_full = [
-            whole_weight_any(piece) for piece in (qkv_piece, out_piece, fc1_piece, fc2_piece)
-        ]
-        grads_mine = tokens_in(grad_out)
     grads_mine = lax.optimization_barrier(grads_mine)
-
-    half_width = width // CORES
-    projected = dot(normed_one, qkv_full) + jnp.concatenate([bias_query, jnp.zeros_like(bias_query), bias_value])
-    projected = projected.astype(BF)
     scalars = jnp.stack([core.astype(jnp.int32), prefix_len.astype(jnp.int32)])
     if parts == 1:
         context = attend_forward(projected, scalars)
@@ -536,26 +538,26 @@
     class Reduction:
         def __init__(self, left_side, right_side, barrier=()):
             self.sides = (left_side, right_side)
-            far_low = grad_block(left_side, right_side, 3, 0)
-            far_high = grad_block(left_side, right_side, 3, 1)
-            self.far = (plane(far_low, 2), plane(far_high, 1))
-            right_side = after(right_side, (far_low, far_high, *barrier))
-            self.x_high = plane(grad_block(left_side, right_side, 1, 1), 1)
-            self.y_low = plane(grad_block(left_side, right_side, 2, 0), 2)
-            self.near = [grad_block(left_side, right_side, 1, 0), grad_block(left_side, right_side, 2, 1)]
-
-        def second(self, barrier=None):
-            far = self.far if barrier is None else tuple(after(value, barrier) for value in self.far)
-            self.sent = [self.near[0] + far[0], self.near[1] + far[1]]
+            self.cut = right_side.shape[1] // chips
+            to_x = grad_block(left_side, right_side, (3, 1), 1)
+            to_y = grad_block(left_side, right_side, (3, 2), 0)
+            self.from_x = plane(to_x, 1)
+            self.from_y = plane(to_y, 2)
+            right_side = after(right_side, (to_x, to_y, *barrier))
+            self.near = [grad_block(left_side, right_side, (1,), 0), grad_block(left_side, right_side, (2,), 1)]
+
+        def second(self, barrier=()):
+            from_x, from_y, *_ = lax.optimization_barrier((self.from_x, self.from_y, *barrier))
+            self.sent = [self.near[0] + from_y[:, : self.cut], self.near[1] + from_x[:, : self.cut]]
             self.x_low = plane(self.sent[0], 1)
             self.y_high = plane(self.sent[1], 2)
 
-        def third(self, barrier=None):
-            x_low, y_high = self.x_low, self.y_high
-            if barrier is not None:
-                x_low, y_high = after(x_low, barrier), after(y_high, barrier)
-            low_part = grad_block(*self.sides, 0, 0).astype(F32) + x_low.astype(F32) + self.y_low.astype(F32)
-            high_part = grad_block(*self.sides, 0, 1).astype(F32) + self.x_high.astype(F32) + y_high.astype(F32)
+        def third(self, barrier=()):
+            x_low, y_high, *_ = lax.optimization_barrier((self.x_low, self.y_high, *barrier))
+            low_part = grad_block(*self.sides, (0,), 0).astype(F32) + x_low.astype(F32)
+            high_part = grad_block(*self.sides, (0,), 1).astype(F32) + y_high.astype(F32)
+            low_part = low_part + self.from_y[:, self.cut :].astype(F32)
+            high_part = high_part + self.from_x[:, self.cut :].astype(F32)
             self.mine = jnp.concatenate([low_part.astype(BF), high_part.astype(BF)])
             return sum_shards(self.mine)
 
@@ -565,13 +567,11 @@
     up_bias_grad = jnp.sum(d_pre, axis=0, dtype=F32)
     if square:
         fc2_red.second()
-        d_pre = after(d_pre, (fc2_red.sent, fc2_red.x_high, fc2_red.y_low))
+        d_pre = after(d_pre, fc2_red.sent)
         fc1_red = Reduction(normed_two, d_pre, (fc2_red.x_low, fc2_red.y_high))
         activated = after(activated, fc1_red.near)
     result_own = middle + (own_sum(activated, lambda v: dot(v, fc2_full)) + bias_down)
     result = tokens_out(result_own.astype(BF))
-    if square:
-        d_pre = after(d_pre, result_own)
     d_normed_two = own_sum(d_pre, lambda v: times_rows(v, fc1_full))
     back_two = jax.vjp(normalize, middle, gain_two, shift_two)[1]
     d_middle, gain_two_grad, shift_two_grad = back_two(d_normed_two)
@@ -580,7 +580,7 @@
     out_bias_grad = jnp.sum(d_attn_own, axis=0, dtype=F32)
     d_attn = jnp.concatenate([d_attn_own, swap(d_attn_own)])
     if square:
-        fc1_red.second(fc2_red.sent)
+        fc1_red.second((*fc2_red.sent, result_own))
         out_red = Reduction(context, d_attn)
     d_context = times_rows(d_attn, out_full).astype(BF)
     if square:
@@ -600,18 +600,19 @@
     d_projected = jnp.concatenate([d_queries, d_keys, d_values], axis=1)
     if square:
         fc2_part = fc2_red.third()
-        d_projected = after(d_projected, (fc2_red.mine, result, fc1_red.x_high, fc1_red.y_low))
+        d_projected = after(d_projected, (fc2_red.mine, result))
         qkv_red = Reduction(normed_one, d_projected)
         out_red.second()
-        fc1_part = fc1_red.third(qkv_red.near)
-        qkv_red.second((fc1_red.mine, out_red.sent))
-        d_projected = after(d_projected, qkv_red.sent)
+        d_projected = after(d_projected, qkv_red.near)
+        fc1_part = fc1_red.third((*qkv_red.near, d_projected))
+        qkv_red.second((fc1_red.mine, *out_red.sent))
     query_bias_grad = jnp.sum(d_projected[:, :half_width], axis=0, dtype=F32)
     value_bias_grad = jnp.sum(d_projected[:, width:], axis=0, dtype=F32)
     d_normed_one = own_sum(d_projected, lambda v: times_rows(v, qkv_full))
     back_one = jax.vjp(normalize, hidden_f, gain_one, shift_one)[1]
     d_inputs, gain_one_grad, shift_one_grad = back_one(d_normed_one)
     grad_in_own = (d_middle + d_inputs).astype(BF)
+    grad_in = tokens_out(grad_in_own)
 
     def half_slot(value):
         value = value.reshape(shards, 1, -1)
@@ -648,10 +649,9 @@
 
     packed = packed + swap(packed)
     if square:
-        out_part = out_red.third((qkv_red.sent, qkv_red.x_high, qkv_red.y_low))
+        out_part = out_red.third((*qkv_red.sent, grad_in))
         fc2_first = spread_first(after(fc2_part, (qkv_red.sent, out_red.mine)))
-        qkv_part = qkv_red.third(grad_in_own)
-        grad_in = tokens_out(after(grad_in_own, qkv_part))
+        qkv_part = qkv_red.third()
         packed = sum_plane(packed, [0])
         fc1_first = spread_first(after(fc1_part, (fc2_first[1:], qkv_red.mine, packed)))
         fc2_pair = spread_second(*fc2_first)
@@ -665,9 +665,8 @@
         qkv_first = spread_first(after(qkv_part, (out_pair[0], fc1_pair[0], fc2_weight_grad)))
         out_weight_grad = spread_last(*out_pair, None)
         qkv_own, qkv_other = spread_second(*after(qkv_first, (fc1_weight_grad, out_pair[1])))
-        qkv_weight_grad = spread_last(qkv_own, after(qkv_other, (out_weight_grad, grad_in)), qkv_chunk)
+        qkv_weight_grad = spread_last(qkv_own, after(qkv_other, out_weight_grad), qkv_chunk)
     else:
-        grad_in = tokens_out(grad_in_own)
         summed = sum_line(sum_plane(packed, range(chips.bit_length() - 1)))
         fc2_weight_grad = spread_any(sum_any(activated, grad_both), None)
         fc1_weight_grad = spread_any(sum_any(normed_two, d_pre), fc1_chunk)

time: 1340 us -> 1340 us (level)
  starting transfers between devices: 130 us -> 157 us
  waiting for transfers between devices: 508 us -> 484 us
    all_gather x4, waiting for transfers between devices: 159 us -> 60 us  [gather_shards(): return lax.all_gather(piece, 'sh')]
    ppermute x14, starting transfers between devices: 1.98 us -> 56.4 us  [swap(): return lax.ppermute(value, 'co', [(0, 1), (1, 0)])]
    ppermute x4, waiting for transfers between devices: 0.01 us -> 33.7 us  [tokens_in(): lax.ppermute(lax.dynamic_index_in_dim(value, (turn + shard) % 2, 0, False...]
    ppermute x58 -> x50, waiting for transfers between devices: 272 us -> 301 us  [plane(): return lax.ppermute(value, 'ch', [(i, i ^ bit) for i in range(chips)])]
    ppermute x4, waiting for transfers between devices: 60.4 us -> 84.6 us  [tokens_out(): lax.ppermute(lax.dynamic_index_in_dim(value, (turn + micro) % 2, 0, False...]
    ppermute x6, starting transfers between devices: 42.6 us -> 18.6 us  [along(): lax.ppermute(value, 'sh', [(i, (i + hop) % shards) for i in range(shards)])]
    dot_general x32 -> x24, matrix products: 121 us -> 112 us  [cross_rows(): lax.dot_general(left_side, right_side, (((0,), (0,)), ((), ())), preferre...]
    ppermute x58 -> x50, starting transfers between devices: 60.8 us -> 56 us  [plane(): return lax.ppermute(value, 'ch', [(i, i ^ bit) for i in range(chips)])]
  transfers between devices with their start and end apart: 94 -> 86, of which waited for: 30 -> 30; matrix products, arithmetic and copies ran while one was open for 33% -> 32% of each run, Pallas kernels for 13% -> 13%
where the time goes in v4:
time: 1340 us; the launch traced here: 1320 us
  waiting for transfers between devices  484 us (36%)
  matrix products  283 us (21%)
  Pallas kernels  193 us (14%)
  starting transfers between devices  157 us (12%)
  local copies, waits for them, and re-layouts  102 us (8%)
  other arithmetic  88.9 us (7%)
  between operations  16.3 us (1%)
    ppermute x50, waiting for transfers between devices, plane(): return lax.ppermute(value, 'ch', [(i, i ^ bit) for i in range(chips)])  301 us
    pallas_call x8, Pallas kernels, place(): pl.pallas_call(body, grid_spec=pltpu.PrefetchScalarGridSpec(num_scalar_pr...  138 us
    dot_general x24, matrix products, cross_rows(): lax.dot_general(left_side, right_side, (((0,), (0,)), ((), ())), preferre...  112 us
    dot_general x6, matrix products, times_rows(): lax.dot_general(left_side, right_side, (((1,), (1,)), ((), ())), preferre...  89.9 us
    ppermute x4, waiting for transfers between devices, tokens_out(): lax.ppermute(lax.dynamic_index_in_dim(value, (turn + micro) % 2, 0, False...  84.6 us
    dot_general x6, matrix products, dot(): return jnp.dot(left_side, right_side, preferred_element_type=F32)  80.8 us
    all_gather x4, waiting for transfers between devices, gather_shards(): return lax.all_gather(piece, 'sh')  60 us
    ppermute x14, starting transfers between devices, swap(): return lax.ppermute(value, 'co', [(0, 1), (1, 0)])  56.4 us
  transfers between devices with their start and end apart: 86, of which 30 were waited for; matrix products, arithmetic and copies ran while one was open for 32% of the time, Pallas kernels for 13%

profile of v4, /device:TPU:0, one launch (start us, length us, event | category | flops | bytes accessed | tf_op | source)
XLA Modules:
  0.0 1322.9 jit_solution(7902624944031506871)
XLA Ops:
  45.0 60.0 %all-gather.9.cloned.1.call-done = bf16[2048,768]{1,0:T(8,128)(2,1)} async-done(((bf16[512,768]{1,0:T(8,128)(2,1)}), bf16[2048,768]{1,0:T(8,128)(2,1)}) %all-gather.9.cloned.1.call-update) | async-done | bytes 3145744 | tf_op jit(solution)/shard_map/all_gather | solution.py:292
  119.8 33.7 %collective-permute-done.4 = bf16[256,2048]{1,0:T(8,128)(2,1)S(1)} collective-permute-done((bf16[256,2048]{1,0:T(8,128)(2,1)S(1)}, bf16[256,2048]{1,0:T(8,128)(2,1)S(1)}, u32[]{:S(2)}, u32[]{:S(2)}) %collective-permute-start.4) | collective-permute-done | bytes 1048608 | tf_op jit(solution)/shard_map/ppermute | solution.py:272
  157.1 56.1 %collective-permute-start.6 = (bf16[512,2048]{1,0:T(8,128)(2,1)}, bf16[512,2048]{1,0:T(8,128)(2,1)}, u32[]{:S(2)}, u32[]{:S(2)}) collective-permute-start(bf16[512,2048]{1,0:T(8,128)(2,1)} %fusion.14), channel_id=1, source_target_pairs={{0,4},{4,0},{1,5},{5,1},{2,6},{6,2},{3,7},{7,3},{8,12},{12,8},{9,1... | collective-permute-start | bytes 6291464 | tf_op jit(solution)/shard_map/ppermute | solution.py:257
  224.6 40.0 %collective-permute-done.12.refs_3_ = bf16[768,512]{1,0:T(8,128)(2,1)} collective-permute-done((bf16[768,512]{1,0:T(8,128)(2,1)S(1)}, bf16[768,512]{1,0:T(8,128)(2,1)}, u32[]{:S(2)}, u32[]{:S(2)}) %collective-permute-start.12) | collective-permute-done | bytes 786464 | tf_op jit(solution)/shard_map/ppermute | solution.py:254
  267.4 22.5 %shard_map.631 = bf16[2048,3072]{1,0:T(8,128)(2,1)} custom-call(s32[14,32]{1,0:T(8,128)} %get-tuple-element.202.table_ref, bf16[512,3072]{1,0:T(8,128)(2,1)} %get-tuple-element.138.refs_0_, bf16[1536,768]{1,0:T(8,128)(2,1)} %pad_maximum_fusion.26.refs_1_, bf16[1536,768]{1,0:T(8,128)(2,1)} %copy-done.19, bf16[1536,768]{1,0:T(8,128)(2,1)} %copy-done.18, ...), custom_call_target="tpu_custom_call" | custom-call | tf_op jit(solution)/shard_map/pallas_call | solution.py:77
  289.9 18.4 %add_convert_fusion.q_ref.k_ref.v_ref = bf16[1024,3072]{1,0:T(8,128)(2,1)} fusion(bf16[2048,3072]{1,0:T(8,128)(2,1)} %shard_map.631, f32[3072]{0:T(1024)S(1)} %pad_maximum_fusion.42, bf16[512,2048]{1,0:T(8,128)(2,1)} %collective-permute-done.6, bf16[512,2048]{1,0:T(8,128)(2,1)} %fusion.14), kind=kOutput, calls=%fused_computation.10 | convolution fusion | flops 12899581952 | bytes 23080960 | tf_op jit(solution)/shard_map/dot_general | solution.py:30
  316.9 64.6 %collective-permute-done.15.refs_3_ = bf16[1536,1024]{1,0:T(8,128)(2,1)} collective-permute-done((bf16[1536,1024]{1,0:T(8,128)(2,1)}, bf16[1536,1024]{1,0:T(8,128)(2,1)}, u32[]{:S(2)}, u32[]{:S(2)}) %collective-permute-start.15) | collective-permute-done | bytes 3145760 | tf_op jit(solution)/shard_map/ppermute | solution.py:254
  393.0 20.5 %shard_map.632 = bf16[1024,1024]{1,0:T(8,128)(2,1)} custom-call(s32[2]{0:T(128)} %pad_add_fusion.10.scal_ref, bf16[1024,3072]{1,0:T(8,128)(2,1)} %add_convert_fusion.q_ref.k_ref.v_ref, bf16[1024,3072]{1,0:T(8,128)(2,1)} %add_convert_fusion.q_ref.k_ref.v_ref, bf16[1024,3072]{1,0:T(8,128)(2,1)} %add_convert_fusion.q_ref.k_ref.v_ref), custom_call_target="tpu_custom_call" | custom-call | tf_op jit(solution)/shard_map/pallas_call | solution.py:172
  413.5 13.7 %collective-permute-done.18.refs_5_ = bf16[384,512]{1,0:T(8,128)(2,1)S(1)} collective-permute-done((bf16[384,512]{1,0:T(8,128)(2,1)S(1)}, bf16[384,512]{1,0:T(8,128)(2,1)S(1)}, u32[]{:S(2)}, u32[]{:S(2)}) %collective-permute-start.18) | collective-permute-done | bytes 393248 | tf_op jit(solution)/shard_map/ppermute | solution.py:254
  430.3 19.1 %shard_map.633 = bf16[1024,2048]{1,0:T(8,128)(2,1)} custom-call(s32[14,32]{1,0:T(8,128)} %get-tuple-element.201.table_ref, bf16[512,2048]{1,0:T(8,128)(2,1)} %refs_0_.3, bf16[768,512]{1,0:T(8,128)(2,1)} %copy-done.25, bf16[768,512]{1,0:T(8,128)(2,1)} %collective-permute-done.11.refs_2_, bf16[768,512]{1,0:T(8,128)(2,1)} %collective-permute-done.12.refs_3_, ...), custom_call_target="tpu_custom_call" | custom-call | tf_op jit(solution)/shard_map/pallas_call | solution.py:77
  480.3 24.7 %shard_map.634 = bf16[2048,4096]{1,0:T(8,128)(2,1)} custom-call(s32[14,32]{1,0:T(8,128)} %get-tuple-element.200.table_ref, bf16[512,8192]{1,0:T(8,128)(2,1)} %refs_0_.4, bf16[1536,1024]{1,0:T(8,128)(2,1)} %pad_maximum_fusion.19.refs_1_, bf16[1536,1024]{1,0:T(8,128)(2,1)} %collective-permute-done.13.refs_2_, ...), custom_call_target="tpu_custom_call" | custom-call | tf_op jit(solution)/shard_map/pallas_call | solution.py:77
  505.3 25.0 %collective-permute-done.22.refs_3_ = bf16[3072,512]{1,0:T(8,128)(2,1)} collective-permute-done((bf16[3072,512]{1,0:T(8,128)(2,1)}, bf16[3072,512]{1,0:T(8,128)(2,1)}, u32[]{:S(2)}, u32[]{:S(2)}) %collective-permute-start.22) | collective-permute-done | bytes 3145760 | tf_op jit(solution)/shard_map/ppermute | solution.py:254
  540.4 21.8 %multiply_convert_fusion.1 = (bf16[1024,4096]{1,0:T(8,128)(2,1)}, f32[1024,4096]{1,0:T(8,128)}) fusion(f32[4096]{0:T(1024)S(1)} %bitcast.180, bf16[1024,2048]{1,0:T(8,128)(2,1)S(1)} %pad_maximum_fusion.8, bf16[2048,4096]{1,0:T(8,128)(2,1)S(1)} %copy-done.12), kind=kOutput, calls=%fused_computation.8 | convolution fusion | flops 17205035008 | bytes 46153728 | tf_op jit(solution)/shard_map/dot_general | solution.py:30
  572.0 24.7 %shard_map.635 = bf16[4096,2048]{1,0:T(8,128)(2,1)} custom-call(s32[14,32]{1,0:T(8,128)} %get-tuple-element.201.table_ref, bf16[2048,2048]{1,0:T(8,128)(2,1)} %refs_0_.5, bf16[3072,512]{1,0:T(8,128)(2,1)} %pad_maximum_fusion.20.refs_1_, bf16[3072,512]{1,0:T(8,128)(2,1)} %collective-permute-done.21.refs_2_, ...), custom_call_target="tpu_custom_call" | custom-call | tf_op jit(solution)/shard_map/pallas_call | solution.py:77
  617.1 27.7 %convert_reduce_fusion = (f32[4096]{0:T(1024)S(1)}, bf16[1024,4096]{1,0:T(8,128)(2,1)}) fusion(f32[1024,4096]{1,0:T(8,128)} %get-tuple-element.211, f32[4096]{0:T(1024)S(1)} %bitcast.181, bf16[1024,2048]{1,0:T(8,128)(2,1)} %constant_dynamic-update-slice_fusion, bf16[4096,2048]{1,0:T(8,128)(2,1)S(1)} %bitcast.150), kind=kOutput, calls=%fused_computation.6 | convolution fusion | flops 17242779648 | bytes 46170112 | tf_op jit(solution)/shard_map/dot_general | solution.py:38
  657.9 48.5 %collective-permute-done.29 = bf16[2048,1024]{1,0:T(8,128)(2,1)} collective-permute-done((bf16[2048,1024]{1,0:T(8,128)(2,1)}, bf16[2048,1024]{1,0:T(8,128)(2,1)}, u32[]{:S(2)}, u32[]{:S(2)}) %collective-permute-start.29) | collective-permute-done | bytes 4194336 | tf_op jit(solution)/shard_map/ppermute | solution.py:254
  719.6 13.6 %fusion.70 = bf16[512,2048]{1,0:T(8,128)(2,1)} fusion(bf16[2048,4096]{1,0:T(8,128)(2,1)} %shard_map.634, bf16[1024,4096]{1,0:T(8,128)(2,1)S(1)} %bitcast.155), kind=kOutput, calls=%fused_computation.112 | convolution fusion | flops 8590983168 | bytes 23068672 | tf_op jit(solution)/shard_map/dot_general | solution.py:38
  775.4 17.9 %multiply_reduce_fusion = (f32[2048]{0:T(1024)S(1)}, f32[512]{0:T(512)S(1)}, f32[2048]{0:T(1024)S(1)}, f32[512,2048]{1,0:T(8,128)}) fusion(f32[512,2048]{1,0:T(8,128)} %copy-done.4, f32[512]{0:T(512)S(1)} %copy-done.67, f32[512]{0:T(512)S(1)} %copy-done.59, f32[2048]{0:T(1024)S(1)} %bitcast.171, bf16[512,2048]{1,0:T(8,128)(2,1)} %collective-permute-done.35, ...), kind=kOutput, calls=%fused_computation.55 | convolution fusion | flops 8600416256 | bytes 31488000 | tf_op jit(solution)/shard_map/dot_general | solution.py:38
  800.1 15.3 %fusion.67 = bf16[512,2048]{1,0:T(8,128)(2,1)} fusion(bf16[4096,2048]{1,0:T(8,128)(2,1)} %shard_map.635, bf16[1024,4096]{1,0:T(8,128)(2,1)} %get-tuple-element.87), kind=kOutput, calls=%fused_computation.111 | convolution fusion | flops 8590983168 | bytes 23068672 | tf_op jit(solution)/shard_map/dot_general | solution.py:30
  832.2 14.7 %add_add_fusion.2 = bf16[512,2048]{1,0:T(8,128)(2,1)S(1)} fusion(f32[512,2048]{1,0:T(8,128)S(1)} %copy-done.5, bf16[512,2048]{1,0:T(8,128)(2,1)} %collective-permute-done.32, bf16[4096,2048]{1,0:T(8,128)(2,1)} %shard_map.635, bf16[1024,4096]{1,0:T(8,128)(2,1)} %get-tuple-element.87, f32[2048]{0:T(1024)S(1)} %bitcast.184), kind=kOutput, calls=%fused_computation.69 | convolution fusion | flops 8595177472 | bytes 29368320 | tf_op jit(solution)/shard_map/dot_general | solution.py:30
  873.4 34.3 %shard_map.636 = (bf16[1024,1024]{1,0:T(8,128)(2,1)}, bf16[1024,1024]{1,0:T(8,128)(2,1)}, bf16[1024,1024]{1,0:T(8,128)(2,1)}) custom-call(s32[2]{0:T(128)} %pad_add_fusion.10.scal_ref, bf16[1024,3072]{1,0:T(8,128)(2,1)} %add_convert_fusion.q_ref.k_ref.v_ref, bf16[1024,3072]{1,0:T(8,128)(2,1)} %add_convert_fusion.q_ref.k_ref.v_ref, ...), custom_call_target="tpu_custom_call" | custom-call | tf_op jit(solution)/shard_map/pallas_call | solution.py:188
  914.5 33.8 %collective-permute-done.34 = bf16[256,2048]{1,0:T(8,128)(2,1)} collective-permute-done((bf16[256,2048]{1,0:T(8,128)(2,1)}, bf16[256,2048]{1,0:T(8,128)(2,1)}, u32[]{:S(2)}, u32[]{:S(2)}) %collective-permute-start.34) | collective-permute-done | bytes 1048608 | tf_op jit(solution)/shard_map/ppermute | solution.py:281
  974.7 10.7 fusion.52
  1014.3 12.8 fusion.185
  1036.7 9.5 collective-permute-start.40
  1050.3 10.7 collective-permute-done.45
  1070.2 50.8 %collective-permute-done.41 = bf16[256,2048]{1,0:T(8,128)(2,1)} collective-permute-done((bf16[256,2048]{1,0:T(8,128)(2,1)}, bf16[256,2048]{1,0:T(8,128)(2,1)}, u32[]{:S(2)}, u32[]{:S(2)}) %collective-permute-start.41) | collective-permute-done | bytes 1048608 | tf_op jit(solution)/shard_map/ppermute | solution.py:281
  1146.6 19.6 %collective-permute-done.43 = f32[4,6144]{1,0:T(4,128)S(1)} collective-permute-done((f32[4,6144]{1,0:T(4,128)S(1)}, f32[4,6144]{1,0:T(4,128)S(1)}, u32[]{:S(2)}, u32[]{:S(2)}) %collective-permute-start.43) | collective-permute-done | bytes 98336 | tf_op jit(solution)/shard_map/ppermute | solution.py:254
  1175.4 14.9 %collective-permute-done.62 = bf16[512,512]{1,0:T(8,128)(2,1)S(1)} collective-permute-done((bf16[512,512]{1,0:T(8,128)(2,1)S(1)}, bf16[512,512]{1,0:T(8,128)(2,1)S(1)}, u32[]{:S(2)}, u32[]{:S(2)}) %collective-permute-start.62) | collective-permute-done | bytes 524320 | tf_op jit(solution)/shard_map/ppermute | solution.py:254
  1231.9 11.7 shard_map.637
  1245.3 11.7 shard_map.638
  1299.0 16.6 %shard_map.640 = f32[512,6144]{1,0:T(8,128)} custom-call(s32[6,24]{1,0:T(8,128)} %pad_add_fusion.8.table_ref, bf16[2048,768]{1,0:T(8,128)(2,1)} %copy-done.20, bf16[2048,768]{1,0:T(8,128)(2,1)} %collective-permute-done.77.refs_1_), custom_call_target="tpu_custom_call" | custom-call | tf_op jit(solution)/shard_map/pallas_call | solution.py:77
  (589 shorter events, 486.9 us)
Async XLA Ops:
  7.2 97.8 %all-gather.9.cloned.1.call-start = ((), (), s32[]{:S(2)}) async-start(), calls=%async_computation.8 | async-start | bytes 3932160 | tf_op jit(solution)/shard_map/all_gather | solution.py:292
  43.1 178.2 %all-gather.13.cloned.1.call-start = ((), (), s32[]{:S(2)}) async-start(), calls=%async_computation.10 | async-start | bytes 1310720 | tf_op jit(solution)/shard_map/all_gather | solution.py:292
  44.9 263.5 %all-gather.11.cloned.1.call-start = ((), (), s32[]{:S(2)}) async-start(), calls=%async_computation.9 | async-start | bytes 5242880 | tf_op jit(solution)/shard_map/all_gather | solution.py:292
  116.1 339.5 %all-gather.15.cloned.1.call-start = ((), (), s32[]{:S(2)}) async-start(), calls=%async_computation.11 | async-start | bytes 5242880 | tf_op jit(solution)/shard_map/all_gather | solution.py:292
  116.8 96.5 %collective-permute-start.8 = (bf16[1536,768]{1,0:T(8,128)(2,1)}, bf16[1536,768]{1,0:T(8,128)(2,1)S(1)}, u32[]{:S(2)}, u32[]{:S(2)}) collective-permute-start(bf16[1536,768]{1,0:T(8,128)(2,1)} %pad_maximum_fusion.26.refs_1_), channel_id=1, source_target_pairs={{0,16},{8,24},{16,0},{24,8},{1,17},{9,25},{17,1},{25,9},{2,18},{10... | collective-permute-start | bytes 7077896 | tf_op jit(solution)/shard_map/ppermute | solution.py:254
  118.4 98.9 %collective-permute-start.7 = (bf16[1536,768]{1,0:T(8,128)(2,1)}, bf16[1536,768]{1,0:T(8,128)(2,1)S(1)}, u32[]{:S(2)}, u32[]{:S(2)}) collective-permute-start(bf16[1536,768]{1,0:T(8,128)(2,1)} %pad_maximum_fusion.26.refs_1_), channel_id=1, source_target_pairs={{0,8},{8,0},{16,24},{24,16},{1,9},{9,1},{17,25},{25,17},{2,10},{10... | collective-permute-start | bytes 7077896 | tf_op jit(solution)/shard_map/ppermute | solution.py:254
  157.1 132.8 %collective-permute-start.6 = (bf16[512,2048]{1,0:T(8,128)(2,1)}, bf16[512,2048]{1,0:T(8,128)(2,1)}, u32[]{:S(2)}, u32[]{:S(2)}) collective-permute-start(bf16[512,2048]{1,0:T(8,128)(2,1)} %fusion.14), channel_id=1, source_target_pairs={{0,4},{4,0},{1,5},{5,1},{2,6},{6,2},{3,7},{7,3},{8,12},{12,8},{9,1... | collective-permute-start | bytes 6291464 | tf_op jit(solution)/shard_map/ppermute | solution.py:257
  312.4 69.2 %collective-permute-start.15 = (bf16[1536,1024]{1,0:T(8,128)(2,1)}, bf16[1536,1024]{1,0:T(8,128)(2,1)}, u32[]{:S(2)}, u32[]{:S(2)}) collective-permute-start(bf16[1536,1024]{1,0:T(8,128)(2,1)} %pad_maximum_fusion.19.refs_1_), channel_id=1, source_target_pairs={{0,16},{8,24},{16,0},{24,8},{1,17},{9,25},{17,1},{25,9},{2,18},{10... | collective-permute-start | bytes 9437192 | tf_op jit(solution)/shard_map/ppermute | solution.py:254
  313.8 71.0 %collective-permute-start.13 = (bf16[1536,1024]{1,0:T(8,128)(2,1)}, bf16[1536,1024]{1,0:T(8,128)(2,1)}, u32[]{:S(2)}, u32[]{:S(2)}) collective-permute-start(bf16[1536,1024]{1,0:T(8,128)(2,1)} %pad_maximum_fusion.19.refs_1_), channel_id=1, source_target_pairs={{0,8},{8,0},{16,24},{24,16},{1,9},{9,1},{17,25},{25,17},{2,10},{10... | collective-permute-start | bytes 9437192 | tf_op jit(solution)/shard_map/ppermute | solution.py:254
  316.7 824.8 %reduce-scatter.11.cloned.1.call-start = ((), (), s32[]{:S(2)}) async-start(), calls=%async_computation.7 | async-start | bytes 5242880 | tf_op jit(solution)/shard_map/reduce_scatter | solution.py:347
  459.5 70.8 %collective-permute-start.22 = (bf16[3072,512]{1,0:T(8,128)(2,1)}, bf16[3072,512]{1,0:T(8,128)(2,1)}, u32[]{:S(2)}, u32[]{:S(2)}) collective-permute-start(bf16[3072,512]{1,0:T(8,128)(2,1)} %pad_maximum_fusion.20.refs_1_), channel_id=1, source_target_pairs={{0,16},{8,24},{16,0},{24,8},{1,17},{9,25},{17,1},{25,9},{2,18},{10... | collective-permute-start | bytes 9437192 | tf_op jit(solution)/shard_map/ppermute | solution.py:254
  461.0 72.4 %collective-permute-start.21 = (bf16[3072,512]{1,0:T(8,128)(2,1)}, bf16[3072,512]{1,0:T(8,128)(2,1)}, u32[]{:S(2)}, u32[]{:S(2)}) collective-permute-start(bf16[3072,512]{1,0:T(8,128)(2,1)} %pad_maximum_fusion.20.refs_1_), channel_id=1, source_target_pairs={{0,8},{8,0},{16,24},{24,16},{1,9},{9,1},{17,25},{25,17},{2,10},{10... | collective-permute-start | bytes 9437192 | tf_op jit(solution)/shard_map/ppermute | solution.py:254
  469.6 67.9 %collective-permute-start.20 = (bf16[512,2048]{1,0:T(8,128)(2,1)}, bf16[512,2048]{1,0:T(8,128)(2,1)}, u32[]{:S(2)}, u32[]{:S(2)}) collective-permute-start(bf16[512,2048]{1,0:T(8,128)(2,1)} %add_convert_fusion.6), channel_id=1, source_target_pairs={{0,4},{4,0},{1,5},{5,1},{2,6},{6,2},{3,7},{7,3},{8,12},{12,8},{9,1... | collective-permute-start | bytes 6291464 | tf_op jit(solution)/shard_map/ppermute | solution.py:257
  615.1 91.3 %collective-permute-start.29 = (bf16[2048,1024]{1,0:T(8,128)(2,1)}, bf16[2048,1024]{1,0:T(8,128)(2,1)}, u32[]{:S(2)}, u32[]{:S(2)}) collective-permute-start(bf16[2048,1024]{1,0:T(8,128)(2,1)} %convolution_convert_fusion.2), channel_id=1, source_target_pairs={{0,16},{8,24},{16,0},{24,8},{1,17},{9,25},{17,1},{25,9},{2,18},{10... | collective-permute-start | bytes 12582920 | tf_op jit(solution)/shard_map/ppermute | solution.py:254
  616.5 91.0 %collective-permute-start.28 = (bf16[2048,1024]{1,0:T(8,128)(2,1)}, bf16[2048,1024]{1,0:T(8,128)(2,1)}, u32[]{:S(2)}, u32[]{:S(2)}) collective-permute-start(bf16[2048,1024]{1,0:T(8,128)(2,1)} %convolution_convert_fusion.3), channel_id=1, source_target_pairs={{0,8},{8,0},{16,24},{24,16},{1,9},{9,1},{17,25},{25,17},{2,10},{10... | collective-permute-start | bytes 12582920 | tf_op jit(solution)/shard_map/ppermute | solution.py:254
  748.4 109.3 %collective-permute-start.37 = (bf16[1024,2048]{1,0:T(8,128)(2,1)}, bf16[1024,2048]{1,0:T(8,128)(2,1)}, u32[]{:S(2)}, u32[]{:S(2)}) collective-permute-start(bf16[1024,2048]{1,0:T(8,128)(2,1)} %fusion.29), channel_id=1, source_target_pairs={{0,8},{8,0},{16,24},{24,16},{1,9},{9,1},{17,25},{25,17},{2,10},{10... | collective-permute-start | bytes 12582920 | tf_op jit(solution)/shard_map/ppermute | solution.py:254
  750.0 107.8 %collective-permute-start.38 = (bf16[1024,2048]{1,0:T(8,128)(2,1)}, bf16[1024,2048]{1,0:T(8,128)(2,1)}, u32[]{:S(2)}, u32[]{:S(2)}) collective-permute-start(bf16[1024,2048]{1,0:T(8,128)(2,1)} %fusion.28), channel_id=1, source_target_pairs={{0,16},{8,24},{16,0},{24,8},{1,17},{9,25},{17,1},{25,9},{2,18},{10... | collective-permute-start | bytes 12582920 | tf_op jit(solution)/shard_map/ppermute | solution.py:254
  826.0 340.3 %reduce-scatter.9.cloned.1.call-start = ((), (), s32[]{:S(2)}) async-start(), calls=%async_computation.6 | async-start | bytes 5242880 | tf_op jit(solution)/shard_map/reduce_scatter | solution.py:347
  831.6 158.2 %collective-permute-start.49 = (bf16[512,1024]{1,0:T(8,128)(2,1)}, bf16[512,1024]{1,0:T(8,128)(2,1)}, u32[]{:S(2)}, u32[]{:S(2)}) collective-permute-start(bf16[512,1024]{1,0:T(8,128)(2,1)} %fusion.105), channel_id=1, source_target_pairs={{0,8},{8,0},{16,24},{24,16},{1,9},{9,1},{17,25},{25,17},{2,10},{10... | collective-permute-start | bytes 3145736 | tf_op jit(solution)/shard_map/ppermute | solution.py:254
  848.5 65.2 %collective-permute-start.33 = (bf16[256,2048]{1,0:T(8,128)(2,1)}, bf16[256,2048]{1,0:T(8,128)(2,1)S(1)}, u32[]{:S(2)}, u32[]{:S(2)}) collective-permute-start(bf16[256,2048]{1,0:T(8,128)(2,1)} %get-tuple-element.165), channel_id=1, source_target_pairs={{0,0},{2,1},{4,2},{6,3},{1,4},{3,5},{5,6},{7,7},{8,8},{10,9},{12,1... | collective-permute-start | bytes 3145736 | tf_op jit(solution)/shard_map/ppermute | solution.py:281
  850.5 97.8 %collective-permute-start.34 = (bf16[256,2048]{1,0:T(8,128)(2,1)}, bf16[256,2048]{1,0:T(8,128)(2,1)}, u32[]{:S(2)}, u32[]{:S(2)}) collective-permute-start(bf16[256,2048]{1,0:T(8,128)(2,1)} %get-tuple-element.166), channel_id=1, source_target_pairs={{2,0},{0,1},{6,2},{4,3},{3,4},{1,5},{7,6},{5,7},{10,8},{8,9},{14,1... | collective-permute-start | bytes 3145736 | tf_op jit(solution)/shard_map/ppermute | solution.py:281
  860.9 131.8 %collective-permute-start.48 = (bf16[1024,1024]{1,0:T(8,128)(2,1)}, bf16[1024,1024]{1,0:T(8,128)(2,1)}, u32[]{:S(2)}, u32[]{:S(2)}) collective-permute-start(bf16[1024,1024]{1,0:T(8,128)(2,1)} %slice_add_fusion), channel_id=1, source_target_pairs={{0,16},{8,24},{16,0},{24,8},{1,17},{9,25},{17,1},{25,9},{2,18},{10... | collective-permute-start | bytes 6291464 | tf_op jit(solution)/shard_map/ppermute | solution.py:254
  865.5 127.1 %collective-permute-start.47 = (bf16[1024,1024]{1,0:T(8,128)(2,1)}, bf16[1024,1024]{1,0:T(8,128)(2,1)}, u32[]{:S(2)}, u32[]{:S(2)}) collective-permute-start(bf16[1024,1024]{1,0:T(8,128)(2,1)} %slice_add_fusion.1), channel_id=1, source_target_pairs={{0,8},{8,0},{16,24},{24,16},{1,9},{9,1},{17,25},{25,17},{2,10},{10... | collective-permute-start | bytes 6291464 | tf_op jit(solution)/shard_map/ppermute | solution.py:254
  913.7 77.6 %collective-permute-start.50 = (bf16[512,1024]{1,0:T(8,128)(2,1)S(1)}, bf16[512,1024]{1,0:T(8,128)(2,1)S(1)}, u32[]{:S(2)}, u32[]{:S(2)}) collective-permute-start(bf16[512,1024]{1,0:T(8,128)(2,1)S(1)} %fusion.104), channel_id=1, source_target_pairs={{0,16},{8,24},{16,0},{24,8},{1,17},{9,25},{17,1},{25,9},{2,18},{10... | collective-permute-start | bytes 3145736 | tf_op jit(solution)/shard_map/ppermute | solution.py:254
  989.7 71.3 %collective-permute-start.45 = (bf16[1024,1536]{1,0:T(8,128)(2,1)}, bf16[1024,1536]{1,0:T(8,128)(2,1)}, u32[]{:S(2)}, u32[]{:S(2)}) collective-permute-start(bf16[1024,1536]{1,0:T(8,128)(2,1)} %convolution_convert_fusion.1), channel_id=1, source_target_pairs={{0,8},{8,0},{16,24},{24,16},{1,9},{9,1},{17,25},{25,17},{2,10},{10... | collective-permute-start | bytes 9437192 | tf_op jit(solution)/shard_map/ppermute | solution.py:254
  991.2 71.3 %collective-permute-start.46 = (bf16[1024,1536]{1,0:T(8,128)(2,1)}, bf16[1024,1536]{1,0:T(8,128)(2,1)}, u32[]{:S(2)}, u32[]{:S(2)}) collective-permute-start(bf16[1024,1536]{1,0:T(8,128)(2,1)} %convolution_convert_fusion), channel_id=1, source_target_pairs={{0,16},{8,24},{16,0},{24,8},{1,17},{9,25},{17,1},{25,9},{2,18},{10... | collective-permute-start | bytes 9437192 | tf_op jit(solution)/shard_map/ppermute | solution.py:254
  1002.6 213.4 %reduce-scatter.7.cloned.1.call-start = ((), (), s32[]{:S(2)}) async-start(), calls=%async_computation.5 | async-start | bytes 1310720 | tf_op jit(solution)/shard_map/reduce_scatter | solution.py:347
  1007.4 116.8 %collective-permute-start.56 = (bf16[512,512]{1,0:T(8,128)(2,1)}, bf16[512,512]{1,0:T(8,128)(2,1)}, u32[]{:S(2)}, u32[]{:S(2)}) collective-permute-start(bf16[512,512]{1,0:T(8,128)(2,1)} %fusion.116), channel_id=1, source_target_pairs={{0,8},{8,0},{16,24},{24,16},{1,9},{9,1},{17,25},{25,17},{2,10},{10... | collective-permute-start | bytes 1572872 | tf_op jit(solution)/shard_map/ppermute | solution.py:254
  1046.2 74.8 %collective-permute-start.41 = (bf16[256,2048]{1,0:T(8,128)(2,1)}, bf16[256,2048]{1,0:T(8,128)(2,1)}, u32[]{:S(2)}, u32[]{:S(2)}) collective-permute-start(bf16[256,2048]{1,0:T(8,128)(2,1)} %get-tuple-element.162), channel_id=1, source_target_pairs={{2,0},{0,1},{6,2},{4,3},{3,4},{1,5},{7,6},{5,7},{10,8},{8,9},{14,1... | collective-permute-start | bytes 3145736 | tf_op jit(solution)/shard_map/ppermute | solution.py:281
  1065.3 69.6 %collective-permute-start.52 = (bf16[1024,768]{1,0:T(8,128)(2,1)}, bf16[1024,768]{1,0:T(8,128)(2,1)S(1)}, u32[]{:S(2)}, u32[]{:S(2)}) collective-permute-start(bf16[1024,768]{1,0:T(8,128)(2,1)} %slice_add_fusion.4), channel_id=1, source_target_pairs={{0,16},{8,24},{16,0},{24,8},{1,17},{9,25},{17,1},{25,9},{2,18},{10... | collective-permute-start | bytes 4718600 | tf_op jit(solution)/shard_map/ppermute | solution.py:254
  1068.7 66.2 %collective-permute-start.51 = (bf16[1024,768]{1,0:T(8,128)(2,1)}, bf16[1024,768]{1,0:T(8,128)(2,1)}, u32[]{:S(2)}, u32[]{:S(2)}) collective-permute-start(bf16[1024,768]{1,0:T(8,128)(2,1)} %slice_add_fusion.5), channel_id=1, source_target_pairs={{0,8},{8,0},{16,24},{24,16},{1,9},{9,1},{17,25},{25,17},{2,10},{10... | collective-permute-start | bytes 4718600 | tf_op jit(solution)/shard_map/ppermute | solution.py:254
  1129.4 114.3 %reduce-scatter.5.cloned.1.call-start = ((), (), s32[]{:S(2)}) async-start(), calls=%async_computation.4 | async-start | bytes 3932160 | tf_op jit(solution)/shard_map/reduce_scatter | solution.py:347
  (152 other events, 3914.1 us)
Sparse Core Ops, SparseCore 0:
  43.2 61.7 all-gather.8
  107.2 44.1 all-gather.12
  153.0 90.0 all-gather.10
  316.8 80.6 all-gather.14
  826.1 110.9 reduce-scatter.10
  1002.7 100.8 reduce-scatter.8
  1129.5 25.7 reduce-scatter.6
  1158.2 58.9 reduce-scatter.4

commit v5 on v4

--- a/solution.py
+++ b/solution.py
@@ -267,11 +267,12 @@
                     pairs.append(((c * CORES + o) * shards + s, (c * CORES + slot % 2) * shards + z))
         return pairs
 
-    def tokens_in(value):
+    def tokens_in(value, barrier=()):
         got = [
             lax.ppermute(lax.dynamic_index_in_dim(value, (turn + shard) % 2, 0, False), ALL, token_pairs(turn))
             for turn in (0, 1)
         ]
+        got = lax.optimization_barrier((*got, *barrier))
         even = micro % 2 == 0
         return jnp.concatenate([jnp.where(even, got[0], got[1]), jnp.where(even, got[1], got[0])])
 
@@ -296,9 +297,10 @@
             [lax.dynamic_index_in_dim(held, (shard - hop) % shards, 0, False) for hop in range(1, shards)]
         )
 
-    def spread_others(others):
+    def spread_others(others, barrier=()):
         from_x = plane(others, 1)
         from_y = plane(others, 2)
+        from_x, from_y, *_ = lax.optimization_barrier((from_x, from_y, *barrier))
         tall = (shards - 1, 2, others.shape[0] // (2 * (shards - 1)), others.shape[1])
         low_cut = from_x.reshape(tall)[:, 0].reshape(-1, tall[3])
         high_cut = from_y.reshape(tall)[:, 1].reshape(-1, tall[3])
@@ -421,7 +423,7 @@
     square = chips == 4
     small = jnp.concatenate(vectors)
     ring = [small] + [along(small, hop) for hop in range(shards - 1, 0, -1)]
-    qkv_piece, *ring = lax.optimization_barrier((qkv_piece, *ring))
+    qkv_piece, tokens, *ring = lax.optimization_barrier((qkv_piece, tokens_in(hidden_in), *ring))
     gathered = lax.dynamic_slice_in_dim(jnp.stack(ring + ring), (shards - shard) % shards, shards, 0)
     vec = [gathered[:, edges[i] : edges[i + 1]].astype(F32) for i in range(len(vectors))]
     gain_one, shift_one, _, _, bias_out, gain_two, shift_two, bias_down, _ = [v.reshape(-1) for v in vec]
@@ -432,10 +434,8 @@
     prefix_pair = [jnp.where(core == 0, a, b) for a, b in ((prefix, swap(prefix)), (swap(prefix), prefix))]
     prefix_len = jnp.concatenate(prefix_pair, axis=1).reshape(-1)[sequence]
 
-    tokens_from = hidden_in
     if square:
         qkv_others = others_of(gather_shards(qkv_piece))
-        tokens_from = after(hidden_in, qkv_others)
         out_got = gather_shards(out_piece)
         fc1_got = gather_shards(fc1_piece)
         fc2_got = gather_shards(after(fc2_piece, out_got))
@@ -444,7 +444,6 @@
         out_others = others_of(after(out_got, (qkv_low, qkv_high)))
         out_x, out_y, out_low, out_high = spread_others(out_others)
 
-    tokens = lax.optimization_barrier(tokens_in(tokens_from))
     hidden_f = tokens.astype(F32)
     normed_own = normalize(hidden_f, gain_one, shift_one).astype(BF)
     normed_one = jnp.concatenate([normed_own, swap(normed_own)])
@@ -468,7 +467,32 @@
     projected = projected.astype(BF)
     if square:
         fc1_others = others_of(after(fc1_got, (projected, out_low, out_high)))
-        fc1_x, fc1_y, fc1_low, fc1_high = spread_others(fc1_others)
+    scalars = jnp.stack([core.astype(jnp.int32), prefix_len.astype(jnp.int32)])
+    if parts == 1:
+        context = attend_forward(projected, scalars)
+    else:
+        part = shard % parts
+
+        def to_part(value, hop):
+            pairs = [(i, i // parts * parts + (i % parts + hop) % parts) for i in range(shards)]
+            return lax.ppermute(value, "sh", pairs)
+
+        def positions(which):
+            at = jnp.arange(rows)
+            return which * CORES * rows + jnp.concatenate([core * rows + at, (1 - core) * rows + at])
+
+        q_four = projected[:, :half_width].reshape(CORES * rows, -1, HEAD_DIM)
+        both = projected[:, half_width:]
+        held = jnp.concatenate([both] + [to_part(both, hop) for hop in range(1, parts)])
+        k_four = held[:, :half_width].reshape(held.shape[0], -1, HEAD_DIM)
+        v_four = held[:, half_width:].reshape(held.shape[0], -1, HEAD_DIM)
+        k_pos = jnp.concatenate([positions((part - hop) % parts) for hop in range(parts)])
+        soft_full = spread_softmax(q_four, k_four, positions(part), k_pos, prefix_len)
+        context = jnp.einsum("hqk,khd->qhd", soft_full.astype(BF), v_four, preferred_element_type=F32)
+        context = context.reshape(CORES * rows, half_width).astype(BF)
+
+    if square:
+        fc1_x, fc1_y, fc1_low, fc1_high = spread_others(fc1_others, (context,))
         fc1_ends = plane(fc1_low, 2), plane(fc1_high, 1)
         fc2_others = others_of(after(fc2_got, fc1_ends))
         fc2_x, fc2_y, fc2_low, fc2_high = spread_others(fc2_others)
@@ -488,43 +512,17 @@
         )
         grads_mine = tokens_in(after(grad_out, fc2_others))
     grads_mine = lax.optimization_barrier(grads_mine)
-    scalars = jnp.stack([core.astype(jnp.int32), prefix_len.astype(jnp.int32)])
-    if parts == 1:
-        context = attend_forward(projected, scalars)
-    else:
-        part = shard % parts
-
-        def to_part(value, hop):
-            pairs = [(i, i // parts * parts + (i % parts + hop) % parts) for i in range(shards)]
-            return lax.ppermute(value, "sh", pairs)
-
-        def positions(which):
-            at = jnp.arange(rows)
-            return which * CORES * rows + jnp.concatenate([core * rows + at, (1 - core) * rows + at])
-
-        q_four = projected[:, :half_width].reshape(CORES * rows, -1, HEAD_DIM)
-        both = projected[:, half_width:]
-        held = jnp.concatenate([both] + [to_part(both, hop) for hop in range(1, parts)])
-        k_four = held[:, :half_width].reshape(held.shape[0], -1, HEAD_DIM)
-        v_four = held[:, half_width:].reshape(held.shape[0], -1, HEAD_DIM)
-        k_pos = jnp.concatenate([positions((part - hop) % parts) for hop in range(parts)])
-        soft_full = spread_softmax(q_four, k_four, positions(part), k_pos, prefix_len)
-        context = jnp.einsum("hqk,khd->qhd", soft_full.astype(BF), v_four, preferred_element_type=F32)
-        context = context.reshape(CORES * rows, half_width).astype(BF)
-
-    if square:
-        context = after(context, fc1_ends)
 
     def own_sum(left_side, product):
         away = swap(product(left_side[rows:]).astype(BF))
         return product(left_side[:rows]) + away.astype(F32)
 
     middle = hidden_f + (own_sum(context, lambda v: dot(v, out_full)) + bias_out)
+    if square:
+        middle = after(middle, (fc1_low, fc1_high, fc2_got))
     normed_two_own = normalize(middle, gain_two, shift_two).astype(BF)
     normed_two = jnp.concatenate([normed_two_own, swap(normed_two_own)])
     grads_mine = after(grads_mine, normed_two)
-    if square:
-        normed_two = after(normed_two, (fc2_low, fc2_high))
     pre_act = dot(normed_two, fc1_full) + bias_up
     below = 0.5 * (1.0 + lax.erf(pre_act * math.sqrt(0.5)))
     density = jnp.exp(-0.5 * pre_act * pre_act) * (1.0 / math.sqrt(2.0 * math.pi))
@@ -600,7 +598,7 @@
     d_projected = jnp.concatenate([d_queries, d_keys, d_values], axis=1)
     if square:
         fc2_part = fc2_red.third()
-        d_projected = after(d_projected, (fc2_red.mine, result))
+        d_projected = after(d_projected, fc2_red.mine)
         qkv_red = Reduction(normed_one, d_projected)
         out_red.second()
         d_projected = after(d_projected, qkv_red.near)
@@ -649,11 +647,11 @@
 
     packed = packed + swap(packed)
     if square:
-        out_part = out_red.third((*qkv_red.sent, grad_in))
+        out_part = out_red.third((*qkv_red.sent, result))
         fc2_first = spread_first(after(fc2_part, (qkv_red.sent, out_red.mine)))
         qkv_part = qkv_red.third()
         packed = sum_plane(packed, [0])
-        fc1_first = spread_first(after(fc1_part, (fc2_first[1:], qkv_red.mine, packed)))
+        fc1_first = spread_first(after(fc1_part, (fc2_first[1:], qkv_red.mine, packed, grad_in)))
         fc2_pair = spread_second(*fc2_first)
         packed = sum_plane(packed, [1])
         out_first = spread_first(after(out_part, (fc1_first[1:], fc2_pair[0], packed)))

time: 1340 us -> 1270 us (0.948)
  starting transfers between devices: 157 us -> 99.1 us
  matrix products: 283 us -> 297 us
    ppermute x14, starting transfers between devices: 56.4 us -> 18 us  [swap(): return lax.ppermute(value, 'co', [(0, 1), (1, 0)])]
    ppermute x4, waiting for transfers between devices: 84.6 us -> 51.1 us  [tokens_out(): lax.ppermute(lax.dynamic_index_in_dim(value, (turn + micro) % 2, 0, False...]
    ppermute x50, waiting for transfers between devices: 301 us -> 332 us  [plane(): return lax.ppermute(value, 'ch', [(i, i ^ bit) for i in range(chips)])]
    ppermute x4, waiting for transfers between devices: 33.7 us -> 4.9 us  [tokens_in(): lax.ppermute(lax.dynamic_index_in_dim(value, (turn + shard) % 2, 0, False...]
    all_gather x4, waiting for transfers between devices: 60 us -> 80.2 us  [gather_shards(): return lax.all_gather(piece, 'sh')]
    unnamed x250 -> x230, local copies, waits for them, and re-layouts: 50.8 us -> 42.5 us
  transfers between devices with their start and end apart: 86 -> 86, of which waited for: 30 -> 34; matrix products, arithmetic and copies ran while one was open for 32% -> 36% of each run, Pallas kernels for 13% -> 14%
where the time goes in v5:
time: 1270 us; the launch traced here: 1260 us
  waiting for transfers between devices  473 us (37%)
  matrix products  297 us (23%)
  Pallas kernels  194 us (15%)
  starting transfers between devices  99.1 us (8%)
  local copies, waits for them, and re-layouts  91.2 us (7%)
  other arithmetic  89.5 us (7%)
  between operations  16.5 us (1%)
    ppermute x50, waiting for transfers between devices, plane(): return lax.ppermute(value, 'ch', [(i, i ^ bit) for i in range(chips)])  332 us
    pallas_call x8, Pallas kernels, place(): pl.pallas_call(body, grid_spec=pltpu.PrefetchScalarGridSpec(num_scalar_pr...  139 us
    dot_general x24, matrix products, cross_rows(): lax.dot_general(left_side, right_side, (((0,), (0,)), ((), ())), preferre...  123 us
    dot_general x6, matrix products, times_rows(): lax.dot_general(left_side, right_side, (((1,), (1,)), ((), ())), preferre...  92.9 us
    dot_general x6, matrix products, dot(): return jnp.dot(left_side, right_side, preferred_element_type=F32)  81.5 us
    all_gather x4, waiting for transfers between devices, gather_shards(): return lax.all_gather(piece, 'sh')  80.2 us
    ppermute x50, starting transfers between devices, plane(): return lax.ppermute(value, 'ch', [(i, i ^ bit) for i in range(chips)])  54.7 us
    ppermute x4, waiting for transfers between devices, tokens_out(): lax.ppermute(lax.dynamic_index_in_dim(value, (turn + micro) % 2, 0, False...  51.1 us
  transfers between devices with their start and end apart: 86, of which 34 were waited for; matrix products, arithmetic and copies ran while one was open for 36% of the time, Pallas kernels for 14%

profile of v5, /device:TPU:0, one launch (start us, length us, event | category | flops | bytes accessed | tf_op | source)
XLA Modules:
  0.0 1260.2 jit_solution(6615489123056235856)
XLA Ops:
  56.3 80.2 %all-gather.9.cloned.1.call-done = bf16[2048,768]{1,0:T(8,128)(2,1)} async-done(((bf16[512,768]{1,0:T(8,128)(2,1)}), bf16[2048,768]{1,0:T(8,128)(2,1)}) %all-gather.9.cloned.1.call-update) | async-done | bytes 3145744 | tf_op jit(solution)/shard_map/all_gather | solution.py:293
  146.5 46.4 %collective-permute-done.8.refs_3_ = bf16[1536,768]{1,0:T(8,128)(2,1)} collective-permute-done((bf16[1536,768]{1,0:T(8,128)(2,1)}, bf16[1536,768]{1,0:T(8,128)(2,1)}, u32[]{:S(2)}, u32[]{:S(2)}) %collective-permute-start.8) | collective-permute-done | bytes 2359328 | tf_op jit(solution)/shard_map/ppermute | solution.py:254
  207.8 34.8 %collective-permute-done.12.refs_3_ = bf16[768,512]{1,0:T(8,128)(2,1)} collective-permute-done((bf16[768,512]{1,0:T(8,128)(2,1)S(1)}, bf16[768,512]{1,0:T(8,128)(2,1)}, u32[]{:S(2)}, u32[]{:S(2)}) %collective-permute-start.12) | collective-permute-done | bytes 786464 | tf_op jit(solution)/shard_map/ppermute | solution.py:254
  245.7 22.7 %shard_map.631 = bf16[2048,3072]{1,0:T(8,128)(2,1)} custom-call(s32[14,32]{1,0:T(8,128)} %get-tuple-element.224.table_ref, bf16[512,3072]{1,0:T(8,128)(2,1)} %get-tuple-element.160.refs_0_, bf16[1536,768]{1,0:T(8,128)(2,1)} %pad_maximum_fusion.26.refs_1_, bf16[1536,768]{1,0:T(8,128)(2,1)} %collective-permute-done.7.refs_2_, ...), custom_call_target="tpu_custom_call" | custom-call | tf_op jit(solution)/shard_map/pallas_call | solution.py:77
  268.4 18.5 %add_convert_fusion.q_ref.k_ref.v_ref = bf16[1024,3072]{1,0:T(8,128)(2,1)} fusion(bf16[2048,3072]{1,0:T(8,128)(2,1)} %shard_map.631, f32[3072]{0:T(1024)S(1)} %pad_maximum_fusion.42, bf16[512,2048]{1,0:T(8,128)(2,1)} %collective-permute-done.6, bf16[512,2048]{1,0:T(8,128)(2,1)} %fusion.14), kind=kOutput, calls=%fused_computation.10 | convolution fusion | flops 12899581952 | bytes 23080960 | tf_op jit(solution)/shard_map/dot_general | solution.py:30
  297.2 20.4 %shard_map.632 = bf16[1024,1024]{1,0:T(8,128)(2,1)} custom-call(s32[2]{0:T(128)} %pad_add_fusion.10.scal_ref, bf16[1024,3072]{1,0:T(8,128)(2,1)} %add_convert_fusion.q_ref.k_ref.v_ref, bf16[1024,3072]{1,0:T(8,128)(2,1)} %add_convert_fusion.q_ref.k_ref.v_ref, bf16[1024,3072]{1,0:T(8,128)(2,1)} %add_convert_fusion.q_ref.k_ref.v_ref), custom_call_target="tpu_custom_call" | custom-call | tf_op jit(solution)/shard_map/pallas_call | solution.py:172
  317.6 49.4 %collective-permute-done.13.refs_4_ = bf16[384,512]{1,0:T(8,128)(2,1)S(1)} collective-permute-done((bf16[384,512]{1,0:T(8,128)(2,1)S(1)}, bf16[384,512]{1,0:T(8,128)(2,1)S(1)}, u32[]{:S(2)}, u32[]{:S(2)}) %collective-permute-start.13) | collective-permute-done | bytes 393248 | tf_op jit(solution)/shard_map/ppermute | solution.py:254
  368.3 19.3 %shard_map.633 = bf16[1024,2048]{1,0:T(8,128)(2,1)} custom-call(s32[14,32]{1,0:T(8,128)} %get-tuple-element.223.table_ref, bf16[512,2048]{1,0:T(8,128)(2,1)} %refs_0_.3, bf16[768,512]{1,0:T(8,128)(2,1)} %copy-done.19, bf16[768,512]{1,0:T(8,128)(2,1)} %collective-permute-done.11.refs_2_, bf16[768,512]{1,0:T(8,128)(2,1)} %collective-permute-done.12.refs_3_, ...), custom_call_target="tpu_custom_call" | custom-call | tf_op jit(solution)/shard_map/pallas_call | solution.py:77
  413.2 21.9 %collective-permute-done.19.refs_4_ = bf16[768,1024]{1,0:T(8,128)(2,1)} collective-permute-done((bf16[768,1024]{1,0:T(8,128)(2,1)}, bf16[768,1024]{1,0:T(8,128)(2,1)}, u32[]{:S(2)}, u32[]{:S(2)}) %collective-permute-start.19) | collective-permute-done | bytes 1572896 | tf_op jit(solution)/shard_map/ppermute | solution.py:254
  446.4 25.1 %shard_map.634 = bf16[2048,4096]{1,0:T(8,128)(2,1)} custom-call(s32[14,32]{1,0:T(8,128)} %get-tuple-element.222.table_ref, bf16[512,8192]{1,0:T(8,128)(2,1)} %refs_0_.4, bf16[1536,1024]{1,0:T(8,128)(2,1)} %pad_maximum_fusion.19.refs_1_, bf16[1536,1024]{1,0:T(8,128)(2,1)} %collective-permute-done.16.refs_2_, ...), custom_call_target="tpu_custom_call" | custom-call | tf_op jit(solution)/shard_map/pallas_call | solution.py:77
  471.8 15.4 %collective-permute-start.23 = (bf16[512,2048]{1,0:T(8,128)(2,1)S(1)}, bf16[512,2048]{1,0:T(8,128)(2,1)}, u32[]{:S(2)}, u32[]{:S(2)}) collective-permute-start(bf16[512,2048]{1,0:T(8,128)(2,1)S(1)} %pad_maximum_fusion.32), channel_id=1, source_target_pairs={{0,4},{4,0},{1,5},{5,1},{2,6},{6,2},{3,7},{7,3},{8,12},{12,8},{9,1... | collective-permute-start | bytes 6291464 | tf_op jit(solution)/shard_map/ppermute | solution.py:257
  487.2 27.7 %multiply_convert_fusion.1 = (bf16[1024,4096]{1,0:T(8,128)(2,1)}, f32[1024,4096]{1,0:T(8,128)}) fusion(f32[4096]{0:T(1024)S(1)} %bitcast.178, bf16[2048,4096]{1,0:T(8,128)(2,1)} %shard_map.634, bf16[512,2048]{1,0:T(8,128)(2,1)} %collective-permute-done.18, bf16[512,2048]{1,0:T(8,128)(2,1)} %add_convert_fusion.6), kind=kOutput, calls=%fused_computation.8 | convolution fusion | flops 17213423616 | bytes 46153728 | tf_op jit(solution)/shard_map/dot_general | solution.py:30
  545.4 10.5 collective-permute-done.26.refs_4_
  556.9 24.7 %shard_map.635 = bf16[4096,2048]{1,0:T(8,128)(2,1)} custom-call(s32[14,32]{1,0:T(8,128)} %get-tuple-element.223.table_ref, bf16[2048,2048]{1,0:T(8,128)(2,1)} %refs_0_.5, bf16[3072,512]{1,0:T(8,128)(2,1)} %pad_maximum_fusion.20.refs_1_, bf16[3072,512]{1,0:T(8,128)(2,1)} %collective-permute-done.24.refs_2_, ...), custom_call_target="tpu_custom_call" | custom-call | tf_op jit(solution)/shard_map/pallas_call | solution.py:77
  581.5 29.5 %convert_reduce_fusion = (f32[4096]{0:T(1024)S(1)}, bf16[1024,4096]{1,0:T(8,128)(2,1)}) fusion(f32[1024,4096]{1,0:T(8,128)} %get-tuple-element.231, f32[4096]{0:T(1024)S(1)} %bitcast.179, bf16[1024,2048]{1,0:T(8,128)(2,1)} %copy-done.14, bf16[4096,2048]{1,0:T(8,128)(2,1)} %shard_map.635), kind=kOutput, calls=%fused_computation.6 | convolution fusion | flops 17242779648 | bytes 46170112 | tf_op jit(solution)/shard_map/dot_general | solution.py:38
  611.7 33.9 %collective-permute-done.29 = bf16[2048,1024]{1,0:T(8,128)(2,1)} collective-permute-done((bf16[2048,1024]{1,0:T(8,128)(2,1)}, bf16[2048,1024]{1,0:T(8,128)(2,1)}, u32[]{:S(2)}, u32[]{:S(2)}) %collective-permute-start.29) | collective-permute-done | bytes 4194336 | tf_op jit(solution)/shard_map/ppermute | solution.py:254
  661.7 13.5 %fusion.70 = bf16[512,2048]{1,0:T(8,128)(2,1)} fusion(bf16[2048,4096]{1,0:T(8,128)(2,1)} %shard_map.634, bf16[1024,4096]{1,0:T(8,128)(2,1)S(1)} %bitcast.152), kind=kOutput, calls=%fused_computation.116 | convolution fusion | flops 8590983168 | bytes 23068672 | tf_op jit(solution)/shard_map/dot_general | solution.py:38
  704.3 17.7 %multiply_reduce_fusion = (f32[2048]{0:T(1024)S(1)}, f32[512]{0:T(512)S(1)}, f32[2048]{0:T(1024)S(1)}, f32[512,2048]{1,0:T(8,128)}) fusion(f32[512,2048]{1,0:T(8,128)} %convert_add_fusion, f32[512]{0:T(512)S(1)} %copy-done.56, f32[512]{0:T(512)S(1)} %copy-done.48, f32[2048]{0:T(1024)S(1)} %bitcast.169, bf16[512,2048]{1,0:T(8,128)(2,1)} %collective-permute-done.35, ...), kind=kOutput, calls=%fused_computation.59 | convolution fusion | flops 8600416256 | bytes 31488000 | tf_op jit(solution)/shard_map/dot_general | solution.py:38
  742.7 11.7 fusion.67
  774.9 14.1 %add_add_fusion.2 = bf16[512,2048]{1,0:T(8,128)(2,1)S(1)} fusion(f32[512,2048]{1,0:T(8,128)S(1)} %copy-done.3, bf16[512,2048]{1,0:T(8,128)(2,1)} %collective-permute-done.32, bf16[4096,2048]{1,0:T(8,128)(2,1)} %shard_map.635, bf16[1024,4096]{1,0:T(8,128)(2,1)} %get-tuple-element.109, f32[2048]{0:T(1024)S(1)} %bitcast.182), kind=kOutput, calls=%fused_computation.73 | convolution fusion | flops 8595177472 | bytes 29368320 | tf_op jit(solution)/shard_map/dot_general | solution.py:30
  811.9 34.3 %shard_map.636 = (bf16[1024,1024]{1,0:T(8,128)(2,1)}, bf16[1024,1024]{1,0:T(8,128)(2,1)}, bf16[1024,1024]{1,0:T(8,128)(2,1)}) custom-call(s32[2]{0:T(128)} %pad_add_fusion.10.scal_ref, bf16[1024,3072]{1,0:T(8,128)(2,1)} %add_convert_fusion.q_ref.k_ref.v_ref, bf16[1024,3072]{1,0:T(8,128)(2,1)} %add_convert_fusion.q_ref.k_ref.v_ref, ...), custom_call_target="tpu_custom_call" | custom-call | tf_op jit(solution)/shard_map/pallas_call | solution.py:188
  875.8 11.7 fusion.52
  924.3 12.8 %fusion.192 = (f32[2048]{0:T(1024)S(1)}, f32[512]{0:T(512)S(1)}, f32[512,2048]{1,0:T(8,128)}) fusion(f32[2048]{0:T(1024)S(1)} %bitcast.163, f32[512]{0:T(512)S(1)} %copy-done.44, bf16[512,2048]{1,0:T(8,128)(2,1)S(1)} %copy-done.1, bf16[512,2048]{1,0:T(8,128)(2,1)} %collective-permute-done.39, bf16[2048,3072]{1,0:T(8,128)(2,1)} %shard_map.631, ...), kind=kOutput, calls=%fused_computation.376 | convolution fusion | flops 6450836992 | bytes 24137728 | tf_op jit(solution)/shard_map/dot_general | solution.py:38
  947.7 35.7 %collective-permute-done.45 = bf16[1024,1536]{1,0:T(8,128)(2,1)} collective-permute-done((bf16[1024,1536]{1,0:T(8,128)(2,1)}, bf16[1024,1536]{1,0:T(8,128)(2,1)}, u32[]{:S(2)}, u32[]{:S(2)}) %collective-permute-start.45) | collective-permute-done | bytes 3145760 | tf_op jit(solution)/shard_map/ppermute | solution.py:254
  1001.8 9.6 collective-permute-start.40
  1011.8 17.0 %collective-permute-done.52 = bf16[1024,768]{1,0:T(8,128)(2,1)} collective-permute-done((bf16[1024,768]{1,0:T(8,128)(2,1)}, bf16[1024,768]{1,0:T(8,128)(2,1)}, u32[]{:S(2)}, u32[]{:S(2)}) %collective-permute-start.52) | collective-permute-done | bytes 1572896 | tf_op jit(solution)/shard_map/ppermute | solution.py:254
  1040.4 22.5 %collective-permute-done.43 = f32[4,6144]{1,0:T(4,128)S(1)} collective-permute-done((f32[4,6144]{1,0:T(4,128)S(1)}, f32[4,6144]{1,0:T(4,128)S(1)}, u32[]{:S(2)}, u32[]{:S(2)}) %collective-permute-start.43) | collective-permute-done | bytes 98336 | tf_op jit(solution)/shard_map/ppermute | solution.py:254
  1063.0 51.0 %collective-permute-done.41 = bf16[256,2048]{1,0:T(8,128)(2,1)} collective-permute-done((bf16[256,2048]{1,0:T(8,128)(2,1)}, bf16[256,2048]{1,0:T(8,128)(2,1)}, u32[]{:S(2)}, u32[]{:S(2)}) %collective-permute-start.41) | collective-permute-done | bytes 1048608 | tf_op jit(solution)/shard_map/ppermute | solution.py:282
  1124.7 14.1 %collective-permute-done.62 = bf16[512,512]{1,0:T(8,128)(2,1)S(1)} collective-permute-done((bf16[512,512]{1,0:T(8,128)(2,1)S(1)}, bf16[512,512]{1,0:T(8,128)(2,1)S(1)}, u32[]{:S(2)}, u32[]{:S(2)}) %collective-permute-start.62) | collective-permute-done | bytes 524320 | tf_op jit(solution)/shard_map/ppermute | solution.py:254
  1177.4 11.7 shard_map.637
  1190.9 11.7 shard_map.638
  1236.4 16.6 %shard_map.640 = f32[512,6144]{1,0:T(8,128)} custom-call(s32[6,24]{1,0:T(8,128)} %pad_add_fusion.8.table_ref, bf16[2048,768]{1,0:T(8,128)(2,1)} %copy-done.15, bf16[2048,768]{1,0:T(8,128)(2,1)} %collective-permute-done.77.refs_1_), custom_call_target="tpu_custom_call" | custom-call | tf_op jit(solution)/shard_map/pallas_call | solution.py:77
  (570 shorter events, 457.4 us)
Async XLA Ops:
  7.2 129.3 %all-gather.9.cloned.1.call-start = ((), (), s32[]{:S(2)}) async-start(), calls=%async_computation.8 | async-start | bytes 3932160 | tf_op jit(solution)/shard_map/all_gather | solution.py:293
  51.9 151.4 %all-gather.11.cloned.1.call-start = ((), (), s32[]{:S(2)}) async-start(), calls=%async_computation.9 | async-start | bytes 1310720 | tf_op jit(solution)/shard_map/all_gather | solution.py:293
  53.9 233.0 %all-gather.13.cloned.1.call-start = ((), (), s32[]{:S(2)}) async-start(), calls=%async_computation.10 | async-start | bytes 5242880 | tf_op jit(solution)/shard_map/all_gather | solution.py:293
  56.2 349.0 %all-gather.15.cloned.1.call-start = ((), (), s32[]{:S(2)}) async-start(), calls=%async_computation.11 | async-start | bytes 5242880 | tf_op jit(solution)/shard_map/all_gather | solution.py:293
  146.5 121.9 %collective-permute-start.6 = (bf16[512,2048]{1,0:T(8,128)(2,1)}, bf16[512,2048]{1,0:T(8,128)(2,1)}, u32[]{:S(2)}, u32[]{:S(2)}) collective-permute-start(bf16[512,2048]{1,0:T(8,128)(2,1)} %fusion.14), channel_id=1, source_target_pairs={{0,4},{4,0},{1,5},{5,1},{2,6},{6,2},{3,7},{7,3},{8,12},{12,8},{9,1... | collective-permute-start | bytes 6291464 | tf_op jit(solution)/shard_map/ppermute | solution.py:257
  207.5 828.1 %reduce-scatter.11.cloned.1.call-start = ((), (), s32[]{:S(2)}) async-start(), calls=%async_computation.7 | async-start | bytes 5242880 | tf_op jit(solution)/shard_map/reduce_scatter | solution.py:349
  290.9 101.7 %collective-permute-start.17 = (bf16[1536,1024]{1,0:T(8,128)(2,1)}, bf16[1536,1024]{1,0:T(8,128)(2,1)}, u32[]{:S(2)}, u32[]{:S(2)}) collective-permute-start(bf16[1536,1024]{1,0:T(8,128)(2,1)} %pad_maximum_fusion.19.refs_1_), channel_id=1, source_target_pairs={{0,16},{8,24},{16,0},{24,8},{1,17},{9,25},{17,1},{25,9},{2,18},{10... | collective-permute-start | bytes 9437192 | tf_op jit(solution)/shard_map/ppermute | solution.py:254
  292.4 100.3 %collective-permute-start.16 = (bf16[1536,1024]{1,0:T(8,128)(2,1)}, bf16[1536,1024]{1,0:T(8,128)(2,1)}, u32[]{:S(2)}, u32[]{:S(2)}) collective-permute-start(bf16[1536,1024]{1,0:T(8,128)(2,1)} %pad_maximum_fusion.19.refs_1_), channel_id=1, source_target_pairs={{0,8},{8,0},{16,24},{24,16},{1,9},{9,1},{17,25},{25,17},{2,10},{10... | collective-permute-start | bytes 9437192 | tf_op jit(solution)/shard_map/ppermute | solution.py:254
  293.9 73.2 %collective-permute-start.13 = (bf16[384,512]{1,0:T(8,128)(2,1)S(1)}, bf16[384,512]{1,0:T(8,128)(2,1)S(1)}, u32[]{:S(2)}, u32[]{:S(2)}) collective-permute-start(bf16[384,512]{1,0:T(8,128)(2,1)S(1)} %bitcast.161), channel_id=1, source_target_pairs={{0,16},{8,24},{16,0},{24,8},{1,17},{9,25},{17,1},{25,9},{2,18},{10... | collective-permute-start | bytes 1179656 | tf_op jit(solution)/shard_map/ppermute | solution.py:254
  294.5 73.8 %collective-permute-start.14 = (bf16[384,512]{1,0:T(8,128)(2,1)S(1)}, bf16[384,512]{1,0:T(8,128)(2,1)}, u32[]{:S(2)}, u32[]{:S(2)}) collective-permute-start(bf16[384,512]{1,0:T(8,128)(2,1)S(1)} %bitcast.160), channel_id=1, source_target_pairs={{0,8},{8,0},{16,24},{24,16},{1,9},{9,1},{17,25},{25,17},{2,10},{10... | collective-permute-start | bytes 1179656 | tf_op jit(solution)/shard_map/ppermute | solution.py:254
  413.2 74.0 %collective-permute-start.18 = (bf16[512,2048]{1,0:T(8,128)(2,1)}, bf16[512,2048]{1,0:T(8,128)(2,1)}, u32[]{:S(2)}, u32[]{:S(2)}) collective-permute-start(bf16[512,2048]{1,0:T(8,128)(2,1)} %add_convert_fusion.6), channel_id=1, source_target_pairs={{0,4},{4,0},{1,5},{5,1},{2,6},{6,2},{3,7},{7,3},{8,12},{12,8},{9,1... | collective-permute-start | bytes 6291464 | tf_op jit(solution)/shard_map/ppermute | solution.py:257
  443.7 71.3 %collective-permute-start.25 = (bf16[3072,512]{1,0:T(8,128)(2,1)}, bf16[3072,512]{1,0:T(8,128)(2,1)}, u32[]{:S(2)}, u32[]{:S(2)}) collective-permute-start(bf16[3072,512]{1,0:T(8,128)(2,1)} %pad_maximum_fusion.20.refs_1_), channel_id=1, source_target_pairs={{0,16},{8,24},{16,0},{24,8},{1,17},{9,25},{17,1},{25,9},{2,18},{10... | collective-permute-start | bytes 9437192 | tf_op jit(solution)/shard_map/ppermute | solution.py:254
  444.9 70.3 %collective-permute-start.24 = (bf16[3072,512]{1,0:T(8,128)(2,1)}, bf16[3072,512]{1,0:T(8,128)(2,1)}, u32[]{:S(2)}, u32[]{:S(2)}) collective-permute-start(bf16[3072,512]{1,0:T(8,128)(2,1)} %pad_maximum_fusion.20.refs_1_), channel_id=1, source_target_pairs={{0,8},{8,0},{16,24},{24,16},{1,9},{9,1},{17,25},{25,17},{2,10},{10... | collective-permute-start | bytes 9437192 | tf_op jit(solution)/shard_map/ppermute | solution.py:254
  535.8 109.8 %collective-permute-start.29 = (bf16[2048,1024]{1,0:T(8,128)(2,1)}, bf16[2048,1024]{1,0:T(8,128)(2,1)}, u32[]{:S(2)}, u32[]{:S(2)}) collective-permute-start(bf16[2048,1024]{1,0:T(8,128)(2,1)} %convolution_convert_fusion.2), channel_id=1, source_target_pairs={{0,16},{8,24},{16,0},{24,8},{1,17},{9,25},{17,1},{25,9},{2,18},{10... | collective-permute-start | bytes 12582920 | tf_op jit(solution)/shard_map/ppermute | solution.py:254
  536.9 109.4 %collective-permute-start.28 = (bf16[2048,1024]{1,0:T(8,128)(2,1)}, bf16[2048,1024]{1,0:T(8,128)(2,1)}, u32[]{:S(2)}, u32[]{:S(2)}) collective-permute-start(bf16[2048,1024]{1,0:T(8,128)(2,1)} %convolution_convert_fusion.3), channel_id=1, source_target_pairs={{0,8},{8,0},{16,24},{24,16},{1,9},{9,1},{17,25},{25,17},{2,10},{10... | collective-permute-start | bytes 12582920 | tf_op jit(solution)/shard_map/ppermute | solution.py:254
  683.8 120.9 %collective-permute-start.37 = (bf16[1024,2048]{1,0:T(8,128)(2,1)}, bf16[1024,2048]{1,0:T(8,128)(2,1)}, u32[]{:S(2)}, u32[]{:S(2)}) collective-permute-start(bf16[1024,2048]{1,0:T(8,128)(2,1)} %fusion.29), channel_id=1, source_target_pairs={{0,8},{8,0},{16,24},{24,16},{1,9},{9,1},{17,25},{25,17},{2,10},{10... | collective-permute-start | bytes 12582920 | tf_op jit(solution)/shard_map/ppermute | solution.py:254
  692.6 112.2 %collective-permute-start.38 = (bf16[1024,2048]{1,0:T(8,128)(2,1)}, bf16[1024,2048]{1,0:T(8,128)(2,1)}, u32[]{:S(2)}, u32[]{:S(2)}) collective-permute-start(bf16[1024,2048]{1,0:T(8,128)(2,1)} %fusion.28), channel_id=1, source_target_pairs={{0,16},{8,24},{16,0},{24,8},{1,17},{9,25},{17,1},{25,9},{2,18},{10... | collective-permute-start | bytes 12582920 | tf_op jit(solution)/shard_map/ppermute | solution.py:254
  765.7 351.6 %reduce-scatter.9.cloned.1.call-start = ((), (), s32[]{:S(2)}) async-start(), calls=%async_computation.6 | async-start | bytes 5242880 | tf_op jit(solution)/shard_map/reduce_scatter | solution.py:349
  770.0 142.0 %collective-permute-start.49 = (bf16[512,1024]{1,0:T(8,128)(2,1)}, bf16[512,1024]{1,0:T(8,128)(2,1)}, u32[]{:S(2)}, u32[]{:S(2)}) collective-permute-start(bf16[512,1024]{1,0:T(8,128)(2,1)} %fusion.101), channel_id=1, source_target_pairs={{0,8},{8,0},{16,24},{24,16},{1,9},{9,1},{17,25},{25,17},{2,10},{10... | collective-permute-start | bytes 3145736 | tf_op jit(solution)/shard_map/ppermute | solution.py:254
  773.8 139.9 %collective-permute-start.50 = (bf16[512,1024]{1,0:T(8,128)(2,1)}, bf16[512,1024]{1,0:T(8,128)(2,1)}, u32[]{:S(2)}, u32[]{:S(2)}) collective-permute-start(bf16[512,1024]{1,0:T(8,128)(2,1)} %fusion.100), channel_id=1, source_target_pairs={{0,16},{8,24},{16,0},{24,8},{1,17},{9,25},{17,1},{25,9},{2,18},{10... | collective-permute-start | bytes 3145736 | tf_op jit(solution)/shard_map/ppermute | solution.py:254
  794.6 125.5 %collective-permute-start.33 = (bf16[256,2048]{1,0:T(8,128)(2,1)}, bf16[256,2048]{1,0:T(8,128)(2,1)S(1)}, u32[]{:S(2)}, u32[]{:S(2)}) collective-permute-start(bf16[256,2048]{1,0:T(8,128)(2,1)} %get-tuple-element.187), channel_id=1, source_target_pairs={{0,0},{2,1},{4,2},{6,3},{1,4},{3,5},{5,6},{7,7},{8,8},{10,9},{12,1... | collective-permute-start | bytes 3145736 | tf_op jit(solution)/shard_map/ppermute | solution.py:282
  808.1 79.4 %collective-permute-start.48 = (bf16[1024,1024]{1,0:T(8,128)(2,1)}, bf16[1024,1024]{1,0:T(8,128)(2,1)}, u32[]{:S(2)}, u32[]{:S(2)}) collective-permute-start(bf16[1024,1024]{1,0:T(8,128)(2,1)} %slice_add_fusion), channel_id=1, source_target_pairs={{0,16},{8,24},{16,0},{24,8},{1,17},{9,25},{17,1},{25,9},{2,18},{10... | collective-permute-start | bytes 6291464 | tf_op jit(solution)/shard_map/ppermute | solution.py:254
  810.8 78.5 %collective-permute-start.47 = (bf16[1024,1024]{1,0:T(8,128)(2,1)S(1)}, bf16[1024,1024]{1,0:T(8,128)(2,1)}, u32[]{:S(2)}, u32[]{:S(2)}) collective-permute-start(bf16[1024,1024]{1,0:T(8,128)(2,1)S(1)} %slice_add_fusion.1), channel_id=1, source_target_pairs={{0,8},{8,0},{16,24},{24,16},{1,9},{9,1},{17,25},{25,17},{2,10},{10... | collective-permute-start | bytes 6291464 | tf_op jit(solution)/shard_map/ppermute | solution.py:254
  901.4 260.5 %reduce-scatter.7.cloned.1.call-start = ((), (), s32[]{:S(2)}) async-start(), calls=%async_computation.5 | async-start | bytes 1310720 | tf_op jit(solution)/shard_map/reduce_scatter | solution.py:349
  912.1 71.3 %collective-permute-start.45 = (bf16[1024,1536]{1,0:T(8,128)(2,1)}, bf16[1024,1536]{1,0:T(8,128)(2,1)}, u32[]{:S(2)}, u32[]{:S(2)}) collective-permute-start(bf16[1024,1536]{1,0:T(8,128)(2,1)} %convolution_convert_fusion.1), channel_id=1, source_target_pairs={{0,8},{8,0},{16,24},{24,16},{1,9},{9,1},{17,25},{25,17},{2,10},{10... | collective-permute-start | bytes 9437192 | tf_op jit(solution)/shard_map/ppermute | solution.py:254
  913.7 71.3 %collective-permute-start.46 = (bf16[1024,1536]{1,0:T(8,128)(2,1)}, bf16[1024,1536]{1,0:T(8,128)(2,1)}, u32[]{:S(2)}, u32[]{:S(2)}) collective-permute-start(bf16[1024,1536]{1,0:T(8,128)(2,1)} %convolution_convert_fusion), channel_id=1, source_target_pairs={{0,16},{8,24},{16,0},{24,8},{1,17},{9,25},{17,1},{25,9},{2,18},{10... | collective-permute-start | bytes 9437192 | tf_op jit(solution)/shard_map/ppermute | solution.py:254
  920.1 74.5 %collective-permute-start.56 = (bf16[512,512]{1,0:T(8,128)(2,1)}, bf16[512,512]{1,0:T(8,128)(2,1)}, u32[]{:S(2)}, u32[]{:S(2)}) collective-permute-start(bf16[512,512]{1,0:T(8,128)(2,1)} %fusion.123), channel_id=1, source_target_pairs={{0,8},{8,0},{16,24},{24,16},{1,9},{9,1},{17,25},{25,17},{2,10},{10... | collective-permute-start | bytes 1572872 | tf_op jit(solution)/shard_map/ppermute | solution.py:254
  920.8 75.4 %collective-permute-start.57 = (bf16[512,512]{1,0:T(8,128)(2,1)}, bf16[512,512]{1,0:T(8,128)(2,1)}, u32[]{:S(2)}, u32[]{:S(2)}) collective-permute-start(bf16[512,512]{1,0:T(8,128)(2,1)} %fusion.119), channel_id=1, source_target_pairs={{0,16},{8,24},{16,0},{24,8},{1,17},{9,25},{17,1},{25,9},{2,18},{10... | collective-permute-start | bytes 1572872 | tf_op jit(solution)/shard_map/ppermute | solution.py:254
  1001.7 187.4 %reduce-scatter.5.cloned.1.call-start = ((), (), s32[]{:S(2)}) async-start(), calls=%async_computation.4 | async-start | bytes 3932160 | tf_op jit(solution)/shard_map/reduce_scatter | solution.py:349
  1011.4 102.6 %collective-permute-start.41 = (bf16[256,2048]{1,0:T(8,128)(2,1)}, bf16[256,2048]{1,0:T(8,128)(2,1)}, u32[]{:S(2)}, u32[]{:S(2)}) collective-permute-start(bf16[256,2048]{1,0:T(8,128)(2,1)} %get-tuple-element.184), channel_id=1, source_target_pairs={{2,0},{0,1},{6,2},{4,3},{3,4},{1,5},{7,6},{5,7},{10,8},{8,9},{14,1... | collective-permute-start | bytes 3145736 | tf_op jit(solution)/shard_map/ppermute | solution.py:282
  1035.6 81.6 %collective-permute-start.59 = (bf16[1024,512]{1,0:T(8,128)(2,1)}, bf16[1024,512]{1,0:T(8,128)(2,1)S(1)}, u32[]{:S(2)}, u32[]{:S(2)}) collective-permute-start(bf16[1024,512]{1,0:T(8,128)(2,1)} %reduce-scatter.11.cloned.1.call-done), channel_id=1, source_target_pairs={{0,16},{8,24},{16,0},{24,8},{1,17},{9,25},{17,1},{25,9},{2,18},{10... | collective-permute-start | bytes 3145736 | tf_op jit(solution)/shard_map/ppermute | solution.py:254
  1036.9 80.3 %collective-permute-start.58 = (bf16[1024,512]{1,0:T(8,128)(2,1)}, bf16[1024,512]{1,0:T(8,128)(2,1)S(1)}, u32[]{:S(2)}, u32[]{:S(2)}) collective-permute-start(bf16[1024,512]{1,0:T(8,128)(2,1)} %reduce-scatter.11.cloned.1.call-done), channel_id=1, source_target_pairs={{0,8},{8,0},{16,24},{24,16},{1,9},{9,1},{17,25},{25,17},{2,10},{10... | collective-permute-start | bytes 3145736 | tf_op jit(solution)/shard_map/ppermute | solution.py:254
  (142 other events, 3340.0 us)
Sparse Core Ops, SparseCore 0:
  52.0 84.3 all-gather.8
  138.1 26.6 all-gather.10
  166.9 80.1 all-gather.12
  248.4 79.2 all-gather.14
  765.8 89.5 reduce-scatter.10
  901.5 82.3 reduce-scatter.8
  1001.9 39.9 reduce-scatter.6
  1044.7 75.5 reduce-scatter.4

commit v6 on v5

--- a/solution.py
+++ b/solution.py
@@ -443,6 +443,7 @@
         qkv_ends = plane(qkv_low, 2), plane(qkv_high, 1)
         out_others = others_of(after(out_got, (qkv_low, qkv_high)))
         out_x, out_y, out_low, out_high = spread_others(out_others)
+        out_ends = plane(out_low, 2), plane(out_high, 1)
 
     hidden_f = tokens.astype(F32)
     normed_own = normalize(hidden_f, gain_one, shift_one).astype(BF)
@@ -454,7 +455,7 @@
             qkv_mine, None, 1, piece_rows, qkv_others, qkv_x, qkv_y, *qkv_ends
         )
         out_full = whole_weight(
-            out_weight, (2 * core, none), 1, piece_rows // 2, out_others, out_x, out_y, plane(out_low, 2), plane(out_high, 1)
+            out_weight, (2 * core, none), 1, piece_rows // 2, out_others, out_x, out_y, *out_ends
         )
     else:
         qkv_full, out_full, fc1_full, fc2_full = [
@@ -466,7 +467,7 @@
     projected = dot(normed_one, qkv_full) + jnp.concatenate([bias_query, jnp.zeros_like(bias_query), bias_value])
     projected = projected.astype(BF)
     if square:
-        fc1_others = others_of(after(fc1_got, (projected, out_low, out_high)))
+        fc1_others = others_of(after(fc1_got, (projected, *out_ends)))
     scalars = jnp.stack([core.astype(jnp.int32), prefix_len.astype(jnp.int32)])
     if parts == 1:
         context = attend_forward(projected, scalars)
@@ -602,7 +603,7 @@
         qkv_red = Reduction(normed_one, d_projected)
         out_red.second()
         d_projected = after(d_projected, qkv_red.near)
-        fc1_part = fc1_red.third((*qkv_red.near, d_projected))
+        fc1_part = fc1_red.third((*qkv_red.near, d_projected, result))
         qkv_red.second((fc1_red.mine, *out_red.sent))
     query_bias_grad = jnp.sum(d_projected[:, :half_width], axis=0, dtype=F32)
     value_bias_grad = jnp.sum(d_projected[:, width:], axis=0, dtype=F32)
@@ -647,11 +648,11 @@
 
     packed = packed + swap(packed)
     if square:
-        out_part = out_red.third((*qkv_red.sent, result))
+        out_part = out_red.third((*qkv_red.sent, grad_in))
         fc2_first = spread_first(after(fc2_part, (qkv_red.sent, out_red.mine)))
         qkv_part = qkv_red.third()
         packed = sum_plane(packed, [0])
-        fc1_first = spread_first(after(fc1_part, (fc2_first[1:], qkv_red.mine, packed, grad_in)))
+        fc1_first = spread_first(after(fc1_part, (fc2_first[1:], qkv_red.mine, packed)))
         fc2_pair = spread_second(*fc2_first)
         packed = sum_plane(packed, [1])
         out_first = spread_first(after(out_part, (fc1_first[1:], fc2_pair[0], packed)))

time: 1270 us -> 1200 us (0.945)
  waiting for transfers between devices: 473 us -> 403 us
    ppermute x50, waiting for transfers between devices: 332 us -> 274 us  [plane(): return lax.ppermute(value, 'ch', [(i, i ^ bit) for i in range(chips)])]
    ppermute x4, waiting for transfers between devices: 51.1 us -> 38.2 us  [tokens_out(): lax.ppermute(lax.dynamic_index_in_dim(value, (turn + micro) % 2, 0, False...]
    unnamed x230 -> x220, local copies, waits for them, and re-layouts: 42.5 us -> 44.2 us
  transfers between devices with their start and end apart: 86 -> 86, of which waited for: 34 -> 33; matrix products, arithmetic and copies ran while one was open for 36% -> 38% of each run, Pallas kernels for 14% -> 15%
where the time goes in v6:
time: 1200 us; the launch traced here: 1190 us
  waiting for transfers between devices  403 us (34%)
  matrix products  293 us (24%)
  Pallas kernels  194 us (16%)
  starting transfers between devices  105 us (9%)
  local copies, waits for them, and re-layouts  91.7 us (8%)
  other arithmetic  91.2 us (8%)
  between operations  16.5 us (1%)
    ppermute x50, waiting for transfers between devices, plane(): return lax.ppermute(value, 'ch', [(i, i ^ bit) for i in range(chips)])  274 us
    pallas_call x8, Pallas kernels, place(): pl.pallas_call(body, grid_spec=pltpu.PrefetchScalarGridSpec(num_scalar_pr...  139 us
    dot_general x24, matrix products, cross_rows(): lax.dot_general(left_side, right_side, (((0,), (0,)), ((), ())), preferre...  119 us
    dot_general x6, matrix products, times_rows(): lax.dot_general(left_side, right_side, (((1,), (1,)), ((), ())), preferre...  92.3 us
    dot_general x6, matrix products, dot(): return jnp.dot(left_side, right_side, preferred_element_type=F32)  81.7 us
    all_gather x4, waiting for transfers between devices, gather_shards(): return lax.all_gather(piece, 'sh')  80.1 us
    ppermute x50, starting transfers between devices, plane(): return lax.ppermute(value, 'ch', [(i, i ^ bit) for i in range(chips)])  52.2 us
    unnamed x220, local copies, waits for them, and re-layouts  44.2 us
  transfers between devices with their start and end apart: 86, of which 33 were waited for; matrix products, arithmetic and copies ran while one was open for 38% of the time, Pallas kernels for 15%

profile of v6, /device:TPU:0, one launch (start us, length us, event | category | flops | bytes accessed | tf_op | source)
XLA Modules:
  0.0 1193.5 jit_solution(16080079736765069445)
XLA Ops:
  56.4 80.1 %all-gather.9.cloned.1.call-done = bf16[2048,768]{1,0:T(8,128)(2,1)} async-done(((bf16[512,768]{1,0:T(8,128)(2,1)}), bf16[2048,768]{1,0:T(8,128)(2,1)}) %all-gather.9.cloned.1.call-update) | async-done | bytes 3145744 | tf_op jit(solution)/shard_map/all_gather | solution.py:293
  146.6 46.4 %collective-permute-done.8.refs_3_ = bf16[1536,768]{1,0:T(8,128)(2,1)} collective-permute-done((bf16[1536,768]{1,0:T(8,128)(2,1)}, bf16[1536,768]{1,0:T(8,128)(2,1)}, u32[]{:S(2)}, u32[]{:S(2)}) %collective-permute-start.8) | collective-permute-done | bytes 2359328 | tf_op jit(solution)/shard_map/ppermute | solution.py:254
  207.8 34.8 %collective-permute-done.12.refs_3_ = bf16[768,512]{1,0:T(8,128)(2,1)} collective-permute-done((bf16[768,512]{1,0:T(8,128)(2,1)S(1)}, bf16[768,512]{1,0:T(8,128)(2,1)}, u32[]{:S(2)}, u32[]{:S(2)}) %collective-permute-start.12) | collective-permute-done | bytes 786464 | tf_op jit(solution)/shard_map/ppermute | solution.py:254
  248.6 22.7 %shard_map.631 = bf16[2048,3072]{1,0:T(8,128)(2,1)} custom-call(s32[14,32]{1,0:T(8,128)} %get-tuple-element.224.table_ref, bf16[512,3072]{1,0:T(8,128)(2,1)} %get-tuple-element.160.refs_0_, bf16[1536,768]{1,0:T(8,128)(2,1)} %pad_maximum_fusion.26.refs_1_, bf16[1536,768]{1,0:T(8,128)(2,1)} %collective-permute-done.7.refs_2_, ...), custom_call_target="tpu_custom_call" | custom-call | tf_op jit(solution)/shard_map/pallas_call | solution.py:77
  271.3 18.5 %add_convert_fusion.q_ref.k_ref.v_ref = bf16[1024,3072]{1,0:T(8,128)(2,1)} fusion(bf16[2048,3072]{1,0:T(8,128)(2,1)} %shard_map.631, f32[3072]{0:T(1024)S(1)} %pad_maximum_fusion.42, bf16[512,2048]{1,0:T(8,128)(2,1)} %collective-permute-done.6, bf16[512,2048]{1,0:T(8,128)(2,1)} %fusion.14), kind=kOutput, calls=%fused_computation.10 | convolution fusion | flops 12899581952 | bytes 23080960 | tf_op jit(solution)/shard_map/dot_general | solution.py:30
  298.2 20.4 %shard_map.632 = bf16[1024,1024]{1,0:T(8,128)(2,1)} custom-call(s32[2]{0:T(128)} %pad_add_fusion.10.scal_ref, bf16[1024,3072]{1,0:T(8,128)(2,1)} %add_convert_fusion.q_ref.k_ref.v_ref, bf16[1024,3072]{1,0:T(8,128)(2,1)} %add_convert_fusion.q_ref.k_ref.v_ref, bf16[1024,3072]{1,0:T(8,128)(2,1)} %add_convert_fusion.q_ref.k_ref.v_ref), custom_call_target="tpu_custom_call" | custom-call | tf_op jit(solution)/shard_map/pallas_call | solution.py:172
  318.6 19.3 %shard_map.633 = bf16[1024,2048]{1,0:T(8,128)(2,1)} custom-call(s32[14,32]{1,0:T(8,128)} %get-tuple-element.223.table_ref, bf16[512,2048]{1,0:T(8,128)(2,1)} %refs_0_.3, bf16[768,512]{1,0:T(8,128)(2,1)} %copy-done.18, bf16[768,512]{1,0:T(8,128)(2,1)} %collective-permute-done.11.refs_2_, bf16[768,512]{1,0:T(8,128)(2,1)} %collective-permute-done.12.refs_3_, ...), custom_call_target="tpu_custom_call" | custom-call | tf_op jit(solution)/shard_map/pallas_call | solution.py:77
  343.1 17.8 %collective-permute-done.17.refs_3_ = bf16[1536,1024]{1,0:T(8,128)(2,1)} collective-permute-done((bf16[1536,1024]{1,0:T(8,128)(2,1)}, bf16[1536,1024]{1,0:T(8,128)(2,1)}, u32[]{:S(2)}, u32[]{:S(2)}) %collective-permute-start.17) | collective-permute-done | bytes 3145760 | tf_op jit(solution)/shard_map/ppermute | solution.py:254
  381.3 17.6 %collective-permute-done.19.refs_4_ = bf16[768,1024]{1,0:T(8,128)(2,1)} collective-permute-done((bf16[768,1024]{1,0:T(8,128)(2,1)}, bf16[768,1024]{1,0:T(8,128)(2,1)}, u32[]{:S(2)}, u32[]{:S(2)}) %collective-permute-start.19) | collective-permute-done | bytes 1572896 | tf_op jit(solution)/shard_map/ppermute | solution.py:254
  409.4 25.1 %shard_map.634 = bf16[2048,4096]{1,0:T(8,128)(2,1)} custom-call(s32[14,32]{1,0:T(8,128)} %get-tuple-element.222.table_ref, bf16[512,8192]{1,0:T(8,128)(2,1)} %refs_0_.4, bf16[1536,1024]{1,0:T(8,128)(2,1)} %pad_maximum_fusion.19.refs_1_, bf16[1536,1024]{1,0:T(8,128)(2,1)} %collective-permute-done.16.refs_2_, ...), custom_call_target="tpu_custom_call" | custom-call | tf_op jit(solution)/shard_map/pallas_call | solution.py:77
  436.0 11.4 collective-permute-start.23
  447.4 27.8 %multiply_convert_fusion.1 = (bf16[1024,4096]{1,0:T(8,128)(2,1)}, f32[1024,4096]{1,0:T(8,128)}) fusion(f32[4096]{0:T(1024)S(1)} %bitcast.177, bf16[2048,4096]{1,0:T(8,128)(2,1)} %shard_map.634, bf16[512,2048]{1,0:T(8,128)(2,1)} %collective-permute-done.18, bf16[512,2048]{1,0:T(8,128)(2,1)} %add_convert_fusion.6), kind=kOutput, calls=%fused_computation.8 | convolution fusion | flops 17213423616 | bytes 46153728 | tf_op jit(solution)/shard_map/dot_general | solution.py:30
  508.5 10.6 collective-permute-done.26.refs_4_
  520.9 24.7 %shard_map.635 = bf16[4096,2048]{1,0:T(8,128)(2,1)} custom-call(s32[14,32]{1,0:T(8,128)} %get-tuple-element.223.table_ref, bf16[2048,2048]{1,0:T(8,128)(2,1)} %refs_0_.5, bf16[3072,512]{1,0:T(8,128)(2,1)} %pad_maximum_fusion.20.refs_1_, bf16[3072,512]{1,0:T(8,128)(2,1)} %collective-permute-done.24.refs_2_, ...), custom_call_target="tpu_custom_call" | custom-call | tf_op jit(solution)/shard_map/pallas_call | solution.py:77
  545.6 29.5 %convert_reduce_fusion = (f32[4096]{0:T(1024)S(1)}, bf16[1024,4096]{1,0:T(8,128)(2,1)}) fusion(f32[1024,4096]{1,0:T(8,128)} %get-tuple-element.231, f32[4096]{0:T(1024)S(1)} %bitcast.178, bf16[1024,2048]{1,0:T(8,128)(2,1)} %copy-done.13, bf16[4096,2048]{1,0:T(8,128)(2,1)} %shard_map.635), kind=kOutput, calls=%fused_computation.6 | convolution fusion | flops 17242779648 | bytes 46170112 | tf_op jit(solution)/shard_map/dot_general | solution.py:38
  575.7 33.3 %collective-permute-done.29 = bf16[2048,1024]{1,0:T(8,128)(2,1)} collective-permute-done((bf16[2048,1024]{1,0:T(8,128)(2,1)}, bf16[2048,1024]{1,0:T(8,128)(2,1)}, u32[]{:S(2)}, u32[]{:S(2)}) %collective-permute-start.29) | collective-permute-done | bytes 4194336 | tf_op jit(solution)/shard_map/ppermute | solution.py:254
  624.6 13.4 %fusion.70 = bf16[512,2048]{1,0:T(8,128)(2,1)} fusion(bf16[2048,4096]{1,0:T(8,128)(2,1)} %shard_map.634, bf16[1024,4096]{1,0:T(8,128)(2,1)S(1)} %bitcast.152), kind=kOutput, calls=%fused_computation.116 | convolution fusion | flops 8590983168 | bytes 23068672 | tf_op jit(solution)/shard_map/dot_general | solution.py:38
  668.6 17.9 %multiply_reduce_fusion = (f32[2048]{0:T(1024)S(1)}, f32[512]{0:T(512)S(1)}, f32[2048]{0:T(1024)S(1)}, f32[512,2048]{1,0:T(8,128)}) fusion(f32[512,2048]{1,0:T(8,128)} %convert_add_fusion, f32[512]{0:T(512)S(1)} %copy-done.51, f32[512]{0:T(512)S(1)} %copy-done.43, f32[2048]{0:T(1024)S(1)} %bitcast.168, bf16[512,2048]{1,0:T(8,128)(2,1)} %collective-permute-done.35, ...), kind=kOutput, calls=%fused_computation.59 | convolution fusion | flops 8600416256 | bytes 31488000 | tf_op jit(solution)/shard_map/dot_general | solution.py:38
  706.3 11.7 fusion.67
  736.9 14.1 %add_add_fusion.2 = bf16[512,2048]{1,0:T(8,128)(2,1)S(1)} fusion(f32[512,2048]{1,0:T(8,128)S(1)} %copy-done.3, bf16[512,2048]{1,0:T(8,128)(2,1)} %collective-permute-done.32, bf16[4096,2048]{1,0:T(8,128)(2,1)} %shard_map.635, bf16[1024,4096]{1,0:T(8,128)(2,1)} %get-tuple-element.109, f32[2048]{0:T(1024)S(1)} %bitcast.181), kind=kOutput, calls=%fused_computation.73 | convolution fusion | flops 8595177472 | bytes 29368320 | tf_op jit(solution)/shard_map/dot_general | solution.py:30
  756.7 9.6 collective-permute-start.33
  783.6 34.3 %shard_map.636 = (bf16[1024,1024]{1,0:T(8,128)(2,1)}, bf16[1024,1024]{1,0:T(8,128)(2,1)}, bf16[1024,1024]{1,0:T(8,128)(2,1)}) custom-call(s32[2]{0:T(128)} %pad_add_fusion.10.scal_ref, bf16[1024,3072]{1,0:T(8,128)(2,1)} %add_convert_fusion.q_ref.k_ref.v_ref, bf16[1024,3072]{1,0:T(8,128)(2,1)} %add_convert_fusion.q_ref.k_ref.v_ref, ...), custom_call_target="tpu_custom_call" | custom-call | tf_op jit(solution)/shard_map/pallas_call | solution.py:188
  846.7 10.7 fusion.52
  882.3 12.9 %fusion.192 = (f32[2048]{0:T(1024)S(1)}, f32[512]{0:T(512)S(1)}, f32[512,2048]{1,0:T(8,128)}) fusion(f32[2048]{0:T(1024)S(1)} %bitcast.162, f32[512]{0:T(512)S(1)} %copy-done.39, bf16[512,2048]{1,0:T(8,128)(2,1)S(1)} %copy-done.1, bf16[512,2048]{1,0:T(8,128)(2,1)} %collective-permute-done.39, bf16[2048,3072]{1,0:T(8,128)(2,1)} %shard_map.631, ...), kind=kOutput, calls=%fused_computation.376 | convolution fusion | flops 6450836992 | bytes 24137728 | tf_op jit(solution)/shard_map/dot_general | solution.py:38
  913.9 32.2 %collective-permute-done.45 = bf16[1024,1536]{1,0:T(8,128)(2,1)} collective-permute-done((bf16[1024,1536]{1,0:T(8,128)(2,1)}, bf16[1024,1536]{1,0:T(8,128)(2,1)}, u32[]{:S(2)}, u32[]{:S(2)}) %collective-permute-start.45) | collective-permute-done | bytes 3145760 | tf_op jit(solution)/shard_map/ppermute | solution.py:254
  954.1 38.2 %collective-permute-done.41 = bf16[256,2048]{1,0:T(8,128)(2,1)S(1)} collective-permute-done((bf16[256,2048]{1,0:T(8,128)(2,1)S(1)}, bf16[256,2048]{1,0:T(8,128)(2,1)S(1)}, u32[]{:S(2)}, u32[]{:S(2)}) %collective-permute-start.41) | collective-permute-done | bytes 1048608 | tf_op jit(solution)/shard_map/ppermute | solution.py:282
  1015.5 19.6 %collective-permute-done.43 = f32[4,6144]{1,0:T(4,128)S(1)} collective-permute-done((f32[4,6144]{1,0:T(4,128)S(1)}, f32[4,6144]{1,0:T(4,128)S(1)}, u32[]{:S(2)}, u32[]{:S(2)}) %collective-permute-start.43) | collective-permute-done | bytes 98336 | tf_op jit(solution)/shard_map/ppermute | solution.py:254
  1044.3 14.8 %collective-permute-done.62 = bf16[512,512]{1,0:T(8,128)(2,1)S(1)} collective-permute-done((bf16[512,512]{1,0:T(8,128)(2,1)S(1)}, bf16[512,512]{1,0:T(8,128)(2,1)S(1)}, u32[]{:S(2)}, u32[]{:S(2)}) %collective-permute-start.62) | collective-permute-done | bytes 524320 | tf_op jit(solution)/shard_map/ppermute | solution.py:254
  1068.9 9.1 collective-permute-done.68
  1100.7 11.7 shard_map.637
  1114.2 11.7 shard_map.638
  1169.6 16.6 %shard_map.640 = f32[512,6144]{1,0:T(8,128)} custom-call(s32[6,24]{1,0:T(8,128)} %pad_add_fusion.8.table_ref, bf16[2048,768]{1,0:T(8,128)(2,1)} %copy-done.14, bf16[2048,768]{1,0:T(8,128)(2,1)} %collective-permute-done.77.refs_1_), custom_call_target="tpu_custom_call" | custom-call | tf_op jit(solution)/shard_map/pallas_call | solution.py:77
  (560 shorter events, 458.3 us)
Async XLA Ops:
  7.2 129.3 %all-gather.9.cloned.1.call-start = ((), (), s32[]{:S(2)}) async-start(), calls=%async_computation.8 | async-start | bytes 3932160 | tf_op jit(solution)/shard_map/all_gather | solution.py:293
  51.9 151.4 %all-gather.11.cloned.1.call-start = ((), (), s32[]{:S(2)}) async-start(), calls=%async_computation.9 | async-start | bytes 1310720 | tf_op jit(solution)/shard_map/all_gather | solution.py:293
  53.9 235.9 %all-gather.13.cloned.1.call-start = ((), (), s32[]{:S(2)}) async-start(), calls=%async_computation.10 | async-start | bytes 5242880 | tf_op jit(solution)/shard_map/all_gather | solution.py:293
  56.2 317.1 %all-gather.15.cloned.1.call-start = ((), (), s32[]{:S(2)}) async-start(), calls=%async_computation.11 | async-start | bytes 5242880 | tf_op jit(solution)/shard_map/all_gather | solution.py:293
  139.8 53.1 %collective-permute-start.8 = (bf16[1536,768]{1,0:T(8,128)(2,1)}, bf16[1536,768]{1,0:T(8,128)(2,1)}, u32[]{:S(2)}, u32[]{:S(2)}) collective-permute-start(bf16[1536,768]{1,0:T(8,128)(2,1)} %pad_maximum_fusion.26.refs_1_), channel_id=1, source_target_pairs={{0,16},{8,24},{16,0},{24,8},{1,17},{9,25},{17,1},{25,9},{2,18},{10... | collective-permute-start | bytes 7077896 | tf_op jit(solution)/shard_map/ppermute | solution.py:254
  141.3 52.9 %collective-permute-start.7 = (bf16[1536,768]{1,0:T(8,128)(2,1)}, bf16[1536,768]{1,0:T(8,128)(2,1)}, u32[]{:S(2)}, u32[]{:S(2)}) collective-permute-start(bf16[1536,768]{1,0:T(8,128)(2,1)} %pad_maximum_fusion.26.refs_1_), channel_id=1, source_target_pairs={{0,8},{8,0},{16,24},{24,16},{1,9},{9,1},{17,25},{25,17},{2,10},{10... | collective-permute-start | bytes 7077896 | tf_op jit(solution)/shard_map/ppermute | solution.py:254
  146.6 124.7 %collective-permute-start.6 = (bf16[512,2048]{1,0:T(8,128)(2,1)}, bf16[512,2048]{1,0:T(8,128)(2,1)}, u32[]{:S(2)}, u32[]{:S(2)}) collective-permute-start(bf16[512,2048]{1,0:T(8,128)(2,1)} %fusion.14), channel_id=1, source_target_pairs={{0,4},{4,0},{1,5},{5,1},{2,6},{6,2},{3,7},{7,3},{8,12},{12,8},{9,1... | collective-permute-start | bytes 6291464 | tf_op jit(solution)/shard_map/ppermute | solution.py:257
  207.5 802.7 %reduce-scatter.11.cloned.1.call-start = ((), (), s32[]{:S(2)}) async-start(), calls=%async_computation.7 | async-start | bytes 5242880 | tf_op jit(solution)/shard_map/reduce_scatter | solution.py:349
  293.9 67.1 %collective-permute-start.17 = (bf16[1536,1024]{1,0:T(8,128)(2,1)}, bf16[1536,1024]{1,0:T(8,128)(2,1)}, u32[]{:S(2)}, u32[]{:S(2)}) collective-permute-start(bf16[1536,1024]{1,0:T(8,128)(2,1)} %pad_maximum_fusion.19.refs_1_), channel_id=1, source_target_pairs={{0,16},{8,24},{16,0},{24,8},{1,17},{9,25},{17,1},{25,9},{2,18},{10... | collective-permute-start | bytes 9437192 | tf_op jit(solution)/shard_map/ppermute | solution.py:254
  294.4 66.9 %collective-permute-start.16 = (bf16[1536,1024]{1,0:T(8,128)(2,1)}, bf16[1536,1024]{1,0:T(8,128)(2,1)}, u32[]{:S(2)}, u32[]{:S(2)}) collective-permute-start(bf16[1536,1024]{1,0:T(8,128)(2,1)} %pad_maximum_fusion.19.refs_1_), channel_id=1, source_target_pairs={{0,8},{8,0},{16,24},{24,16},{1,9},{9,1},{17,25},{25,17},{2,10},{10... | collective-permute-start | bytes 9437192 | tf_op jit(solution)/shard_map/ppermute | solution.py:254
  381.3 66.1 %collective-permute-start.18 = (bf16[512,2048]{1,0:T(8,128)(2,1)}, bf16[512,2048]{1,0:T(8,128)(2,1)}, u32[]{:S(2)}, u32[]{:S(2)}) collective-permute-start(bf16[512,2048]{1,0:T(8,128)(2,1)} %add_convert_fusion.6), channel_id=1, source_target_pairs={{0,4},{4,0},{1,5},{5,1},{2,6},{6,2},{3,7},{7,3},{8,12},{12,8},{9,1... | collective-permute-start | bytes 6291464 | tf_op jit(solution)/shard_map/ppermute | solution.py:257
  408.1 69.9 %collective-permute-start.25 = (bf16[3072,512]{1,0:T(8,128)(2,1)}, bf16[3072,512]{1,0:T(8,128)(2,1)}, u32[]{:S(2)}, u32[]{:S(2)}) collective-permute-start(bf16[3072,512]{1,0:T(8,128)(2,1)} %pad_maximum_fusion.20.refs_1_), channel_id=1, source_target_pairs={{0,16},{8,24},{16,0},{24,8},{1,17},{9,25},{17,1},{25,9},{2,18},{10... | collective-permute-start | bytes 9437192 | tf_op jit(solution)/shard_map/ppermute | solution.py:254
  408.7 69.9 %collective-permute-start.24 = (bf16[3072,512]{1,0:T(8,128)(2,1)}, bf16[3072,512]{1,0:T(8,128)(2,1)}, u32[]{:S(2)}, u32[]{:S(2)}) collective-permute-start(bf16[3072,512]{1,0:T(8,128)(2,1)} %pad_maximum_fusion.20.refs_1_), channel_id=1, source_target_pairs={{0,8},{8,0},{16,24},{24,16},{1,9},{9,1},{17,25},{25,17},{2,10},{10... | collective-permute-start | bytes 9437192 | tf_op jit(solution)/shard_map/ppermute | solution.py:254
  499.2 109.9 %collective-permute-start.29 = (bf16[2048,1024]{1,0:T(8,128)(2,1)}, bf16[2048,1024]{1,0:T(8,128)(2,1)}, u32[]{:S(2)}, u32[]{:S(2)}) collective-permute-start(bf16[2048,1024]{1,0:T(8,128)(2,1)} %convolution_convert_fusion.2), channel_id=1, source_target_pairs={{0,16},{8,24},{16,0},{24,8},{1,17},{9,25},{17,1},{25,9},{2,18},{10... | collective-permute-start | bytes 12582920 | tf_op jit(solution)/shard_map/ppermute | solution.py:254
  499.8 110.8 %collective-permute-start.28 = (bf16[2048,1024]{1,0:T(8,128)(2,1)}, bf16[2048,1024]{1,0:T(8,128)(2,1)}, u32[]{:S(2)}, u32[]{:S(2)}) collective-permute-start(bf16[2048,1024]{1,0:T(8,128)(2,1)} %convolution_convert_fusion.3), channel_id=1, source_target_pairs={{0,8},{8,0},{16,24},{24,16},{1,9},{9,1},{17,25},{25,17},{2,10},{10... | collective-permute-start | bytes 12582920 | tf_op jit(solution)/shard_map/ppermute | solution.py:254
  623.4 70.0 %collective-permute-start.31 = (bf16[2048,512]{1,0:T(8,128)(2,1)}, bf16[2048,512]{1,0:T(8,128)(2,1)}, u32[]{:S(2)}, u32[]{:S(2)}) collective-permute-start(bf16[2048,512]{1,0:T(8,128)(2,1)} %slice_add_fusion.2), channel_id=1, source_target_pairs={{0,16},{8,24},{16,0},{24,8},{1,17},{9,25},{17,1},{25,9},{2,18},{10... | collective-permute-start | bytes 6291464 | tf_op jit(solution)/shard_map/ppermute | solution.py:254
  624.0 69.4 %collective-permute-start.30 = (bf16[2048,512]{1,0:T(8,128)(2,1)}, bf16[2048,512]{1,0:T(8,128)(2,1)}, u32[]{:S(2)}, u32[]{:S(2)}) collective-permute-start(bf16[2048,512]{1,0:T(8,128)(2,1)} %slice_add_fusion.3), channel_id=1, source_target_pairs={{0,8},{8,0},{16,24},{24,16},{1,9},{9,1},{17,25},{25,17},{2,10},{10... | collective-permute-start | bytes 6291464 | tf_op jit(solution)/shard_map/ppermute | solution.py:254
  646.7 127.7 %collective-permute-start.37 = (bf16[1024,2048]{1,0:T(8,128)(2,1)}, bf16[1024,2048]{1,0:T(8,128)(2,1)}, u32[]{:S(2)}, u32[]{:S(2)}) collective-permute-start(bf16[1024,2048]{1,0:T(8,128)(2,1)} %fusion.29), channel_id=1, source_target_pairs={{0,8},{8,0},{16,24},{24,16},{1,9},{9,1},{17,25},{25,17},{2,10},{10... | collective-permute-start | bytes 12582920 | tf_op jit(solution)/shard_map/ppermute | solution.py:254
  656.4 118.0 %collective-permute-start.38 = (bf16[1024,2048]{1,0:T(8,128)(2,1)}, bf16[1024,2048]{1,0:T(8,128)(2,1)}, u32[]{:S(2)}, u32[]{:S(2)}) collective-permute-start(bf16[1024,2048]{1,0:T(8,128)(2,1)} %fusion.28), channel_id=1, source_target_pairs={{0,16},{8,24},{16,0},{24,8},{1,17},{9,25},{17,1},{25,9},{2,18},{10... | collective-permute-start | bytes 12582920 | tf_op jit(solution)/shard_map/ppermute | solution.py:254
  729.7 305.4 %reduce-scatter.9.cloned.1.call-start = ((), (), s32[]{:S(2)}) async-start(), calls=%async_computation.6 | async-start | bytes 5242880 | tf_op jit(solution)/shard_map/reduce_scatter | solution.py:349
  734.1 148.2 %collective-permute-start.49 = (bf16[512,1024]{1,0:T(8,128)(2,1)}, bf16[512,1024]{1,0:T(8,128)(2,1)}, u32[]{:S(2)}, u32[]{:S(2)}) collective-permute-start(bf16[512,1024]{1,0:T(8,128)(2,1)} %fusion.101), channel_id=1, source_target_pairs={{0,8},{8,0},{16,24},{24,16},{1,9},{9,1},{17,25},{25,17},{2,10},{10... | collective-permute-start | bytes 3145736 | tf_op jit(solution)/shard_map/ppermute | solution.py:254
  756.7 100.6 %collective-permute-start.33 = (bf16[256,2048]{1,0:T(8,128)(2,1)}, bf16[256,2048]{1,0:T(8,128)(2,1)}, u32[]{:S(2)}, u32[]{:S(2)}) collective-permute-start(bf16[256,2048]{1,0:T(8,128)(2,1)} %get-tuple-element.187), channel_id=1, source_target_pairs={{0,0},{2,1},{4,2},{6,3},{1,4},{3,5},{5,6},{7,7},{8,8},{10,9},{12,1... | collective-permute-start | bytes 3145736 | tf_op jit(solution)/shard_map/ppermute | solution.py:282
  766.3 91.9 %collective-permute-start.34 = (bf16[256,2048]{1,0:T(8,128)(2,1)}, bf16[256,2048]{1,0:T(8,128)(2,1)}, u32[]{:S(2)}, u32[]{:S(2)}) collective-permute-start(bf16[256,2048]{1,0:T(8,128)(2,1)} %get-tuple-element.188), channel_id=1, source_target_pairs={{2,0},{0,1},{6,2},{4,3},{3,4},{1,5},{7,6},{5,7},{10,8},{8,9},{14,1... | collective-permute-start | bytes 3145736 | tf_op jit(solution)/shard_map/ppermute | solution.py:282
  777.7 83.7 %collective-permute-start.48 = (bf16[1024,1024]{1,0:T(8,128)(2,1)}, bf16[1024,1024]{1,0:T(8,128)(2,1)}, u32[]{:S(2)}, u32[]{:S(2)}) collective-permute-start(bf16[1024,1024]{1,0:T(8,128)(2,1)} %slice_add_fusion), channel_id=1, source_target_pairs={{0,16},{8,24},{16,0},{24,8},{1,17},{9,25},{17,1},{25,9},{2,18},{10... | collective-permute-start | bytes 6291464 | tf_op jit(solution)/shard_map/ppermute | solution.py:254
  782.1 79.3 %collective-permute-start.47 = (bf16[1024,1024]{1,0:T(8,128)(2,1)}, bf16[1024,1024]{1,0:T(8,128)(2,1)}, u32[]{:S(2)}, u32[]{:S(2)}) collective-permute-start(bf16[1024,1024]{1,0:T(8,128)(2,1)} %slice_add_fusion.1), channel_id=1, source_target_pairs={{0,8},{8,0},{16,24},{24,16},{1,9},{9,1},{17,25},{25,17},{2,10},{10... | collective-permute-start | bytes 6291464 | tf_op jit(solution)/shard_map/ppermute | solution.py:254
  871.5 213.4 %reduce-scatter.7.cloned.1.call-start = ((), (), s32[]{:S(2)}) async-start(), calls=%async_computation.5 | async-start | bytes 1310720 | tf_op jit(solution)/shard_map/reduce_scatter | solution.py:349
  874.8 71.3 %collective-permute-start.45 = (bf16[1024,1536]{1,0:T(8,128)(2,1)}, bf16[1024,1536]{1,0:T(8,128)(2,1)}, u32[]{:S(2)}, u32[]{:S(2)}) collective-permute-start(bf16[1024,1536]{1,0:T(8,128)(2,1)} %convolution_convert_fusion.1), channel_id=1, source_target_pairs={{0,8},{8,0},{16,24},{24,16},{1,9},{9,1},{17,25},{25,17},{2,10},{10... | collective-permute-start | bytes 9437192 | tf_op jit(solution)/shard_map/ppermute | solution.py:254
  875.3 72.0 %collective-permute-start.46 = (bf16[1024,1536]{1,0:T(8,128)(2,1)}, bf16[1024,1536]{1,0:T(8,128)(2,1)}, u32[]{:S(2)}, u32[]{:S(2)}) collective-permute-start(bf16[1024,1536]{1,0:T(8,128)(2,1)} %convolution_convert_fusion), channel_id=1, source_target_pairs={{0,16},{8,24},{16,0},{24,8},{1,17},{9,25},{17,1},{25,9},{2,18},{10... | collective-permute-start | bytes 9437192 | tf_op jit(solution)/shard_map/ppermute | solution.py:254
  904.5 87.8 %collective-permute-start.41 = (bf16[256,2048]{1,0:T(8,128)(2,1)S(1)}, bf16[256,2048]{1,0:T(8,128)(2,1)S(1)}, u32[]{:S(2)}, u32[]{:S(2)}) collective-permute-start(bf16[256,2048]{1,0:T(8,128)(2,1)S(1)} %get-tuple-element.184), channel_id=1, source_target_pairs={{2,0},{0,1},{6,2},{4,3},{3,4},{1,5},{7,6},{5,7},{10,8},{8,9},{14,1... | collective-permute-start | bytes 3145736 | tf_op jit(solution)/shard_map/ppermute | solution.py:282
  910.6 83.4 %collective-permute-start.56 = (bf16[512,512]{1,0:T(8,128)(2,1)S(1)}, bf16[512,512]{1,0:T(8,128)(2,1)S(1)}, u32[]{:S(2)}, u32[]{:S(2)}) collective-permute-start(bf16[512,512]{1,0:T(8,128)(2,1)S(1)} %fusion.123), channel_id=1, source_target_pairs={{0,8},{8,0},{16,24},{24,16},{1,9},{9,1},{17,25},{25,17},{2,10},{10... | collective-permute-start | bytes 1572872 | tf_op jit(solution)/shard_map/ppermute | solution.py:254
  950.1 53.3 %collective-permute-start.52 = (bf16[1024,768]{1,0:T(8,128)(2,1)}, bf16[1024,768]{1,0:T(8,128)(2,1)}, u32[]{:S(2)}, u32[]{:S(2)}) collective-permute-start(bf16[1024,768]{1,0:T(8,128)(2,1)} %slice_add_fusion.4), channel_id=1, source_target_pairs={{0,16},{8,24},{16,0},{24,8},{1,17},{9,25},{17,1},{25,9},{2,18},{10... | collective-permute-start | bytes 4718600 | tf_op jit(solution)/shard_map/ppermute | solution.py:254
  999.1 113.4 %reduce-scatter.5.cloned.1.call-start = ((), (), s32[]{:S(2)}) async-start(), calls=%async_computation.4 | async-start | bytes 3932160 | tf_op jit(solution)/shard_map/reduce_scatter | solution.py:349
  (137 other events, 3032.4 us)
Sparse Core Ops, SparseCore 0:
  52.0 84.3 all-gather.8
  138.6 26.6 all-gather.10
  167.4 80.1 all-gather.12
  249.0 79.2 all-gather.14
  729.8 108.5 reduce-scatter.10
  871.6 104.3 reduce-scatter.8
  999.2 25.7 reduce-scatter.6
  1027.9 58.9 reduce-scatter.4

commit v7 on v6

--- a/solution.py
+++ b/solution.py
@@ -648,9 +648,9 @@
 
     packed = packed + swap(packed)
     if square:
-        out_part = out_red.third((*qkv_red.sent, grad_in))
+        out_part = out_red.third(qkv_red.sent)
         fc2_first = spread_first(after(fc2_part, (qkv_red.sent, out_red.mine)))
-        qkv_part = qkv_red.third()
+        qkv_part = qkv_red.third((grad_in,))
         packed = sum_plane(packed, [0])
         fc1_first = spread_first(after(fc1_part, (fc2_first[1:], qkv_red.mine, packed)))
         fc2_pair = spread_second(*fc2_first)

time: 1200 us -> 1210 us (level)
    ppermute x6, starting transfers between devices: 21.6 us -> 9.06 us  [along(): lax.ppermute(value, 'sh', [(i, (i + hop) % shards) for i in range(shards)])]
    unnamed x220 -> x230, local copies, waits for them, and re-layouts: 44.2 us -> 43.8 us
  transfers between devices with their start and end apart: 86 -> 86, of which waited for: 33 -> 36; matrix products, arithmetic and copies ran while one was open for 38% -> 39% of each run, Pallas kernels for 15% -> 15%
where the time goes in v7:
time: 1210 us; the launch traced here: 1190 us
  waiting for transfers between devices  406 us (34%)
  matrix products  297 us (25%)
  Pallas kernels  194 us (16%)
  local copies, waits for them, and re-layouts  94.5 us (8%)
  other arithmetic  93.7 us (8%)
  starting transfers between devices  93.5 us (8%)
  between operations  16.4 us (1%)
    ppermute x50, waiting for transfers between devices, plane(): return lax.ppermute(value, 'ch', [(i, i ^ bit) for i in range(chips)])  267 us
    pallas_call x8, Pallas kernels, place(): pl.pallas_call(body, grid_spec=pltpu.PrefetchScalarGridSpec(num_scalar_pr...  139 us
    dot_general x24, matrix products, cross_rows(): lax.dot_general(left_side, right_side, (((0,), (0,)), ((), ())), preferre...  123 us
    dot_general x6, matrix products, times_rows(): lax.dot_general(left_side, right_side, (((1,), (1,)), ((), ())), preferre...  92.7 us
    dot_general x6, matrix products, dot(): return jnp.dot(left_side, right_side, preferred_element_type=F32)  80.5 us
    all_gather x4, waiting for transfers between devices, gather_shards(): return lax.all_gather(piece, 'sh')  80.1 us
    ppermute x50, starting transfers between devices, plane(): return lax.ppermute(value, 'ch', [(i, i ^ bit) for i in range(chips)])  52.5 us
    ppermute x4, waiting for transfers between devices, tokens_out(): lax.ppermute(lax.dynamic_index_in_dim(value, (turn + micro) % 2, 0, False...  46.5 us
  transfers between devices with their start and end apart: 86, of which 36 were waited for; matrix products, arithmetic and copies ran while one was open for 39% of the time, Pallas kernels for 15%

profile of v7, /device:TPU:0, one launch (start us, length us, event | category | flops | bytes accessed | tf_op | source)
XLA Modules:
  0.0 1193.9 jit_solution(17842508356269903252)
XLA Ops:
  56.3 80.1 %all-gather.9.cloned.1.call-done = bf16[2048,768]{1,0:T(8,128)(2,1)} async-done(((bf16[512,768]{1,0:T(8,128)(2,1)}), bf16[2048,768]{1,0:T(8,128)(2,1)}) %all-gather.9.cloned.1.call-update) | async-done | bytes 3145744 | tf_op jit(solution)/shard_map/all_gather | solution.py:293
  146.5 46.4 %collective-permute-done.8.refs_3_ = bf16[1536,768]{1,0:T(8,128)(2,1)} collective-permute-done((bf16[1536,768]{1,0:T(8,128)(2,1)}, bf16[1536,768]{1,0:T(8,128)(2,1)}, u32[]{:S(2)}, u32[]{:S(2)}) %collective-permute-start.8) | collective-permute-done | bytes 2359328 | tf_op jit(solution)/shard_map/ppermute | solution.py:254
  207.8 34.8 %collective-permute-done.12.refs_3_ = bf16[768,512]{1,0:T(8,128)(2,1)} collective-permute-done((bf16[768,512]{1,0:T(8,128)(2,1)S(1)}, bf16[768,512]{1,0:T(8,128)(2,1)}, u32[]{:S(2)}, u32[]{:S(2)}) %collective-permute-start.12) | collective-permute-done | bytes 786464 | tf_op jit(solution)/shard_map/ppermute | solution.py:254
  248.6 22.7 %shard_map.631 = bf16[2048,3072]{1,0:T(8,128)(2,1)} custom-call(s32[14,32]{1,0:T(8,128)} %get-tuple-element.224.table_ref, bf16[512,3072]{1,0:T(8,128)(2,1)} %get-tuple-element.160.refs_0_, bf16[1536,768]{1,0:T(8,128)(2,1)} %pad_maximum_fusion.26.refs_1_, bf16[1536,768]{1,0:T(8,128)(2,1)} %collective-permute-done.7.refs_2_, ...), custom_call_target="tpu_custom_call" | custom-call | tf_op jit(solution)/shard_map/pallas_call | solution.py:77
  271.3 18.5 %add_convert_fusion.q_ref.k_ref.v_ref = bf16[1024,3072]{1,0:T(8,128)(2,1)} fusion(bf16[2048,3072]{1,0:T(8,128)(2,1)} %shard_map.631, f32[3072]{0:T(1024)S(1)} %pad_maximum_fusion.42, bf16[512,2048]{1,0:T(8,128)(2,1)} %collective-permute-done.6, bf16[512,2048]{1,0:T(8,128)(2,1)} %fusion.14), kind=kOutput, calls=%fused_computation.10 | convolution fusion | flops 12899581952 | bytes 23080960 | tf_op jit(solution)/shard_map/dot_general | solution.py:30
  298.1 20.5 %shard_map.632 = bf16[1024,1024]{1,0:T(8,128)(2,1)} custom-call(s32[2]{0:T(128)} %pad_add_fusion.10.scal_ref, bf16[1024,3072]{1,0:T(8,128)(2,1)} %add_convert_fusion.q_ref.k_ref.v_ref, bf16[1024,3072]{1,0:T(8,128)(2,1)} %add_convert_fusion.q_ref.k_ref.v_ref, bf16[1024,3072]{1,0:T(8,128)(2,1)} %add_convert_fusion.q_ref.k_ref.v_ref), custom_call_target="tpu_custom_call" | custom-call | tf_op jit(solution)/shard_map/pallas_call | solution.py:172
  318.6 19.3 %shard_map.633 = bf16[1024,2048]{1,0:T(8,128)(2,1)} custom-call(s32[14,32]{1,0:T(8,128)} %get-tuple-element.223.table_ref, bf16[512,2048]{1,0:T(8,128)(2,1)} %refs_0_.3, bf16[768,512]{1,0:T(8,128)(2,1)} %copy-done.19, bf16[768,512]{1,0:T(8,128)(2,1)} %collective-permute-done.11.refs_2_, bf16[768,512]{1,0:T(8,128)(2,1)} %collective-permute-done.12.refs_3_, ...), custom_call_target="tpu_custom_call" | custom-call | tf_op jit(solution)/shard_map/pallas_call | solution.py:77
  343.1 17.8 %collective-permute-done.17.refs_3_ = bf16[1536,1024]{1,0:T(8,128)(2,1)} collective-permute-done((bf16[1536,1024]{1,0:T(8,128)(2,1)}, bf16[1536,1024]{1,0:T(8,128)(2,1)}, u32[]{:S(2)}, u32[]{:S(2)}) %collective-permute-start.17) | collective-permute-done | bytes 3145760 | tf_op jit(solution)/shard_map/ppermute | solution.py:254
  381.3 17.6 %collective-permute-done.19.refs_4_ = bf16[768,1024]{1,0:T(8,128)(2,1)} collective-permute-done((bf16[768,1024]{1,0:T(8,128)(2,1)}, bf16[768,1024]{1,0:T(8,128)(2,1)}, u32[]{:S(2)}, u32[]{:S(2)}) %collective-permute-start.19) | collective-permute-done | bytes 1572896 | tf_op jit(solution)/shard_map/ppermute | solution.py:254
  409.5 25.1 %shard_map.634 = bf16[2048,4096]{1,0:T(8,128)(2,1)} custom-call(s32[14,32]{1,0:T(8,128)} %get-tuple-element.222.table_ref, bf16[512,8192]{1,0:T(8,128)(2,1)} %refs_0_.4, bf16[1536,1024]{1,0:T(8,128)(2,1)} %pad_maximum_fusion.19.refs_1_, bf16[1536,1024]{1,0:T(8,128)(2,1)} %collective-permute-done.16.refs_2_, ...), custom_call_target="tpu_custom_call" | custom-call | tf_op jit(solution)/shard_map/pallas_call | solution.py:77
  435.6 12.0 %collective-permute-start.23 = (bf16[512,2048]{1,0:T(8,128)(2,1)S(1)}, bf16[512,2048]{1,0:T(8,128)(2,1)}, u32[]{:S(2)}, u32[]{:S(2)}) collective-permute-start(bf16[512,2048]{1,0:T(8,128)(2,1)S(1)} %pad_maximum_fusion.32), channel_id=1, source_target_pairs={{0,4},{4,0},{1,5},{5,1},{2,6},{6,2},{3,7},{7,3},{8,12},{12,8},{9,1... | collective-permute-start | bytes 6291464 | tf_op jit(solution)/shard_map/ppermute | solution.py:257
  447.6 27.8 %multiply_convert_fusion.1 = (bf16[1024,4096]{1,0:T(8,128)(2,1)}, f32[1024,4096]{1,0:T(8,128)}) fusion(f32[4096]{0:T(1024)S(1)} %bitcast.177, bf16[2048,4096]{1,0:T(8,128)(2,1)} %shard_map.634, bf16[512,2048]{1,0:T(8,128)(2,1)} %collective-permute-done.18, bf16[512,2048]{1,0:T(8,128)(2,1)} %add_convert_fusion.6), kind=kOutput, calls=%fused_computation.8 | convolution fusion | flops 17213423616 | bytes 46153728 | tf_op jit(solution)/shard_map/dot_general | solution.py:30
  508.4 10.5 collective-permute-done.26.refs_4_
  520.6 24.7 %shard_map.635 = bf16[4096,2048]{1,0:T(8,128)(2,1)} custom-call(s32[14,32]{1,0:T(8,128)} %get-tuple-element.223.table_ref, bf16[2048,2048]{1,0:T(8,128)(2,1)} %refs_0_.5, bf16[3072,512]{1,0:T(8,128)(2,1)} %pad_maximum_fusion.20.refs_1_, bf16[3072,512]{1,0:T(8,128)(2,1)} %collective-permute-done.24.refs_2_, ...), custom_call_target="tpu_custom_call" | custom-call | tf_op jit(solution)/shard_map/pallas_call | solution.py:77
  545.2 29.3 %convert_reduce_fusion = (f32[4096]{0:T(1024)S(1)}, bf16[1024,4096]{1,0:T(8,128)(2,1)}) fusion(f32[1024,4096]{1,0:T(8,128)} %get-tuple-element.231, f32[4096]{0:T(1024)S(1)} %bitcast.178, bf16[1024,2048]{1,0:T(8,128)(2,1)} %copy-done.14, bf16[4096,2048]{1,0:T(8,128)(2,1)} %shard_map.635), kind=kOutput, calls=%fused_computation.6 | convolution fusion | flops 17242779648 | bytes 46170112 | tf_op jit(solution)/shard_map/dot_general | solution.py:38
  575.2 33.5 %collective-permute-done.29 = bf16[2048,1024]{1,0:T(8,128)(2,1)} collective-permute-done((bf16[2048,1024]{1,0:T(8,128)(2,1)}, bf16[2048,1024]{1,0:T(8,128)(2,1)}, u32[]{:S(2)}, u32[]{:S(2)}) %collective-permute-start.29) | collective-permute-done | bytes 4194336 | tf_op jit(solution)/shard_map/ppermute | solution.py:254
  624.5 13.5 %fusion.70 = bf16[512,2048]{1,0:T(8,128)(2,1)} fusion(bf16[2048,4096]{1,0:T(8,128)(2,1)} %shard_map.634, bf16[1024,4096]{1,0:T(8,128)(2,1)S(1)} %bitcast.152), kind=kOutput, calls=%fused_computation.116 | convolution fusion | flops 8590983168 | bytes 23068672 | tf_op jit(solution)/shard_map/dot_general | solution.py:38
  668.5 17.8 %multiply_reduce_fusion = (f32[2048]{0:T(1024)S(1)}, f32[512]{0:T(512)S(1)}, f32[2048]{0:T(1024)S(1)}, f32[512,2048]{1,0:T(8,128)}) fusion(f32[512,2048]{1,0:T(8,128)} %convert_add_fusion, f32[512]{0:T(512)S(1)} %copy-done.54, f32[512]{0:T(512)S(1)} %copy-done.46, f32[2048]{0:T(1024)S(1)} %bitcast.168, bf16[512,2048]{1,0:T(8,128)(2,1)} %collective-permute-done.35, ...), kind=kOutput, calls=%fused_computation.59 | convolution fusion | flops 8600416256 | bytes 31488000 | tf_op jit(solution)/shard_map/dot_general | solution.py:38
  706.9 11.9 fusion.67
  746.2 12.8 %add_add_fusion.2 = bf16[512,2048]{1,0:T(8,128)(2,1)S(1)} fusion(f32[512,2048]{1,0:T(8,128)S(1)} %copy-done.3, bf16[512,2048]{1,0:T(8,128)(2,1)} %collective-permute-done.32, bf16[4096,2048]{1,0:T(8,128)(2,1)} %shard_map.635, bf16[1024,4096]{1,0:T(8,128)(2,1)S(1)} %bitcast.188, f32[2048]{0:T(1024)S(1)} %bitcast.181), kind=kOutput, calls=%fused_computation.73 | convolution fusion | flops 8595177472 | bytes 29368320 | tf_op jit(solution)/shard_map/dot_general | solution.py:30
  779.6 34.3 %shard_map.636 = (bf16[1024,1024]{1,0:T(8,128)(2,1)}, bf16[1024,1024]{1,0:T(8,128)(2,1)}, bf16[1024,1024]{1,0:T(8,128)(2,1)}) custom-call(s32[2]{0:T(128)} %pad_add_fusion.10.scal_ref, bf16[1024,3072]{1,0:T(8,128)(2,1)} %add_convert_fusion.q_ref.k_ref.v_ref, bf16[1024,3072]{1,0:T(8,128)(2,1)} %add_convert_fusion.q_ref.k_ref.v_ref, ...), custom_call_target="tpu_custom_call" | custom-call | tf_op jit(solution)/shard_map/pallas_call | solution.py:188
  843.4 11.6 fusion.52
  890.2 12.8 %fusion.192 = (f32[2048]{0:T(1024)S(1)}, f32[512]{0:T(512)S(1)}, f32[512,2048]{1,0:T(8,128)}) fusion(f32[2048]{0:T(1024)S(1)} %bitcast.162, f32[512]{0:T(512)S(1)} %copy-done.42, bf16[512,2048]{1,0:T(8,128)(2,1)S(1)} %copy-done.1, bf16[512,2048]{1,0:T(8,128)(2,1)} %collective-permute-done.39, bf16[2048,3072]{1,0:T(8,128)(2,1)} %shard_map.631, ...), kind=kOutput, calls=%fused_computation.376 | convolution fusion | flops 6450836992 | bytes 24137728 | tf_op jit(solution)/shard_map/dot_general | solution.py:38
  916.2 9.4 collective-permute-start.40
  929.8 18.0 %collective-permute-done.46 = bf16[1024,1536]{1,0:T(8,128)(2,1)} collective-permute-done((bf16[1024,1536]{1,0:T(8,128)(2,1)}, bf16[1024,1536]{1,0:T(8,128)(2,1)}, u32[]{:S(2)}, u32[]{:S(2)}) %collective-permute-start.46) | collective-permute-done | bytes 3145760 | tf_op jit(solution)/shard_map/ppermute | solution.py:254
  964.6 46.5 %collective-permute-done.41 = bf16[256,2048]{1,0:T(8,128)(2,1)} collective-permute-done((bf16[256,2048]{1,0:T(8,128)(2,1)}, bf16[256,2048]{1,0:T(8,128)(2,1)}, u32[]{:S(2)}, u32[]{:S(2)}) %collective-permute-start.41) | collective-permute-done | bytes 1048608 | tf_op jit(solution)/shard_map/ppermute | solution.py:282
  1025.9 19.6 %collective-permute-done.43 = f32[4,6144]{1,0:T(4,128)S(1)} collective-permute-done((f32[4,6144]{1,0:T(4,128)S(1)}, f32[4,6144]{1,0:T(4,128)S(1)}, u32[]{:S(2)}, u32[]{:S(2)}) %collective-permute-start.43) | collective-permute-done | bytes 98336 | tf_op jit(solution)/shard_map/ppermute | solution.py:254
  1054.6 14.9 %collective-permute-done.62 = bf16[512,512]{1,0:T(8,128)(2,1)S(1)} collective-permute-done((bf16[512,512]{1,0:T(8,128)(2,1)S(1)}, bf16[512,512]{1,0:T(8,128)(2,1)S(1)}, u32[]{:S(2)}, u32[]{:S(2)}) %collective-permute-start.62) | collective-permute-done | bytes 524320 | tf_op jit(solution)/shard_map/ppermute | solution.py:254
  1079.3 9.1 collective-permute-done.68
  1111.0 11.7 shard_map.637
  1124.5 11.7 shard_map.638
  1170.0 16.6 %shard_map.640 = f32[512,6144]{1,0:T(8,128)} custom-call(s32[6,24]{1,0:T(8,128)} %pad_add_fusion.8.table_ref, bf16[2048,768]{1,0:T(8,128)(2,1)} %copy-done.15, bf16[2048,768]{1,0:T(8,128)(2,1)} %collective-permute-done.77.refs_1_), custom_call_target="tpu_custom_call" | custom-call | tf_op jit(solution)/shard_map/pallas_call | solution.py:77
  (571 shorter events, 464.6 us)
Async XLA Ops:
  7.2 129.3 %all-gather.9.cloned.1.call-start = ((), (), s32[]{:S(2)}) async-start(), calls=%async_computation.8 | async-start | bytes 3932160 | tf_op jit(solution)/shard_map/all_gather | solution.py:293
  51.9 151.4 %all-gather.11.cloned.1.call-start = ((), (), s32[]{:S(2)}) async-start(), calls=%async_computation.9 | async-start | bytes 1310720 | tf_op jit(solution)/shard_map/all_gather | solution.py:293
  53.9 235.9 %all-gather.13.cloned.1.call-start = ((), (), s32[]{:S(2)}) async-start(), calls=%async_computation.10 | async-start | bytes 5242880 | tf_op jit(solution)/shard_map/all_gather | solution.py:293
  56.2 317.1 %all-gather.15.cloned.1.call-start = ((), (), s32[]{:S(2)}) async-start(), calls=%async_computation.11 | async-start | bytes 5242880 | tf_op jit(solution)/shard_map/all_gather | solution.py:293
  146.5 124.8 %collective-permute-start.6 = (bf16[512,2048]{1,0:T(8,128)(2,1)}, bf16[512,2048]{1,0:T(8,128)(2,1)}, u32[]{:S(2)}, u32[]{:S(2)}) collective-permute-start(bf16[512,2048]{1,0:T(8,128)(2,1)} %fusion.14), channel_id=1, source_target_pairs={{0,4},{4,0},{1,5},{5,1},{2,6},{6,2},{3,7},{7,3},{8,12},{12,8},{9,1... | collective-permute-start | bytes 6291464 | tf_op jit(solution)/shard_map/ppermute | solution.py:257
  207.5 813.2 %reduce-scatter.11.cloned.1.call-start = ((), (), s32[]{:S(2)}) async-start(), calls=%async_computation.7 | async-start | bytes 5242880 | tf_op jit(solution)/shard_map/reduce_scatter | solution.py:349
  293.9 67.0 %collective-permute-start.17 = (bf16[1536,1024]{1,0:T(8,128)(2,1)}, bf16[1536,1024]{1,0:T(8,128)(2,1)}, u32[]{:S(2)}, u32[]{:S(2)}) collective-permute-start(bf16[1536,1024]{1,0:T(8,128)(2,1)} %pad_maximum_fusion.19.refs_1_), channel_id=1, source_target_pairs={{0,16},{8,24},{16,0},{24,8},{1,17},{9,25},{17,1},{25,9},{2,18},{10... | collective-permute-start | bytes 9437192 | tf_op jit(solution)/shard_map/ppermute | solution.py:254
  294.4 66.8 %collective-permute-start.16 = (bf16[1536,1024]{1,0:T(8,128)(2,1)}, bf16[1536,1024]{1,0:T(8,128)(2,1)}, u32[]{:S(2)}, u32[]{:S(2)}) collective-permute-start(bf16[1536,1024]{1,0:T(8,128)(2,1)} %pad_maximum_fusion.19.refs_1_), channel_id=1, source_target_pairs={{0,8},{8,0},{16,24},{24,16},{1,9},{9,1},{17,25},{25,17},{2,10},{10... | collective-permute-start | bytes 9437192 | tf_op jit(solution)/shard_map/ppermute | solution.py:254
  381.3 66.3 %collective-permute-start.18 = (bf16[512,2048]{1,0:T(8,128)(2,1)}, bf16[512,2048]{1,0:T(8,128)(2,1)}, u32[]{:S(2)}, u32[]{:S(2)}) collective-permute-start(bf16[512,2048]{1,0:T(8,128)(2,1)} %add_convert_fusion.6), channel_id=1, source_target_pairs={{0,4},{4,0},{1,5},{5,1},{2,6},{6,2},{3,7},{7,3},{8,12},{12,8},{9,1... | collective-permute-start | bytes 6291464 | tf_op jit(solution)/shard_map/ppermute | solution.py:257
  407.9 69.6 %collective-permute-start.25 = (bf16[3072,512]{1,0:T(8,128)(2,1)}, bf16[3072,512]{1,0:T(8,128)(2,1)}, u32[]{:S(2)}, u32[]{:S(2)}) collective-permute-start(bf16[3072,512]{1,0:T(8,128)(2,1)} %pad_maximum_fusion.20.refs_1_), channel_id=1, source_target_pairs={{0,16},{8,24},{16,0},{24,8},{1,17},{9,25},{17,1},{25,9},{2,18},{10... | collective-permute-start | bytes 9437192 | tf_op jit(solution)/shard_map/ppermute | solution.py:254
  408.6 69.9 %collective-permute-start.24 = (bf16[3072,512]{1,0:T(8,128)(2,1)}, bf16[3072,512]{1,0:T(8,128)(2,1)}, u32[]{:S(2)}, u32[]{:S(2)}) collective-permute-start(bf16[3072,512]{1,0:T(8,128)(2,1)} %pad_maximum_fusion.20.refs_1_), channel_id=1, source_target_pairs={{0,8},{8,0},{16,24},{24,16},{1,9},{9,1},{17,25},{25,17},{2,10},{10... | collective-permute-start | bytes 9437192 | tf_op jit(solution)/shard_map/ppermute | solution.py:254
  499.1 109.6 %collective-permute-start.29 = (bf16[2048,1024]{1,0:T(8,128)(2,1)}, bf16[2048,1024]{1,0:T(8,128)(2,1)}, u32[]{:S(2)}, u32[]{:S(2)}) collective-permute-start(bf16[2048,1024]{1,0:T(8,128)(2,1)} %convolution_convert_fusion.2), channel_id=1, source_target_pairs={{0,16},{8,24},{16,0},{24,8},{1,17},{9,25},{17,1},{25,9},{2,18},{10... | collective-permute-start | bytes 12582920 | tf_op jit(solution)/shard_map/ppermute | solution.py:254
  499.8 110.7 %collective-permute-start.28 = (bf16[2048,1024]{1,0:T(8,128)(2,1)}, bf16[2048,1024]{1,0:T(8,128)(2,1)}, u32[]{:S(2)}, u32[]{:S(2)}) collective-permute-start(bf16[2048,1024]{1,0:T(8,128)(2,1)} %convolution_convert_fusion.3), channel_id=1, source_target_pairs={{0,8},{8,0},{16,24},{24,16},{1,9},{9,1},{17,25},{25,17},{2,10},{10... | collective-permute-start | bytes 12582920 | tf_op jit(solution)/shard_map/ppermute | solution.py:254
  623.3 69.9 %collective-permute-start.31 = (bf16[2048,512]{1,0:T(8,128)(2,1)}, bf16[2048,512]{1,0:T(8,128)(2,1)}, u32[]{:S(2)}, u32[]{:S(2)}) collective-permute-start(bf16[2048,512]{1,0:T(8,128)(2,1)} %slice_add_fusion.2), channel_id=1, source_target_pairs={{0,16},{8,24},{16,0},{24,8},{1,17},{9,25},{17,1},{25,9},{2,18},{10... | collective-permute-start | bytes 6291464 | tf_op jit(solution)/shard_map/ppermute | solution.py:254
  623.9 69.3 %collective-permute-start.30 = (bf16[2048,512]{1,0:T(8,128)(2,1)}, bf16[2048,512]{1,0:T(8,128)(2,1)}, u32[]{:S(2)}, u32[]{:S(2)}) collective-permute-start(bf16[2048,512]{1,0:T(8,128)(2,1)} %slice_add_fusion.3), channel_id=1, source_target_pairs={{0,8},{8,0},{16,24},{24,16},{1,9},{9,1},{17,25},{25,17},{2,10},{10... | collective-permute-start | bytes 6291464 | tf_op jit(solution)/shard_map/ppermute | solution.py:254
  646.6 125.5 %collective-permute-start.37 = (bf16[1024,2048]{1,0:T(8,128)(2,1)}, bf16[1024,2048]{1,0:T(8,128)(2,1)}, u32[]{:S(2)}, u32[]{:S(2)}) collective-permute-start(bf16[1024,2048]{1,0:T(8,128)(2,1)} %fusion.29), channel_id=1, source_target_pairs={{0,8},{8,0},{16,24},{24,16},{1,9},{9,1},{17,25},{25,17},{2,10},{10... | collective-permute-start | bytes 12582920 | tf_op jit(solution)/shard_map/ppermute | solution.py:254
  656.3 115.8 %collective-permute-start.38 = (bf16[1024,2048]{1,0:T(8,128)(2,1)}, bf16[1024,2048]{1,0:T(8,128)(2,1)}, u32[]{:S(2)}, u32[]{:S(2)}) collective-permute-start(bf16[1024,2048]{1,0:T(8,128)(2,1)} %fusion.28), channel_id=1, source_target_pairs={{0,16},{8,24},{16,0},{24,8},{1,17},{9,25},{17,1},{25,9},{2,18},{10... | collective-permute-start | bytes 12582920 | tf_op jit(solution)/shard_map/ppermute | solution.py:254
  734.3 311.2 %reduce-scatter.9.cloned.1.call-start = ((), (), s32[]{:S(2)}) async-start(), calls=%async_computation.6 | async-start | bytes 5242880 | tf_op jit(solution)/shard_map/reduce_scatter | solution.py:349
  738.8 144.9 %collective-permute-start.49 = (bf16[512,1024]{1,0:T(8,128)(2,1)}, bf16[512,1024]{1,0:T(8,128)(2,1)}, u32[]{:S(2)}, u32[]{:S(2)}) collective-permute-start(bf16[512,1024]{1,0:T(8,128)(2,1)} %fusion.101), channel_id=1, source_target_pairs={{0,8},{8,0},{16,24},{24,16},{1,9},{9,1},{17,25},{25,17},{2,10},{10... | collective-permute-start | bytes 3145736 | tf_op jit(solution)/shard_map/ppermute | solution.py:254
  760.5 94.5 %collective-permute-start.33 = (bf16[256,2048]{1,0:T(8,128)(2,1)}, bf16[256,2048]{1,0:T(8,128)(2,1)S(1)}, u32[]{:S(2)}, u32[]{:S(2)}) collective-permute-start(bf16[256,2048]{1,0:T(8,128)(2,1)} %get-tuple-element.187), channel_id=1, source_target_pairs={{0,0},{2,1},{4,2},{6,3},{1,4},{3,5},{5,6},{7,7},{8,8},{10,9},{12,1... | collective-permute-start | bytes 3145736 | tf_op jit(solution)/shard_map/ppermute | solution.py:282
  762.6 93.9 %collective-permute-start.34 = (bf16[256,2048]{1,0:T(8,128)(2,1)}, bf16[256,2048]{1,0:T(8,128)(2,1)}, u32[]{:S(2)}, u32[]{:S(2)}) collective-permute-start(bf16[256,2048]{1,0:T(8,128)(2,1)} %get-tuple-element.188), channel_id=1, source_target_pairs={{2,0},{0,1},{6,2},{4,3},{3,4},{1,5},{7,6},{5,7},{10,8},{8,9},{14,1... | collective-permute-start | bytes 3145736 | tf_op jit(solution)/shard_map/ppermute | solution.py:282
  775.4 85.4 %collective-permute-start.48 = (bf16[1024,1024]{1,0:T(8,128)(2,1)}, bf16[1024,1024]{1,0:T(8,128)(2,1)}, u32[]{:S(2)}, u32[]{:S(2)}) collective-permute-start(bf16[1024,1024]{1,0:T(8,128)(2,1)} %slice_add_fusion), channel_id=1, source_target_pairs={{0,16},{8,24},{16,0},{24,8},{1,17},{9,25},{17,1},{25,9},{2,18},{10... | collective-permute-start | bytes 6291464 | tf_op jit(solution)/shard_map/ppermute | solution.py:254
  778.6 83.7 %collective-permute-start.47 = (bf16[1024,1024]{1,0:T(8,128)(2,1)S(1)}, bf16[1024,1024]{1,0:T(8,128)(2,1)}, u32[]{:S(2)}, u32[]{:S(2)}) collective-permute-start(bf16[1024,1024]{1,0:T(8,128)(2,1)S(1)} %slice_add_fusion.1), channel_id=1, source_target_pairs={{0,8},{8,0},{16,24},{24,16},{1,9},{9,1},{17,25},{25,17},{2,10},{10... | collective-permute-start | bytes 6291464 | tf_op jit(solution)/shard_map/ppermute | solution.py:254
  856.5 70.9 %collective-permute-start.45 = (bf16[1024,1536]{1,0:T(8,128)(2,1)}, bf16[1024,1536]{1,0:T(8,128)(2,1)}, u32[]{:S(2)}, u32[]{:S(2)}) collective-permute-start(bf16[1024,1536]{1,0:T(8,128)(2,1)} %convolution_convert_fusion.1), channel_id=1, source_target_pairs={{0,8},{8,0},{16,24},{24,16},{1,9},{9,1},{17,25},{25,17},{2,10},{10... | collective-permute-start | bytes 9437192 | tf_op jit(solution)/shard_map/ppermute | solution.py:254
  860.8 87.0 %collective-permute-start.46 = (bf16[1024,1536]{1,0:T(8,128)(2,1)}, bf16[1024,1536]{1,0:T(8,128)(2,1)}, u32[]{:S(2)}, u32[]{:S(2)}) collective-permute-start(bf16[1024,1536]{1,0:T(8,128)(2,1)} %convolution_convert_fusion), channel_id=1, source_target_pairs={{0,16},{8,24},{16,0},{24,8},{1,17},{9,25},{17,1},{25,9},{2,18},{10... | collective-permute-start | bytes 9437192 | tf_op jit(solution)/shard_map/ppermute | solution.py:254
  872.2 223.1 %reduce-scatter.7.cloned.1.call-start = ((), (), s32[]{:S(2)}) async-start(), calls=%async_computation.5 | async-start | bytes 1310720 | tf_op jit(solution)/shard_map/reduce_scatter | solution.py:349
  886.3 67.6 %collective-permute-start.56 = (bf16[512,512]{1,0:T(8,128)(2,1)}, bf16[512,512]{1,0:T(8,128)(2,1)}, u32[]{:S(2)}, u32[]{:S(2)}) collective-permute-start(bf16[512,512]{1,0:T(8,128)(2,1)} %fusion.123), channel_id=1, source_target_pairs={{0,8},{8,0},{16,24},{24,16},{1,9},{9,1},{17,25},{25,17},{2,10},{10... | collective-permute-start | bytes 1572872 | tf_op jit(solution)/shard_map/ppermute | solution.py:254
  889.1 70.0 %collective-permute-start.57 = (bf16[512,512]{1,0:T(8,128)(2,1)}, bf16[512,512]{1,0:T(8,128)(2,1)}, u32[]{:S(2)}, u32[]{:S(2)}) collective-permute-start(bf16[512,512]{1,0:T(8,128)(2,1)} %fusion.119), channel_id=1, source_target_pairs={{0,16},{8,24},{16,0},{24,8},{1,17},{9,25},{17,1},{25,9},{2,18},{10... | collective-permute-start | bytes 1572872 | tf_op jit(solution)/shard_map/ppermute | solution.py:254
  927.4 83.7 %collective-permute-start.41 = (bf16[256,2048]{1,0:T(8,128)(2,1)}, bf16[256,2048]{1,0:T(8,128)(2,1)}, u32[]{:S(2)}, u32[]{:S(2)}) collective-permute-start(bf16[256,2048]{1,0:T(8,128)(2,1)} %get-tuple-element.184), channel_id=1, source_target_pairs={{2,0},{0,1},{6,2},{4,3},{3,4},{1,5},{7,6},{5,7},{10,8},{8,9},{14,1... | collective-permute-start | bytes 3145736 | tf_op jit(solution)/shard_map/ppermute | solution.py:282
  949.4 64.8 %collective-permute-start.52 = (bf16[1024,768]{1,0:T(8,128)(2,1)S(1)}, bf16[1024,768]{1,0:T(8,128)(2,1)S(1)}, u32[]{:S(2)}, u32[]{:S(2)}) collective-permute-start(bf16[1024,768]{1,0:T(8,128)(2,1)S(1)} %slice_add_fusion.4), channel_id=1, source_target_pairs={{0,16},{8,24},{16,0},{24,8},{1,17},{9,25},{17,1},{25,9},{2,18},{10... | collective-permute-start | bytes 4718600 | tf_op jit(solution)/shard_map/ppermute | solution.py:254
  953.9 60.3 %collective-permute-start.51 = (bf16[1024,768]{1,0:T(8,128)(2,1)}, bf16[1024,768]{1,0:T(8,128)(2,1)}, u32[]{:S(2)}, u32[]{:S(2)}) collective-permute-start(bf16[1024,768]{1,0:T(8,128)(2,1)} %slice_add_fusion.5), channel_id=1, source_target_pairs={{0,8},{8,0},{16,24},{24,16},{1,9},{9,1},{17,25},{25,17},{2,10},{10... | collective-permute-start | bytes 4718600 | tf_op jit(solution)/shard_map/ppermute | solution.py:254
  964.5 158.3 %reduce-scatter.5.cloned.1.call-start = ((), (), s32[]{:S(2)}) async-start(), calls=%async_computation.4 | async-start | bytes 3932160 | tf_op jit(solution)/shard_map/reduce_scatter | solution.py:349
  (142 other events, 3211.4 us)
Sparse Core Ops, SparseCore 0:
  52.0 84.3 all-gather.8
  138.1 26.6 all-gather.10
  166.9 80.1 all-gather.12
  248.4 79.2 all-gather.14
  734.5 108.6 reduce-scatter.10
  872.4 98.5 reduce-scatter.8
  973.2 34.8 reduce-scatter.6
  1020.8 58.8 reduce-scatter.4
